TPU v7x, 32 devices: a whole 2x2x4 slice. The times are simulated.
32 devices in a mesh: tract: 2 (over x), epoch: 16 (over z, y, core).
Axes of the slice: x: 2, y: 2, z: 4, core: 2. Of those that a mesh axis runs over, the one named last changes fastest.
Arguments:
- templates: bfloat16 [32, 64, 512], P(('tract', 'epoch')), parts along dimension 0, may hold values from -5 to 5
- epoch_patch: int32 [128], P(('tract', 'epoch')), parts along dimension 0, may hold values from 0 to 15, as said below
- images: bfloat16 [128, 64, 512], P(('tract', 'epoch')), parts along dimension 0, may hold values from -12 to 12
- good_pixels: int32 [128, 64, 512], P(('tract', 'epoch')), parts along dimension 0, may hold values 0 or 1
Outputs:
- difference_coadd: float32 [32, 64, 512], P(('tract', 'epoch')), parts along dimension 0
- kernel_coefs: float32 [128, 27], P(('tract', 'epoch')), parts along dimension 0
There are 2 independent parts, one for each index of `tract`. A program takes and returns all parts, laid end to end along the dimension named above; each array names one. Nothing has to cross between parts.
Inputs may be any that keep to these rules, and one draw needn't show every extreme that they name: `epoch_patch`: epoch e is held by the device of index e // 4 along the epoch axis, and its patch p, held by the device of index p, lies within 4 of that index.
All inputs are finite; a program needn't handle non-finite values. No bound on the sum of `good_pixels` on one device may be relied on, other than what follows from the above.
Results may differ from a plain program's by a relative error of at most 0.0045.
The roundings to bfloat16 on the way count: a program that leaves them out, or rounds other values in their place, can miss the bound.
Values may be sent and summed in bfloat16 or wider, within the bound.
No kernel may reach another device: no remote copies, remote signals or barrier semaphores. Data moves between devices by JAX's collectives and lax.ppermute only.
A program may use at most 64 MiB of HBM per device.

v0:
```python
from functools import partial

import jax
import jax.numpy as jnp
from jax import lax
from jax.sharding import PartitionSpec as P

ROWS = 64
COLS = 512
RADIUS = 4
KHALF = 9
NBASIS = 27


SIGMAS = (1.0, 2.0, 4.0)
RIDGE_TERM = 0.1


def passed_along(block, axis, distance):
    devices = range(lax.axis_size(axis))
    route = [(i - distance, i) for i in devices if i - distance in devices]
    return lax.ppermute(block, axis, route)


def shortened(x):
    return jax.tree.map(lambda a: a.astype(jnp.bfloat16) if a.dtype == jnp.float32 else a, x)


def kernel_taps():
    places = jnp.arange(-KHALF, KHALF + 1).astype(jnp.float32)
    profiles = []
    for spread in SIGMAS:
        for degree in range(3):
            profile = places**degree * jnp.exp(-places * places / (2.0 * spread * spread))
            profiles.append(profile / jnp.sqrt(jnp.sum(profile * profile)))
    return jnp.stack(profiles).astype(jnp.bfloat16)


def window_band(kernel_rows, block):
    inputs = jnp.arange(block + 2 * KHALF, dtype=jnp.int32)
    outputs = jnp.arange(block, dtype=jnp.int32)
    tap_index = outputs[None, :] - inputs[:, None] + 2 * KHALF
    matrix = jnp.zeros((kernel_rows.shape[0], block + 2 * KHALF, block), jnp.bfloat16)
    for tap in range(2 * KHALF + 1):
        matrix = jnp.where((tap_index == tap)[None], kernel_rows[:, tap][:, None, None], matrix)
    return matrix


def fit_epoch(nearby, column_band, row_band, record):
    science, good_mask, choose = record
    column_block = column_band.shape[2]
    row_block = row_band.shape[1]
    template = jnp.einsum("q,qyx->yx", choose, nearby, preferred_element_type=jnp.float32).astype(
        jnp.bfloat16
    )
    padded_template = jnp.pad(template, ((0, 0), (KHALF, KHALF)))
    block_list = []
    for spread in range(3):
        column_pieces = []
        for start in range(0, COLS, column_block):
            window = padded_template[:, start : start + column_block + 2 * KHALF]
            column_pieces.append(
                jnp.einsum(
                    "yw,iwx->iyx",
                    window,
                    column_band[3 * spread : 3 * spread + 3],
                    preferred_element_type=jnp.float32,
                ).astype(jnp.bfloat16)
            )
        partial_x = jnp.concatenate(column_pieces, 2)
        padded_rows = jnp.pad(partial_x, ((0, 0), (KHALF, KHALF), (0, 0)))
        start = 0
        window = padded_rows[:, start : start + row_block + 2 * KHALF, :]
        row_pieces = [
            jnp.einsum(
                "jyb,ibx->ijyx",
                row_band[3 * spread : 3 * spread + 3],
                window,
                preferred_element_type=jnp.float32,
            ).astype(jnp.bfloat16)
        ]
        block_set = jnp.concatenate(row_pieces, 2)
        block_list.append(block_set.reshape(9, ROWS * COLS))
    basis_set = jnp.concatenate(block_list, 0)
    weight = good_mask.reshape(-1).astype(jnp.bfloat16)
    pixels = science.reshape(-1)
    normal = jnp.einsum(
        "kp,lp->kl", basis_set, basis_set * weight, preferred_element_type=jnp.float32
    )
    normal = normal / (ROWS * COLS) + RIDGE_TERM * jnp.eye(NBASIS, dtype=jnp.float32)
    target = jnp.einsum(
        "kp,p->k", basis_set, pixels * weight, preferred_element_type=jnp.float32
    ) / (ROWS * COLS)
    factor = jnp.linalg.cholesky(normal)
    coefficients = jax.scipy.linalg.cho_solve((factor, True), target)
    fitted = jnp.zeros((ROWS * COLS,), jnp.float32)
    for spread in range(3):
        fitted = fitted + jnp.dot(
            coefficients[9 * spread : 9 * spread + 9],
            basis_set[9 * spread : 9 * spread + 9].astype(jnp.float32),
            precision=lax.Precision.HIGHEST,
        )
    difference = good_mask.reshape(-1).astype(jnp.float32) * (pixels.astype(jnp.float32) - fitted)
    return (coefficients, difference.reshape(ROWS, COLS))


def shards(templates, epoch_patch, images, good_pixels):
    window = 2 * RADIUS + 1
    collected = {0: templates}
    for offset in range(-RADIUS, RADIUS + 1):
        if offset != 0:
            collected[offset] = passed_along(templates, "epoch", -offset)
    nearby = jnp.concatenate([collected[offset] for offset in range(-RADIUS, RADIUS + 1)], 0)
    kernel_rows = kernel_taps()
    column_band = window_band(kernel_rows, min(128, COLS))
    row_band = jnp.swapaxes(window_band(kernel_rows, min(128, ROWS)), 1, 2)
    offsets = epoch_patch - lax.axis_index("epoch") + RADIUS
    choose = offsets[:, None] == jnp.arange(window, dtype=jnp.int32)[None, :]
    coefficients, differences = lax.map(
        partial(fit_epoch, nearby, column_band, row_band),
        (images, good_pixels, choose.astype(jnp.bfloat16)),
    )
    portion = jnp.einsum(
        "eq,eyx->qyx", choose.astype(jnp.float32), differences, precision=lax.Precision.HIGHEST
    )
    deep_sum = portion[RADIUS : RADIUS + 1]
    for offset in range(-RADIUS, RADIUS + 1):
        if offset != 0:
            position = RADIUS + offset
            deep_sum = deep_sum + passed_along(
                shortened(portion[position : position + 1]), "epoch", offset
            )
    return (deep_sum, coefficients)


def solution(mesh):
    in_specs = (
        P(("tract", "epoch"), None, None),
        P(("tract", "epoch")),
        P(("tract", "epoch"), None, None),
        P(("tract", "epoch"), None, None),
    )
    out_specs = (P(("tract", "epoch"), None, None), P(("tract", "epoch"), None))
    return jax.shard_map(shards, mesh=mesh, in_specs=in_specs, out_specs=out_specs, check_vma=False)
```

profile of v0, /device:TPU:1, one launch (start us, length us, event | category | flops | bytes accessed | tf_op | source)
XLA Modules:
  0.0 188.9 jit_solution(16297186205018700916)
XLA Ops:
  0.6 4.2 %collective-permute-start = (bf16[1,64,512]{2,1,0:T(8,128)(2,1)}, bf16[1,64,512]{2,1,0:T(8,128)(2,1)S(1)}, u32[]{:S(2)}, u32[]{:S(2)}) collective-permute-start(bf16[1,64,512]{2,1,0:T(8,128)(2,1)} %param.6), channel_id=1, source_target_pairs={{0,4},{1,5},{2,6},{3,7},{4,8},{5,9},{6,10},{7,11},{8,12},{9,13},{1... | collective-permute-start | bytes 196616 | tf_op jit(solution)/shard_map/ppermute | solution.py:22
  4.8 4.0 %collective-permute-start.1 = (bf16[1,64,512]{2,1,0:T(8,128)(2,1)}, bf16[1,64,512]{2,1,0:T(8,128)(2,1)S(1)}, u32[]{:S(2)}, u32[]{:S(2)}) collective-permute-start(bf16[1,64,512]{2,1,0:T(8,128)(2,1)} %param.6), channel_id=1, source_target_pairs={{0,3},{1,4},{2,5},{3,6},{4,7},{5,8},{6,9},{7,10},{8,11},{9,12},{10... | collective-permute-start | bytes 196616 | tf_op jit(solution)/shard_map/ppermute | solution.py:22
  8.9 3.1 %collective-permute-start.2 = (bf16[1,64,512]{2,1,0:T(8,128)(2,1)}, bf16[1,64,512]{2,1,0:T(8,128)(2,1)S(1)}, u32[]{:S(2)}, u32[]{:S(2)}) collective-permute-start(bf16[1,64,512]{2,1,0:T(8,128)(2,1)} %param.6), channel_id=1, source_target_pairs={{0,2},{1,3},{2,4},{3,5},{4,6},{5,7},{6,8},{7,9},{8,10},{9,11},{10,... | collective-permute-start | bytes 196616 | tf_op jit(solution)/shard_map/ppermute | solution.py:22
  12.0 2.8 %collective-permute-start.3 = (bf16[1,64,512]{2,1,0:T(8,128)(2,1)}, bf16[1,64,512]{2,1,0:T(8,128)(2,1)S(1)}, u32[]{:S(2)}, u32[]{:S(2)}) collective-permute-start(bf16[1,64,512]{2,1,0:T(8,128)(2,1)} %param.6), channel_id=1, source_target_pairs={{0,1},{1,2},{2,3},{3,4},{4,5},{5,6},{6,7},{7,8},{8,9},{9,10},{10,1... | collective-permute-start | bytes 196616 | tf_op jit(solution)/shard_map/ppermute | solution.py:22
  14.8 1.9 %collective-permute-start.4 = (bf16[1,64,512]{2,1,0:T(8,128)(2,1)}, bf16[1,64,512]{2,1,0:T(8,128)(2,1)S(1)}, u32[]{:S(2)}, u32[]{:S(2)}) collective-permute-start(bf16[1,64,512]{2,1,0:T(8,128)(2,1)} %param.6), channel_id=1, source_target_pairs={{1,0},{2,1},{3,2},{4,3},{5,4},{6,5},{7,6},{8,7},{9,8},{10,9},{11,1... | collective-permute-start | bytes 196616 | tf_op jit(solution)/shard_map/ppermute | solution.py:22
  30.2 1.5 select_select_fusion.1
  31.8 1.1 select_select_fusion.2
  33.0 1.3 collective-permute-start.5
  34.3 1.3 collective-permute-start.6
  35.6 1.5 collective-permute-start.7
  37.2 1.4 collective-permute-done.5
  38.6 3.7 %collective-permute-done.6 = bf16[1,64,512]{2,1,0:T(8,128)(2,1)S(1)} collective-permute-done((bf16[1,64,512]{2,1,0:T(8,128)(2,1)}, bf16[1,64,512]{2,1,0:T(8,128)(2,1)S(1)}, u32[]{:S(2)}, u32[]{:S(2)}) %collective-permute-start.6) | collective-permute-done | bytes 65568 | tf_op jit(solution)/shard_map/ppermute | solution.py:22
  42.3 1.5 collective-permute-done.7
  43.8 111.7 %while.14 = (s32[]{:T(128)}, f32[4,27]{1,0:T(4,128)}, f32[4,64,512]{2,0,1:T(4,128)}, bf16[4,9]{1,0:T(4,128)(2,1)S(1)}, bf16[9,64,512]{2,1,0:T(8,128)(2,1)S(1)}, ...) while((s32[]{:T(128)}, f32[4,27]{1,0:T(4,128)}, ...), condition=%wide.region_12.13_spmd, body=%wide.region_9.12_spmd.sunk | while | flops 316796448 | bytes 30745948 | solution.py:119
  45.1 1.1 convolution_convert_fusion.19
  47.7 1.1 convolution_convert_fusion.20
  50.4 1.1 convolution_convert_fusion.18
  52.2 1.6 convert_bitcast_fusion.2
  54.4 1.2 fusion.285
  55.8 2.5 %cholesky.56 = f32[27,27]{1,0:T(8,128)S(1)} custom-call(f32[27,27]{1,0:T(8,128)S(1)} %fusion.286), custom_call_target="Cholesky" | custom-call | tf_op jit(solution)/shard_map/while/body/eval_jaxpr/jit(cholesky)/cholesky | solution.py:94
  59.7 2.1 %custom-call.21 = f32[1,27,27]{1,2,0:T(8,128)S(1)} custom-call(f32[1,27,27]{2,1,0:T(8,128)S(1)} %fusion.287), custom_call_target="InvertDiagBlocksLowerTriangular" | custom-call | tf_op jit(solution)/shard_map/while/body/eval_jaxpr/jit(_cho_solve)/triangular_solve | solution.py:95
  63.6 1.0 fusion.284
  66.8 3.6 %dynamic_update_slice.17 = f32[4,64,512]{2,0,1:T(4,128)} dynamic-update-slice(f32[4,64,512]{2,0,1:T(4,128)} %get-tuple-element.290, f32[1,64,512]{2,0,1:T(1,128)S(1)} %bitcast.316, s32[]{:T(128)} %get-tuple-element.288, s32[]{:T(128)} %constant.162.clone.1..sunk, s32[]{:T(128)} %constant.162.clone.1..sunk) | dynamic-update-slice | bytes 262148 | tf_op jit(solution)/shard_map/while/body/jit(dynamic_update_index_in_dim)/dynamic_update_slice | solution.py:119
  70.4 1.3 dynamic_update_slice.16
  73.0 1.1 convolution_convert_fusion.19
  75.7 1.1 convolution_convert_fusion.20
  78.3 1.1 convolution_convert_fusion.18
  80.1 1.6 convert_bitcast_fusion.2
  82.4 1.2 fusion.285
  83.7 2.5 %cholesky.56 = f32[27,27]{1,0:T(8,128)S(1)} custom-call(f32[27,27]{1,0:T(8,128)S(1)} %fusion.286), custom_call_target="Cholesky" | custom-call | tf_op jit(solution)/shard_map/while/body/eval_jaxpr/jit(cholesky)/cholesky | solution.py:94
  87.6 2.1 %custom-call.21 = f32[1,27,27]{1,2,0:T(8,128)S(1)} custom-call(f32[1,27,27]{2,1,0:T(8,128)S(1)} %fusion.287), custom_call_target="InvertDiagBlocksLowerTriangular" | custom-call | tf_op jit(solution)/shard_map/while/body/eval_jaxpr/jit(_cho_solve)/triangular_solve | solution.py:95
  91.5 1.0 fusion.284
  94.7 3.6 %dynamic_update_slice.17 = f32[4,64,512]{2,0,1:T(4,128)} dynamic-update-slice(f32[4,64,512]{2,0,1:T(4,128)} %get-tuple-element.290, f32[1,64,512]{2,0,1:T(1,128)S(1)} %bitcast.316, s32[]{:T(128)} %get-tuple-element.288, s32[]{:T(128)} %constant.162.clone.1..sunk, s32[]{:T(128)} %constant.162.clone.1..sunk) | dynamic-update-slice | bytes 262148 | tf_op jit(solution)/shard_map/while/body/jit(dynamic_update_index_in_dim)/dynamic_update_slice | solution.py:119
  98.4 1.3 dynamic_update_slice.16
  100.9 1.1 convolution_convert_fusion.19
  103.6 1.1 convolution_convert_fusion.20
  106.2 1.1 convolution_convert_fusion.18
  108.0 1.6 convert_bitcast_fusion.2
  110.3 1.2 fusion.285
  111.6 2.5 %cholesky.56 = f32[27,27]{1,0:T(8,128)S(1)} custom-call(f32[27,27]{1,0:T(8,128)S(1)} %fusion.286), custom_call_target="Cholesky" | custom-call | tf_op jit(solution)/shard_map/while/body/eval_jaxpr/jit(cholesky)/cholesky | solution.py:94
  115.5 2.1 %custom-call.21 = f32[1,27,27]{1,2,0:T(8,128)S(1)} custom-call(f32[1,27,27]{2,1,0:T(8,128)S(1)} %fusion.287), custom_call_target="InvertDiagBlocksLowerTriangular" | custom-call | tf_op jit(solution)/shard_map/while/body/eval_jaxpr/jit(_cho_solve)/triangular_solve | solution.py:95
  119.4 1.0 fusion.284
  122.6 3.6 %dynamic_update_slice.17 = f32[4,64,512]{2,0,1:T(4,128)} dynamic-update-slice(f32[4,64,512]{2,0,1:T(4,128)} %get-tuple-element.290, f32[1,64,512]{2,0,1:T(1,128)S(1)} %bitcast.316, s32[]{:T(128)} %get-tuple-element.288, s32[]{:T(128)} %constant.162.clone.1..sunk, s32[]{:T(128)} %constant.162.clone.1..sunk) | dynamic-update-slice | bytes 262148 | tf_op jit(solution)/shard_map/while/body/jit(dynamic_update_index_in_dim)/dynamic_update_slice | solution.py:119
  126.3 1.3 dynamic_update_slice.16
  128.9 1.1 convolution_convert_fusion.19
  131.5 1.1 convolution_convert_fusion.20
  134.2 1.1 convolution_convert_fusion.18
  136.0 1.6 convert_bitcast_fusion.2
  138.2 1.2 fusion.285
  139.5 2.5 %cholesky.56 = f32[27,27]{1,0:T(8,128)S(1)} custom-call(f32[27,27]{1,0:T(8,128)S(1)} %fusion.286), custom_call_target="Cholesky" | custom-call | tf_op jit(solution)/shard_map/while/body/eval_jaxpr/jit(cholesky)/cholesky | solution.py:94
  143.4 2.1 %custom-call.21 = f32[1,27,27]{1,2,0:T(8,128)S(1)} custom-call(f32[1,27,27]{2,1,0:T(8,128)S(1)} %fusion.287), custom_call_target="InvertDiagBlocksLowerTriangular" | custom-call | tf_op jit(solution)/shard_map/while/body/eval_jaxpr/jit(_cho_solve)/triangular_solve | solution.py:95
  150.6 3.6 %dynamic_update_slice.17 = f32[4,64,512]{2,0,1:T(4,128)} dynamic-update-slice(f32[4,64,512]{2,0,1:T(4,128)} %get-tuple-element.290, f32[1,64,512]{2,0,1:T(1,128)S(1)} %bitcast.316, s32[]{:T(128)} %get-tuple-element.288, s32[]{:T(128)} %constant.162.clone.1..sunk, s32[]{:T(128)} %constant.162.clone.1..sunk) | dynamic-update-slice | bytes 262148 | tf_op jit(solution)/shard_map/while/body/jit(dynamic_update_index_in_dim)/dynamic_update_slice | solution.py:119
  154.2 1.3 dynamic_update_slice.16
  155.5 2.2 %fusion.166 = (bf16[9,64,512]{2,0,1:T(8,128)(2,1)S(1)}, f32[9,64,512]{2,0,1:T(8,128)S(1)}) fusion(f32[4,64,512]{2,0,1:T(4,128)} %get-tuple-element.116, s32[4]{0:T(128)S(1)} %subtract_add_fusion.2), kind=kOutput, calls=%fused_computation.262 | convolution fusion | flops 14450724 | bytes 2293776 | tf_op jit(solution)/shard_map/eq,eyx->qyx/dot_general | solution.py:123
  158.5 1.3 collective-permute-start.10
  159.8 2.9 %collective-permute-start.11 = (bf16[1,64,512]{2,0,1:T(2,128)(2,1)S(1)}, bf16[1,64,512]{2,0,1:T(2,128)(2,1)S(1)}, u32[]{:S(2)}, u32[]{:S(2)}) collective-permute-start(bf16[1,64,512]{2,0,1:T(2,128)(2,1)S(1)} %get-tuple-element.168), channel_id=1, source_target_pairs={{1,0},{2,1},{3,2},{4,3},{5,4},{6,5},{7,6},{8,7},{9,8},{10,9},{11,1... | collective-permute-start | bytes 196616 | tf_op jit(solution)/shard_map/ppermute | solution.py:22
  162.7 4.2 %collective-permute-start.12 = (bf16[1,64,512]{2,0,1:T(2,128)(2,1)S(1)}, bf16[1,64,512]{2,0,1:T(2,128)(2,1)S(1)}, u32[]{:S(2)}, u32[]{:S(2)}) collective-permute-start(bf16[1,64,512]{2,0,1:T(2,128)(2,1)S(1)} %get-tuple-element.167), channel_id=1, source_target_pairs={{0,1},{1,2},{2,3},{3,4},{4,5},{5,6},{6,7},{7,8},{8,9},{9,10},{10,1... | collective-permute-start | bytes 196616 | tf_op jit(solution)/shard_map/ppermute | solution.py:22
  166.9 4.5 %collective-permute-start.13 = (bf16[1,64,512]{2,0,1:T(2,128)(2,1)S(1)}, bf16[1,64,512]{2,0,1:T(2,128)(2,1)S(1)}, u32[]{:S(2)}, u32[]{:S(2)}) collective-permute-start(bf16[1,64,512]{2,0,1:T(2,128)(2,1)S(1)} %get-tuple-element.166), channel_id=1, source_target_pairs={{0,2},{1,3},{2,4},{3,5},{4,6},{5,7},{6,8},{7,9},{8,10},{9,11},{10,... | collective-permute-start | bytes 196616 | tf_op jit(solution)/shard_map/ppermute | solution.py:22
  171.4 2.1 %collective-permute-start.14 = (bf16[1,64,512]{2,0,1:T(2,128)(2,1)S(1)}, bf16[1,64,512]{2,0,1:T(2,128)(2,1)S(1)}, u32[]{:S(2)}, u32[]{:S(2)}) collective-permute-start(bf16[1,64,512]{2,0,1:T(2,128)(2,1)S(1)} %get-tuple-element.165), channel_id=1, source_target_pairs={{0,3},{1,4},{2,5},{3,6},{4,7},{5,8},{6,9},{7,10},{8,11},{9,12},{10... | collective-permute-start | bytes 196616 | tf_op jit(solution)/shard_map/ppermute | solution.py:22
  173.5 3.2 %collective-permute-start.15 = (bf16[1,64,512]{2,0,1:T(2,128)(2,1)S(1)}, bf16[1,64,512]{2,0,1:T(2,128)(2,1)S(1)}, u32[]{:S(2)}, u32[]{:S(2)}) collective-permute-start(bf16[1,64,512]{2,0,1:T(2,128)(2,1)S(1)} %get-tuple-element.164), channel_id=1, source_target_pairs={{0,4},{1,5},{2,6},{3,7},{4,8},{5,9},{6,10},{7,11},{8,12},{9,13},{1... | collective-permute-start | bytes 196616 | tf_op jit(solution)/shard_map/ppermute | solution.py:22
  176.7 1.3 collective-permute-start.8
  178.0 1.3 collective-permute-start.9
  179.4 3.1 %collective-permute-done.8 = bf16[1,64,512]{2,0,1:T(2,128)(2,1)S(1)} collective-permute-done((bf16[1,64,512]{2,0,1:T(2,128)(2,1)S(1)}, bf16[1,64,512]{2,0,1:T(2,128)(2,1)S(1)}, u32[]{:S(2)}, u32[]{:S(2)}) %collective-permute-start.8) | collective-permute-done | bytes 65568 | tf_op jit(solution)/shard_map/ppermute | solution.py:22
  182.4 5.1 %collective-permute-done.9 = bf16[1,64,512]{2,0,1:T(2,128)(2,1)S(1)} collective-permute-done((bf16[1,64,512]{2,0,1:T(2,128)(2,1)S(1)}, bf16[1,64,512]{2,0,1:T(2,128)(2,1)S(1)}, u32[]{:S(2)}, u32[]{:S(2)}) %collective-permute-start.9) | collective-permute-done | bytes 65568 | tf_op jit(solution)/shard_map/ppermute | solution.py:22
  (246 shorter events, 55.2 us)
Async XLA Ops:
  0.6 35.0 %copy-start.4 = (bf16[1,64,512]{2,1,0:T(8,128)(2,1)S(1)}, bf16[1,64,512]{2,1,0:T(8,128)(2,1)}, u32[]{:S(2)}) copy-start(bf16[1,64,512]{2,1,0:T(8,128)(2,1)} %param.6) | copy-start | bytes 196612
  0.6 32.3 %collective-permute-start = (bf16[1,64,512]{2,1,0:T(8,128)(2,1)}, bf16[1,64,512]{2,1,0:T(8,128)(2,1)S(1)}, u32[]{:S(2)}, u32[]{:S(2)}) collective-permute-start(bf16[1,64,512]{2,1,0:T(8,128)(2,1)} %param.6), channel_id=1, source_target_pairs={{0,4},{1,5},{2,6},{3,7},{4,8},{5,9},{6,10},{7,11},{8,12},{9,13},{1... | collective-permute-start | bytes 196616 | tf_op jit(solution)/shard_map/ppermute | solution.py:22
  4.8 29.5 %collective-permute-start.1 = (bf16[1,64,512]{2,1,0:T(8,128)(2,1)}, bf16[1,64,512]{2,1,0:T(8,128)(2,1)S(1)}, u32[]{:S(2)}, u32[]{:S(2)}) collective-permute-start(bf16[1,64,512]{2,1,0:T(8,128)(2,1)} %param.6), channel_id=1, source_target_pairs={{0,3},{1,4},{2,5},{3,6},{4,7},{5,8},{6,9},{7,10},{8,11},{9,12},{10... | collective-permute-start | bytes 196616 | tf_op jit(solution)/shard_map/ppermute | solution.py:22
  8.9 26.8 %collective-permute-start.2 = (bf16[1,64,512]{2,1,0:T(8,128)(2,1)}, bf16[1,64,512]{2,1,0:T(8,128)(2,1)S(1)}, u32[]{:S(2)}, u32[]{:S(2)}) collective-permute-start(bf16[1,64,512]{2,1,0:T(8,128)(2,1)} %param.6), channel_id=1, source_target_pairs={{0,2},{1,3},{2,4},{3,5},{4,6},{5,7},{6,8},{7,9},{8,10},{9,11},{10,... | collective-permute-start | bytes 196616 | tf_op jit(solution)/shard_map/ppermute | solution.py:22
  12.0 25.1 %collective-permute-start.3 = (bf16[1,64,512]{2,1,0:T(8,128)(2,1)}, bf16[1,64,512]{2,1,0:T(8,128)(2,1)S(1)}, u32[]{:S(2)}, u32[]{:S(2)}) collective-permute-start(bf16[1,64,512]{2,1,0:T(8,128)(2,1)} %param.6), channel_id=1, source_target_pairs={{0,1},{1,2},{2,3},{3,4},{4,5},{5,6},{6,7},{7,8},{8,9},{9,10},{10,1... | collective-permute-start | bytes 196616 | tf_op jit(solution)/shard_map/ppermute | solution.py:22
  14.8 22.3 %collective-permute-start.4 = (bf16[1,64,512]{2,1,0:T(8,128)(2,1)}, bf16[1,64,512]{2,1,0:T(8,128)(2,1)S(1)}, u32[]{:S(2)}, u32[]{:S(2)}) collective-permute-start(bf16[1,64,512]{2,1,0:T(8,128)(2,1)} %param.6), channel_id=1, source_target_pairs={{1,0},{2,1},{3,2},{4,3},{5,4},{6,5},{7,6},{8,7},{9,8},{10,9},{11,1... | collective-permute-start | bytes 196616 | tf_op jit(solution)/shard_map/ppermute | solution.py:22
  33.0 5.6 %collective-permute-start.5 = (bf16[1,64,512]{2,1,0:T(8,128)(2,1)}, bf16[1,64,512]{2,1,0:T(8,128)(2,1)S(1)}, u32[]{:S(2)}, u32[]{:S(2)}) collective-permute-start(bf16[1,64,512]{2,1,0:T(8,128)(2,1)} %param.6), channel_id=1, source_target_pairs={{2,0},{3,1},{4,2},{5,3},{6,4},{7,5},{8,6},{9,7},{10,8},{11,9},{12,... | collective-permute-start | bytes 196616 | tf_op jit(solution)/shard_map/ppermute | solution.py:22
  34.3 8.0 %collective-permute-start.6 = (bf16[1,64,512]{2,1,0:T(8,128)(2,1)}, bf16[1,64,512]{2,1,0:T(8,128)(2,1)S(1)}, u32[]{:S(2)}, u32[]{:S(2)}) collective-permute-start(bf16[1,64,512]{2,1,0:T(8,128)(2,1)} %param.6), channel_id=1, source_target_pairs={{3,0},{4,1},{5,2},{6,3},{7,4},{8,5},{9,6},{10,7},{11,8},{12,9},{13... | collective-permute-start | bytes 196616 | tf_op jit(solution)/shard_map/ppermute | solution.py:22
  35.6 8.1 %collective-permute-start.7 = (bf16[1,64,512]{2,1,0:T(8,128)(2,1)S(1)}, bf16[1,64,512]{2,1,0:T(8,128)(2,1)S(1)}, u32[]{:S(2)}, u32[]{:S(2)}) collective-permute-start(bf16[1,64,512]{2,1,0:T(8,128)(2,1)S(1)} %copy-done.4), channel_id=1, source_target_pairs={{4,0},{5,1},{6,2},{7,3},{8,4},{9,5},{10,6},{11,7},{12,8},{13,9},{1... | collective-permute-start | bytes 196616 | tf_op jit(solution)/shard_map/ppermute | solution.py:22
  43.8 2.4 %copy-start = (bf16[9,64,512]{2,1,0:T(8,128)(2,1)}, bf16[9,64,512]{2,1,0:T(8,128)(2,1)S(1)}, u32[]{:S(2)}) copy-start(bf16[9,64,512]{2,1,0:T(8,128)(2,1)S(1)} %get-tuple-element.304) | copy-start | bytes 1769476 | tf_op jit(solution)/shard_map/while
  53.8 0.6 copy-start.3
  64.6 2.2 %copy-start.2 = (f32[8,4,8,128]{3,2,1,0:T(8,128)S(1)}, f32[8,4,8,128]{3,2,1,0:T(8,128)}, u32[]{:S(2)}) copy-start(f32[8,4,8,128]{3,2,1,0:T(8,128)} %get-tuple-element.275) | copy-start | bytes 393220 | tf_op jit(solution)/shard_map/while
  65.5 6.2 %copy-start.1 = (bf16[9,64,512]{2,1,0:T(8,128)(2,1)S(1)}, bf16[9,64,512]{2,1,0:T(8,128)(2,1)}, u32[]{:S(2)}) copy-start(bf16[9,64,512]{2,1,0:T(8,128)(2,1)} %copy-done) | copy-start | bytes 1769476 | tf_op jit(solution)/shard_map/while
  71.7 2.4 %copy-start = (bf16[9,64,512]{2,1,0:T(8,128)(2,1)}, bf16[9,64,512]{2,1,0:T(8,128)(2,1)S(1)}, u32[]{:S(2)}) copy-start(bf16[9,64,512]{2,1,0:T(8,128)(2,1)S(1)} %get-tuple-element.304) | copy-start | bytes 1769476 | tf_op jit(solution)/shard_map/while
  81.7 0.6 copy-start.3
  92.5 2.2 %copy-start.2 = (f32[8,4,8,128]{3,2,1,0:T(8,128)S(1)}, f32[8,4,8,128]{3,2,1,0:T(8,128)}, u32[]{:S(2)}) copy-start(f32[8,4,8,128]{3,2,1,0:T(8,128)} %get-tuple-element.275) | copy-start | bytes 393220 | tf_op jit(solution)/shard_map/while
  93.4 6.2 %copy-start.1 = (bf16[9,64,512]{2,1,0:T(8,128)(2,1)S(1)}, bf16[9,64,512]{2,1,0:T(8,128)(2,1)}, u32[]{:S(2)}) copy-start(bf16[9,64,512]{2,1,0:T(8,128)(2,1)} %copy-done) | copy-start | bytes 1769476 | tf_op jit(solution)/shard_map/while
  99.6 2.4 %copy-start = (bf16[9,64,512]{2,1,0:T(8,128)(2,1)}, bf16[9,64,512]{2,1,0:T(8,128)(2,1)S(1)}, u32[]{:S(2)}) copy-start(bf16[9,64,512]{2,1,0:T(8,128)(2,1)S(1)} %get-tuple-element.304) | copy-start | bytes 1769476 | tf_op jit(solution)/shard_map/while
  109.7 0.6 copy-start.3
  120.4 2.2 %copy-start.2 = (f32[8,4,8,128]{3,2,1,0:T(8,128)S(1)}, f32[8,4,8,128]{3,2,1,0:T(8,128)}, u32[]{:S(2)}) copy-start(f32[8,4,8,128]{3,2,1,0:T(8,128)} %get-tuple-element.275) | copy-start | bytes 393220 | tf_op jit(solution)/shard_map/while
  121.3 6.2 %copy-start.1 = (bf16[9,64,512]{2,1,0:T(8,128)(2,1)S(1)}, bf16[9,64,512]{2,1,0:T(8,128)(2,1)}, u32[]{:S(2)}) copy-start(bf16[9,64,512]{2,1,0:T(8,128)(2,1)} %copy-done) | copy-start | bytes 1769476 | tf_op jit(solution)/shard_map/while
  127.6 2.4 %copy-start = (bf16[9,64,512]{2,1,0:T(8,128)(2,1)}, bf16[9,64,512]{2,1,0:T(8,128)(2,1)S(1)}, u32[]{:S(2)}) copy-start(bf16[9,64,512]{2,1,0:T(8,128)(2,1)S(1)} %get-tuple-element.304) | copy-start | bytes 1769476 | tf_op jit(solution)/shard_map/while
  137.6 0.6 copy-start.3
  148.3 2.2 %copy-start.2 = (f32[8,4,8,128]{3,2,1,0:T(8,128)S(1)}, f32[8,4,8,128]{3,2,1,0:T(8,128)}, u32[]{:S(2)}) copy-start(f32[8,4,8,128]{3,2,1,0:T(8,128)} %get-tuple-element.275) | copy-start | bytes 393220 | tf_op jit(solution)/shard_map/while
  149.3 6.2 %copy-start.1 = (bf16[9,64,512]{2,1,0:T(8,128)(2,1)S(1)}, bf16[9,64,512]{2,1,0:T(8,128)(2,1)}, u32[]{:S(2)}) copy-start(bf16[9,64,512]{2,1,0:T(8,128)(2,1)} %copy-done) | copy-start | bytes 1769476 | tf_op jit(solution)/shard_map/while
  158.5 15.0 %collective-permute-start.10 = (bf16[1,64,512]{2,0,1:T(2,128)(2,1)S(1)}, bf16[1,64,512]{2,0,1:T(2,128)(2,1)S(1)}, u32[]{:S(2)}, u32[]{:S(2)}) collective-permute-start(bf16[1,64,512]{2,0,1:T(2,128)(2,1)S(1)} %get-tuple-element.169), channel_id=1, source_target_pairs={{2,0},{3,1},{4,2},{5,3},{6,4},{7,5},{8,6},{9,7},{10,8},{11,9},{12,... | collective-permute-start | bytes 196616 | tf_op jit(solution)/shard_map/ppermute | solution.py:22
  159.8 16.9 %collective-permute-start.11 = (bf16[1,64,512]{2,0,1:T(2,128)(2,1)S(1)}, bf16[1,64,512]{2,0,1:T(2,128)(2,1)S(1)}, u32[]{:S(2)}, u32[]{:S(2)}) collective-permute-start(bf16[1,64,512]{2,0,1:T(2,128)(2,1)S(1)} %get-tuple-element.168), channel_id=1, source_target_pairs={{1,0},{2,1},{3,2},{4,3},{5,4},{6,5},{7,6},{8,7},{9,8},{10,9},{11,1... | collective-permute-start | bytes 196616 | tf_op jit(solution)/shard_map/ppermute | solution.py:22
  162.7 15.3 %collective-permute-start.12 = (bf16[1,64,512]{2,0,1:T(2,128)(2,1)S(1)}, bf16[1,64,512]{2,0,1:T(2,128)(2,1)S(1)}, u32[]{:S(2)}, u32[]{:S(2)}) collective-permute-start(bf16[1,64,512]{2,0,1:T(2,128)(2,1)S(1)} %get-tuple-element.167), channel_id=1, source_target_pairs={{0,1},{1,2},{2,3},{3,4},{4,5},{5,6},{6,7},{7,8},{8,9},{9,10},{10,1... | collective-permute-start | bytes 196616 | tf_op jit(solution)/shard_map/ppermute | solution.py:22
  166.9 12.5 %collective-permute-start.13 = (bf16[1,64,512]{2,0,1:T(2,128)(2,1)S(1)}, bf16[1,64,512]{2,0,1:T(2,128)(2,1)S(1)}, u32[]{:S(2)}, u32[]{:S(2)}) collective-permute-start(bf16[1,64,512]{2,0,1:T(2,128)(2,1)S(1)} %get-tuple-element.166), channel_id=1, source_target_pairs={{0,2},{1,3},{2,4},{3,5},{4,6},{5,7},{6,8},{7,9},{8,10},{9,11},{10,... | collective-permute-start | bytes 196616 | tf_op jit(solution)/shard_map/ppermute | solution.py:22
  171.4 7.9 %collective-permute-start.14 = (bf16[1,64,512]{2,0,1:T(2,128)(2,1)S(1)}, bf16[1,64,512]{2,0,1:T(2,128)(2,1)S(1)}, u32[]{:S(2)}, u32[]{:S(2)}) collective-permute-start(bf16[1,64,512]{2,0,1:T(2,128)(2,1)S(1)} %get-tuple-element.165), channel_id=1, source_target_pairs={{0,3},{1,4},{2,5},{3,6},{4,7},{5,8},{6,9},{7,10},{8,11},{9,12},{10... | collective-permute-start | bytes 196616 | tf_op jit(solution)/shard_map/ppermute | solution.py:22
  173.5 5.8 %collective-permute-start.15 = (bf16[1,64,512]{2,0,1:T(2,128)(2,1)S(1)}, bf16[1,64,512]{2,0,1:T(2,128)(2,1)S(1)}, u32[]{:S(2)}, u32[]{:S(2)}) collective-permute-start(bf16[1,64,512]{2,0,1:T(2,128)(2,1)S(1)} %get-tuple-element.164), channel_id=1, source_target_pairs={{0,4},{1,5},{2,6},{3,7},{4,8},{5,9},{6,10},{7,11},{8,12},{9,13},{1... | collective-permute-start | bytes 196616 | tf_op jit(solution)/shard_map/ppermute | solution.py:22
  176.7 5.7 %collective-permute-start.8 = (bf16[1,64,512]{2,0,1:T(2,128)(2,1)S(1)}, bf16[1,64,512]{2,0,1:T(2,128)(2,1)S(1)}, u32[]{:S(2)}, u32[]{:S(2)}) collective-permute-start(bf16[1,64,512]{2,0,1:T(2,128)(2,1)S(1)} %get-tuple-element.163), channel_id=1, source_target_pairs={{4,0},{5,1},{6,2},{7,3},{8,4},{9,5},{10,6},{11,7},{12,8},{13,9},{1... | collective-permute-start | bytes 196616 | tf_op jit(solution)/shard_map/ppermute | solution.py:22
  178.0 9.5 %collective-permute-start.9 = (bf16[1,64,512]{2,0,1:T(2,128)(2,1)S(1)}, bf16[1,64,512]{2,0,1:T(2,128)(2,1)S(1)}, u32[]{:S(2)}, u32[]{:S(2)}) collective-permute-start(bf16[1,64,512]{2,0,1:T(2,128)(2,1)S(1)} %get-tuple-element.170), channel_id=1, source_target_pairs={{3,0},{4,1},{5,2},{6,3},{7,4},{8,5},{9,6},{10,7},{11,8},{12,9},{13... | collective-permute-start | bytes 196616 | tf_op jit(solution)/shard_map/ppermute | solution.py:22
where the time goes:
time: 191 us; the launch traced here: 189 us
  matrix products  44.6 us (23%)
  other arithmetic  44.1 us (23%)
  starting transfers between devices  40.9 us (21%)
  local copies, waits for them, and re-layouts  36.6 us (19%)
  waiting for transfers between devices  14.8 us (8%)
  between operations  7.05 us (4%)
    ppermute x16, starting transfers between devices, passed_along(): return lax.ppermute(block, axis, route)  40.9 us
    dynamic_update_slice x8, local copies, waits for them, and re-layouts, shards(): lax.map(partial(fit_epoch, nearby, column_band, row_band), (images, good_...  19.6 us
    ppermute x16, waiting for transfers between devices, passed_along(): return lax.ppermute(block, axis, route)  14.8 us
    while x72, local copies, waits for them, and re-layouts  14.3 us
    dot_general x12, matrix products, fit_epoch(): jnp.einsum('jyb,ibx->ijyx', row_band[3 * spread:3 * spread + 3], window,...  13.4 us
    another operation x12, other arithmetic, fit_epoch(): factor = jnp.linalg.cholesky(normal)  12.8 us
    another operation x8, other arithmetic, fit_epoch(): coefficients = jax.scipy.linalg.cho_solve((factor, True), target)  10.9 us
    dot_general x48, matrix products, fit_epoch(): jnp.einsum('yw,iwx->iyx', window, column_band[3 * spread:3 * spread + 3],...  9.94 us
  transfers between devices with their start and end apart: 16, of which 5 were waited for; matrix products, arithmetic and copies ran while one was open for 5% of the time, Pallas kernels for 0%

commit v1 on v0

v1 whole, which is shorter than its diff:
```python
from functools import partial

import jax
import jax.numpy as jnp
import numpy as np
from jax import lax
from jax.experimental import pallas as pl
from jax.experimental.pallas import tpu as pltpu
from jax.sharding import PartitionSpec as P

RADIUS = 4
KHALF = 9
SIGMAS = (1.0, 2.0, 4.0)
DEGREES = 3
NBASIS = (len(SIGMAS) * DEGREES) * DEGREES
RIDGE_TERM = 0.1
AXIS = "epoch"
CORES = 2
REACH = RADIUS // CORES
LANES = 128
SUB = 8
TAPS = 2 * KHALF + 1
SLOT = 32


def kernel_taps():
    places = np.arange(-KHALF, KHALF + 1).astype(np.float64)
    profiles = []
    for spread in SIGMAS:
        for degree in range(DEGREES):
            profile = places**degree * np.exp(-places * places / (2.0 * spread * spread))
            profiles.append(profile / np.sqrt(np.sum(profile * profile)))
    return np.stack(profiles).astype(np.float32).astype(jnp.bfloat16)


def column_bands(taps):
    kernels = taps.shape[0]
    bands = np.zeros((2 * LANES, kernels, LANES), taps.dtype)
    for x in range(LANES):
        for tap in range(TAPS):
            bands[x + 2 * KHALF - tap, :, x] = taps[:, tap]
    return bands.reshape(2 * LANES, kernels * LANES)


def row_bands(taps, rows):
    bands = np.zeros((len(SIGMAS), rows // SUB, DEGREES, SUB, rows), taps.dtype)
    for y in range(rows):
        for tap in range(TAPS):
            source = y - tap + KHALF
            if 0 <= source < rows:
                bands[:, y // SUB, :, y % SUB, source] = taps[:, tap].reshape(len(SIGMAS), DEGREES)
    return bands.reshape(len(SIGMAS), rows * DEGREES, rows)


def split3(x):
    high = x.astype(jnp.bfloat16)
    rest = x - high.astype(jnp.float32)
    middle = rest.astype(jnp.bfloat16)
    low = (rest - middle.astype(jnp.float32)).astype(jnp.bfloat16)
    return high, middle, low


def fit_kernel(
    select_ref,
    own_ref,
    other_ref,
    near_ref,
    far_ref,
    swapped_near_ref,
    swapped_far_ref,
    images_ref,
    good_ref,
    column_ref,
    row_ref,
    coefs_ref,
    own_sum_ref,
    near_sum_ref,
    far_sum_ref,
    swap_sum_ref,
    window_ref,
    smooth_ref,
    basis_ref,
    sums_ref,
):
    epochs, rows, cols = images_ref.shape
    blocks = cols // LANES
    groups = rows // SUB
    planes = NBASIS + 1
    height = planes * SUB
    kernels = len(SIGMAS) * DEGREES
    f32, bf16 = jnp.float32, jnp.bfloat16

    sources = [
        own_ref.at[0],
        other_ref.at[0],
        near_ref.at[0],
        near_ref.at[1],
        far_ref.at[0],
        far_ref.at[1],
        swapped_near_ref.at[0],
        swapped_near_ref.at[1],
        swapped_far_ref.at[0],
        swapped_far_ref.at[1],
    ]
    lane = lax.broadcasted_iota(jnp.int32, (rows, cols + LANES), 1)
    inside = jnp.logical_and(lane >= KHALF, lane < cols + KHALF)
    for e in range(epochs):
        for index, source in enumerate(sources):

            @pl.when(select_ref[e] == index)
            def _():
                template = source[...].astype(f32)
                wide = jnp.concatenate([template, template[:, :LANES]], 1)
                wide = jnp.where(inside, pltpu.roll(wide, KHALF, 1), 0.0).astype(bf16)
                for b in range(blocks):
                    at = (e * blocks + b) * rows
                    window_ref[at : at + rows, :] = wide[:, b * LANES : (b + 2) * LANES]

    sums_ref[...] = jnp.zeros_like(sums_ref)

    for k in range(kernels):
        smooth_ref[:, k * LANES : (k + 1) * LANES] = jnp.dot(
            window_ref[...],
            column_ref[:, k * LANES : (k + 1) * LANES],
            preferred_element_type=f32,
        ).astype(bf16)

    row_a = lax.broadcasted_iota(jnp.int32, (height, height), 0)
    row_b = lax.broadcasted_iota(jnp.int32, (height, height), 1)
    same_row = row_a % SUB == row_b % SUB
    plane_of = lax.broadcasted_iota(jnp.int32, (height, LANES), 0) // SUB
    lane_of = lax.broadcasted_iota(jnp.int32, (height, LANES), 1)
    packed = jnp.zeros((height, LANES), f32)
    for e in range(epochs):
        for b in range(blocks):
            at = (e * blocks + b) * rows
            weight = good_ref[e, :, b * LANES : (b + 1) * LANES].astype(f32)
            image = images_ref[e, :, b * LANES : (b + 1) * LANES].astype(f32)
            out = [
                jnp.dot(
                    row_ref[s],
                    smooth_ref[at : at + rows, s * DEGREES * LANES : (s + 1) * DEGREES * LANES],
                    preferred_element_type=f32,
                )
                for s in range(len(SIGMAS))
            ]
            for g in range(groups):
                tiles = [
                    out[s][(g * DEGREES + j) * SUB : (g * DEGREES + j + 1) * SUB, i * LANES : (i + 1) * LANES]
                    for s in range(len(SIGMAS))
                    for i in range(DEGREES)
                    for j in range(DEGREES)
                ]
                mask = weight[g * SUB : (g + 1) * SUB]
                tiles = [tile * mask for tile in tiles + [image[g * SUB : (g + 1) * SUB]]]
                at_lane = g * cols + b * LANES
                basis_ref[e, :, at_lane : at_lane + LANES] = jnp.concatenate(tiles, 0).astype(bf16)
        basis = basis_ref[e]
        gram = lax.dot_general(
            basis, basis, (((1,), (1,)), ((), ())), preferred_element_type=f32
        )
        gram = jnp.where(same_row, gram, 0.0)
        place = (lane_of == plane_of + e * SLOT).astype(bf16)
        for part in split3(gram):
            packed = packed + jnp.dot(part, place, preferred_element_type=f32)
    fold = (
        lax.broadcasted_iota(jnp.int32, (SLOT, height), 0)
        == lax.broadcasted_iota(jnp.int32, (SLOT, height), 1) // SUB
    ).astype(bf16)
    system = jnp.zeros((SLOT, LANES), f32)
    for part in split3(packed):
        system = system + jnp.dot(fold, part, preferred_element_type=f32)
    plane = lax.broadcasted_iota(jnp.int32, (SLOT, LANES), 0)
    lane = lax.broadcasted_iota(jnp.int32, (SLOT, LANES), 1)
    slot = lane % SLOT
    system = system / (rows * cols) + jnp.where(plane == slot, RIDGE_TERM, 0.0)
    start = lane - slot
    for p in range(NBASIS):
        pivot_row = jnp.broadcast_to(system[p : p + 1], (SLOT, LANES))
        column = jnp.take_along_axis(system, start + p, axis=1)
        pivot = jnp.broadcast_to(column[p : p + 1], (SLOT, LANES))
        factor = jnp.where(plane == p, 0.0, column / pivot)
        system = system - factor * pivot_row
    diagonal = jnp.sum(jnp.where(plane == slot, system, 0.0), 0, keepdims=True)
    pivots = jnp.take_along_axis(
        jnp.broadcast_to(diagonal, (SLOT, LANES)), start + plane, axis=1
    )
    solved = jnp.take_along_axis(system, start + NBASIS, axis=1) / jnp.where(plane < NBASIS, pivots, 1.0)
    for e in range(epochs):
        column = jnp.broadcast_to(solved[:, e * SLOT : e * SLOT + 1], (SLOT, LANES))
        as_row = jnp.sum(jnp.where(plane == lane, column, 0.0), 0, keepdims=True)
        coefs_ref[e : e + 1, :] = as_row[:, :NBASIS]
        scale = [jnp.broadcast_to(column[k : k + 1], (SUB, LANES)) for k in range(NBASIS)]
        target = select_ref[e]
        for g in range(groups):
            for b in range(blocks):
                at_lane = g * cols + b * LANES
                tile = basis_ref[e, :, at_lane : at_lane + LANES].astype(f32)
                value = tile[NBASIS * SUB : planes * SUB]
                for k in range(NBASIS):
                    value = value - scale[k] * tile[k * SUB : (k + 1) * SUB]
                here = (target, slice(g * SUB, (g + 1) * SUB), slice(b * LANES, (b + 1) * LANES))
                sums_ref[here] = sums_ref[here] + value
    own_sum_ref[...] = sums_ref[0:2]
    near_sum_ref[...] = sums_ref[2:4]
    far_sum_ref[...] = sums_ref[4:6]
    swap_sum_ref[...] = sums_ref[6:10].astype(bf16)


def between_cores(block):
    n = lax.axis_size(AXIS)
    return lax.ppermute(block, AXIS, [(i, i ^ 1) for i in range(n)])


def between_chips(block, distance):
    chips = lax.axis_size(AXIS) // CORES
    route = []
    for chip in range(chips):
        for core in range(CORES):
            origin = chip + (distance if core == 0 else -distance)
            if 0 <= origin < chips:
                route.append((CORES * origin + core, CORES * chip + core))
            else:
                route.append((CORES * chip + 1 - core, CORES * chip + core))
    return lax.ppermute(block, AXIS, route)


def buffer_of(epoch_patch):
    device = lax.axis_index(AXIS)
    core = device % CORES
    chip_offset = epoch_patch // CORES - device // CORES
    same_core = epoch_patch % CORES == core
    side = jnp.where(core == 0, 1, -1)
    far = jnp.abs(chip_offset) - 1
    mine = 2 + 2 * far + jnp.where(same_core, 0, 1)
    theirs = 6 + 2 * far + jnp.where(same_core, 1, 0)
    away = jnp.where(chip_offset * side > 0, mine, theirs)
    return jnp.where(chip_offset == 0, jnp.where(same_core, 0, 1), away).astype(jnp.int32)


def shards(templates, epoch_patch, images, good_pixels):
    epochs, rows, cols = images.shape
    f32, bf16 = jnp.float32, jnp.bfloat16
    assert templates.shape[0] == 1 and epochs * SLOT <= LANES
    assert lax.axis_size(AXIS) % CORES == 0 and cols % LANES == 0 and rows % SUB == 0
    other = between_cores(templates)
    pair = jnp.concatenate([templates, other], 0)
    near, far = between_chips(pair, 1), between_chips(pair, 2)
    swapped_near, swapped_far = between_cores(near), between_cores(far)
    taps = kernel_taps()
    column = jnp.asarray(column_bands(taps))
    row = jnp.asarray(row_bands(taps, rows))
    height = (NBASIS + 1) * SUB
    tiles = epochs * (cols // LANES) * rows
    coefs, own_sum, near_sum, far_sum, swap_sum = pl.pallas_call(
        fit_kernel,
        out_shape=(
            jax.ShapeDtypeStruct((epochs, NBASIS), f32),
            jax.ShapeDtypeStruct((2, rows, cols), f32),
            jax.ShapeDtypeStruct((2, rows, cols), f32),
            jax.ShapeDtypeStruct((2, rows, cols), f32),
            jax.ShapeDtypeStruct((4, rows, cols), bf16),
        ),
        in_specs=[pl.BlockSpec(memory_space=pltpu.SMEM)]
        + [pl.BlockSpec(memory_space=pltpu.VMEM)] * 10,
        out_specs=[pl.BlockSpec(memory_space=pltpu.VMEM)] * 5,
        scratch_shapes=[
            pltpu.VMEM((tiles, 2 * LANES), bf16),
            pltpu.VMEM((tiles, column.shape[1]), bf16),
            pltpu.VMEM((epochs, height, rows // SUB * cols), bf16),
            pltpu.VMEM((10, rows, cols), f32),
        ],
        name="fit",
    )(
        buffer_of(epoch_patch),
        templates,
        other,
        near,
        far,
        swapped_near,
        swapped_far,
        images,
        good_pixels,
        column,
        row,
    )
    received = between_cores(swap_sum)
    near_sum = (near_sum + received[0:2].astype(f32)).astype(bf16)
    far_sum = (far_sum + received[2:4].astype(f32)).astype(bf16)
    near_back, far_back = between_chips(near_sum, -1), between_chips(far_sum, -2)
    total = own_sum + near_back.astype(f32) + far_back.astype(f32)
    deep_sum = total[0:1] + between_cores(total[1:2].astype(bf16)).astype(f32)
    return (deep_sum, coefs)


def solution(mesh):
    spec = P(("tract", AXIS), None, None)
    in_specs = (spec, P(("tract", AXIS)), spec, spec)
    out_specs = (spec, P(("tract", AXIS), None))
    return jax.shard_map(shards, mesh=mesh, in_specs=in_specs, out_specs=out_specs, check_vma=False)
```

time: 191 us -> 39.8 us (0.21)
  matrix products: 44.6 us -> 0 us
  other arithmetic: 44.1 us -> 2.49 us
  local copies, waits for them, and re-layouts: 36.6 us -> 2.13 us
  starting transfers between devices: 40.9 us -> 8.5 us
  Pallas kernels: 0 us -> 15.7 us
  between operations: 7.05 us -> 0.69 us
  waiting for transfers between devices: 14.8 us -> 9.94 us
    dot_general x85 -> x0, matrix products: 43.5 us -> none  [the longest x12 13.4 us: fit_epoch(): jnp.einsum('jyb,ibx->ijyx', row_band[3 * spread:3 * spread + 3], window,...]
    ppermute x16 -> x9, starting transfers between devices: 40.9 us -> 8.5 us  [the longest x4 6.29 us: between_chips(): return lax.ppermute(block, AXIS, route)]
    another operation x25 -> x0, other arithmetic: 23.8 us -> none  [the longest x12 12.8 us: fit_epoch(): factor = jnp.linalg.cholesky(normal)]
    dynamic_update_slice x8 -> x0, local copies, waits for them, and re-layouts: 19.6 us -> none  [shards(): lax.map(partial(fit_epoch, nearby, column_band, row_band), (images, good_...]
    pallas_call x0 -> x1, Pallas kernels: none -> 15.7 us  [shards(): pl.pallas_call(fit_kernel, out_shape=(jax.ShapeDtypeStruct((epochs, NBASI...]
    while x72 -> x0, local copies, waits for them, and re-layouts: 14.3 us -> none
    while x4 -> x0, other arithmetic: 6.34 us -> none
    reduce_sum x9 -> x0, other arithmetic: 5.75 us -> none  [kernel_taps(): profiles.append(profile / jnp.sqrt(jnp.sum(profile * profile)))]
  transfers between devices with their start and end apart: 16 -> 9, of which waited for: 5 -> 8; matrix products, arithmetic and copies ran while one was open for 5% -> 4% of each run, Pallas kernels for 0% -> 0%
where the time goes in v1:
time: 39.8 us; the launch traced here: 39.4 us
  Pallas kernels  15.7 us (39%)
  waiting for transfers between devices  9.94 us (25%)
  starting transfers between devices  8.5 us (21%)
  other arithmetic  2.49 us (6%)
  local copies, waits for them, and re-layouts  2.13 us (5%)
  between operations  0.69 us (2%)
    pallas_call x1, Pallas kernels, shards(): pl.pallas_call(fit_kernel, out_shape=(jax.ShapeDtypeStruct((epochs, NBASI...  15.7 us
    ppermute x4, starting transfers between devices, between_chips(): return lax.ppermute(block, AXIS, route)  6.29 us
    ppermute x4, waiting for transfers between devices, between_chips(): return lax.ppermute(block, AXIS, route)  6.01 us
    ppermute x5, waiting for transfers between devices, between_cores(): return lax.ppermute(block, AXIS, [(i, i ^ 1) for i in range(n)])  3.93 us
    ppermute x5, starting transfers between devices, between_cores(): return lax.ppermute(block, AXIS, [(i, i ^ 1) for i in range(n)])  2.21 us
    unnamed x15, local copies, waits for them, and re-layouts  2.11 us
    convert_element_type x1, other arithmetic, shards(): near_sum = (near_sum + received[0:2].astype(f32)).astype(bf16)  1.15 us
  transfers between devices with their start and end apart: 9, of which 8 were waited for; matrix products, arithmetic and copies ran while one was open for 4% of the time, Pallas kernels for 0%

profile of v1, /device:TPU:1, one launch (start us, length us, event | category | flops | bytes accessed | tf_op | source)
XLA Modules:
  0.0 39.4 jit_solution(4902388961543011996)
XLA Ops:
  0.6 0.1 collective-permute-start
  0.7 0.8 %constant_dynamic-update-slice_fusion.1 = bf16[2,64,512]{2,1,0:T(8,128)(2,1)S(1)} fusion(bf16[1,64,512]{2,1,0:T(8,128)(2,1)} %own_ref.1), kind=kLoop, calls=%fused_computation.6 | loop fusion | bytes 131072
  1.6 0.6 %collective-permute-done.other_ref = bf16[1,64,512]{2,1,0:T(8,128)(2,1)S(1)} collective-permute-done((bf16[1,64,512]{2,1,0:T(8,128)(2,1)}, bf16[1,64,512]{2,1,0:T(8,128)(2,1)S(1)}, u32[]{:S(2)}, u32[]{:S(2)}) %collective-permute-start) | collective-permute-done | bytes 65568 | tf_op jit(solution)/shard_map/ppermute | solution.py:212
  2.2 0.0 copy-start.1
  2.2 0.6 %copy-done.1 = bf16[1,64,512]{2,1,0:T(8,128)(2,1)} copy-done((bf16[1,64,512]{2,1,0:T(8,128)(2,1)}, bf16[1,64,512]{2,1,0:T(8,128)(2,1)S(1)}, u32[]{:S(2)}) %copy-start.1) | copy-done | bytes 65560
  2.8 2.4 %collective-permute-start.2 = (bf16[2,64,512]{2,1,0:T(8,128)(2,1)S(1)}, bf16[2,64,512]{2,1,0:T(8,128)(2,1)S(1)}, u32[]{:S(2)}, u32[]{:S(2)}) collective-permute-start(bf16[2,64,512]{2,1,0:T(8,128)(2,1)S(1)} %constant_dynamic-update-slice_fusion), channel_id=1, source_target_pairs={{4,0},{0,1},{6,2},{2,3},{8,4},{1,5},{10,6},{3,7},{12,8},{5,9},{14,... | collective-permute-start | bytes 393224 | tf_op jit(solution)/shard_map/ppermute | solution.py:225
  5.2 1.2 %collective-permute-start.1 = (bf16[2,64,512]{2,1,0:T(8,128)(2,1)S(1)}, bf16[2,64,512]{2,1,0:T(8,128)(2,1)S(1)}, u32[]{:S(2)}, u32[]{:S(2)}) collective-permute-start(bf16[2,64,512]{2,1,0:T(8,128)(2,1)S(1)} %constant_dynamic-update-slice_fusion), channel_id=1, source_target_pairs={{2,0},{0,1},{4,2},{1,3},{6,4},{3,5},{8,6},{5,7},{10,8},{7,9},{12,1... | collective-permute-start | bytes 393224 | tf_op jit(solution)/shard_map/ppermute | solution.py:225
  6.5 0.0 copy-start.6
  6.5 0.7 %collective-permute-done.2.far_ref = bf16[2,64,512]{2,1,0:T(8,128)(2,1)S(1)} collective-permute-done((bf16[2,64,512]{2,1,0:T(8,128)(2,1)S(1)}, bf16[2,64,512]{2,1,0:T(8,128)(2,1)S(1)}, u32[]{:S(2)}, u32[]{:S(2)}) %collective-permute-start.2) | collective-permute-done | bytes 131104 | tf_op jit(solution)/shard_map/ppermute | solution.py:225
  7.2 0.0 copy-start.2
  7.2 1.6 %collective-permute-start.4 = (bf16[2,64,512]{2,1,0:T(8,128)(2,1)S(1)}, bf16[2,64,512]{2,1,0:T(8,128)(2,1)S(1)}, u32[]{:S(2)}, u32[]{:S(2)}) collective-permute-start(bf16[2,64,512]{2,1,0:T(8,128)(2,1)S(1)} %collective-permute-done.2.far_ref), channel_id=1, source_target_pairs={{0,1},{1,0},{2,3},{3,2},{4,5},{5,4},{6,7},{7,6},{8,9},{9,8},{10,11... | collective-permute-start | bytes 393224 | tf_op jit(solution)/shard_map/ppermute | solution.py:212
  8.8 1.0 %collective-permute-done.1.near_ref = bf16[2,64,512]{2,1,0:T(8,128)(2,1)S(1)} collective-permute-done((bf16[2,64,512]{2,1,0:T(8,128)(2,1)S(1)}, bf16[2,64,512]{2,1,0:T(8,128)(2,1)S(1)}, u32[]{:S(2)}, u32[]{:S(2)}) %collective-permute-start.1) | collective-permute-done | bytes 131104 | tf_op jit(solution)/shard_map/ppermute | solution.py:225
  9.8 0.0 copy-start.3
  9.8 0.0 collective-permute-start.3
  9.8 0.0 copy-done.6
  9.8 0.6 %compare_select_fusion.1.select_ref = s32[4]{0:T(128)} fusion(s32[4]{0:T(128)S(1)} %copy-done.6, s32[]{:T(128)S(6)} %select_n.46, s32[]{:T(128)S(6)} %select_n.44, s32[]{:T(128)S(6)} %select_n.42), kind=kLoop, calls=%fused_computation.9 | loop fusion | flops 140 | bytes 44 | tf_op jit(solution)/shard_map/jit(_where)/select_n | solution.py:238
  10.4 0.0 collective-permute-done.4.swapped_far_ref
  10.4 0.0 copy-start.4
  10.4 0.7 %collective-permute-done.3.swapped_near_ref = bf16[2,64,512]{2,1,0:T(8,128)(2,1)S(1)} collective-permute-done((bf16[2,64,512]{2,1,0:T(8,128)(2,1)S(1)}, bf16[2,64,512]{2,1,0:T(8,128)(2,1)S(1)}, u32[]{:S(2)}, u32[]{:S(2)}) %collective-permute-start.3) | collective-permute-done | bytes 131104 | tf_op jit(solution)/shard_map/ppermute | solution.py:212
  11.1 0.0 copy-done.2
  11.1 0.0 copy-done.3
  11.1 0.0 copy-done.4
  11.1 0.0 copy-start.5
  11.1 0.6 %copy-done.5 = bf16[2,64,512]{2,1,0:T(8,128)(2,1)} copy-done((bf16[2,64,512]{2,1,0:T(8,128)(2,1)}, bf16[2,64,512]{2,1,0:T(8,128)(2,1)S(1)}, u32[]{:S(2)}) %copy-start.5) | copy-done | bytes 131096
  11.8 15.7 %fit.1 = (f32[4,27]{1,0:T(4,128)}, f32[2,64,512]{2,1,0:T(8,128)}, f32[2,64,512]{2,1,0:T(8,128)}, f32[2,64,512]{2,1,0:T(8,128)}, bf16[4,64,512]{2,1,0:T(8,128)(2,1)}) custom-call(s32[4]{0:T(128)} %compare_select_fusion.1.select_ref, bf16[1,64,512]{2,1,0:T(8,128)(2,1)} %own_ref.1, bf16[1,64,512]{2,1,0:T(8,128)(2,1)} %copy-done.1, ...), custom_call_target="tpu_custom_call" | custom-call | tf_op jit(solution)/shard_map/fit/pallas_call | solution.py:255
  27.5 0.4 %collective-permute-start.5 = (bf16[4,64,512]{2,1,0:T(8,128)(2,1)}, bf16[4,64,512]{2,1,0:T(8,128)(2,1)S(1)}, u32[]{:S(2)}, u32[]{:S(2)}) collective-permute-start(bf16[4,64,512]{2,1,0:T(8,128)(2,1)} %get-tuple-element.9), channel_id=1, source_target_pairs={{0,1},{1,0},{2,3},{3,2},{4,5},{5,4},{6,7},{7,6},{8,9},{9,8},{10,11... | collective-permute-start | bytes 786440 | tf_op jit(solution)/shard_map/ppermute | solution.py:212
  27.9 1.4 %collective-permute-done.5 = bf16[4,64,512]{2,1,0:T(8,128)(2,1)S(1)} collective-permute-done((bf16[4,64,512]{2,1,0:T(8,128)(2,1)}, bf16[4,64,512]{2,1,0:T(8,128)(2,1)S(1)}, u32[]{:S(2)}, u32[]{:S(2)}) %collective-permute-start.5) | collective-permute-done | bytes 262176 | tf_op jit(solution)/shard_map/ppermute | solution.py:212
  29.3 0.0 copy-start
  29.3 1.1 %add_convert_fusion.1 = (bf16[2,64,512]{2,1,0:T(8,128)(2,1)S(1)}, bf16[2,64,512]{2,1,0:T(8,128)(2,1)S(1)}) fusion(f32[2,64,512]{2,1,0:T(8,128)} %get-tuple-element.8, bf16[4,64,512]{2,1,0:T(8,128)(2,1)S(1)} %collective-permute-done.5, f32[2,64,512]{2,1,0:T(8,128)} %get-tuple-element.10), kind=kLoop, calls=%fused_computation.2 | loop fusion | flops 393216 | bytes 1048576 | tf_op jit(solution)/shard_map/convert_element_type | solution.py:288
  30.4 0.4 %collective-permute-start.6 = (bf16[2,64,512]{2,1,0:T(8,128)(2,1)S(1)}, bf16[2,64,512]{2,1,0:T(8,128)(2,1)S(1)}, u32[]{:S(2)}, u32[]{:S(2)}) collective-permute-start(bf16[2,64,512]{2,1,0:T(8,128)(2,1)S(1)} %get-tuple-element.12), channel_id=1, source_target_pairs={{1,0},{3,1},{0,2},{5,3},{2,4},{7,5},{4,6},{9,7},{6,8},{11,9},{8,10... | collective-permute-start | bytes 393224 | tf_op jit(solution)/shard_map/ppermute | solution.py:225
  30.9 2.2 %collective-permute-start.7 = (bf16[2,64,512]{2,1,0:T(8,128)(2,1)S(1)}, bf16[2,64,512]{2,1,0:T(8,128)(2,1)S(1)}, u32[]{:S(2)}, u32[]{:S(2)}) collective-permute-start(bf16[2,64,512]{2,1,0:T(8,128)(2,1)S(1)} %get-tuple-element.13), channel_id=1, source_target_pairs={{1,0},{5,1},{3,2},{7,3},{0,4},{9,5},{2,6},{11,7},{4,8},{13,9},{6,1... | collective-permute-start | bytes 393224 | tf_op jit(solution)/shard_map/ppermute | solution.py:225
  33.0 1.7 %collective-permute-done.6 = bf16[2,64,512]{2,1,0:T(8,128)(2,1)S(1)} collective-permute-done((bf16[2,64,512]{2,1,0:T(8,128)(2,1)S(1)}, bf16[2,64,512]{2,1,0:T(8,128)(2,1)S(1)}, u32[]{:S(2)}, u32[]{:S(2)}) %collective-permute-start.6) | collective-permute-done | bytes 131104 | tf_op jit(solution)/shard_map/ppermute | solution.py:225
  34.8 2.6 %collective-permute-done.7 = bf16[2,64,512]{2,1,0:T(8,128)(2,1)S(1)} collective-permute-done((bf16[2,64,512]{2,1,0:T(8,128)(2,1)S(1)}, bf16[2,64,512]{2,1,0:T(8,128)(2,1)S(1)}, u32[]{:S(2)}, u32[]{:S(2)}) %collective-permute-start.7) | collective-permute-done | bytes 131104 | tf_op jit(solution)/shard_map/ppermute | solution.py:225
  37.4 0.0 copy-done
  37.4 0.1 collective-permute-start.8
  37.5 1.2 %collective-permute-done.8 = bf16[1,64,512]{2,1,0:T(8,128)(2,1)S(1)} collective-permute-done((bf16[1,64,512]{2,1,0:T(8,128)(2,1)S(1)}, bf16[1,64,512]{2,1,0:T(8,128)(2,1)S(1)}, u32[]{:S(2)}, u32[]{:S(2)}) %collective-permute-start.8) | collective-permute-done | bytes 65568 | tf_op jit(solution)/shard_map/ppermute | solution.py:212
  38.8 0.7 %slice_add_fusion = f32[1,64,512]{2,1,0:T(8,128)} fusion(f32[2,64,512]{2,1,0:T(8,128)S(1)} %convert_add_fusion, bf16[1,64,512]{2,1,0:T(8,128)(2,1)S(1)} %collective-permute-done.8), kind=kLoop, calls=%fused_computation.4 | loop fusion | flops 65536 | bytes 327680 | tf_op jit(solution)/shard_map/add | solution.py:292
  (3 shorter events, 0.1 us)
Async XLA Ops:
  0.6 1.5 %collective-permute-start = (bf16[1,64,512]{2,1,0:T(8,128)(2,1)}, bf16[1,64,512]{2,1,0:T(8,128)(2,1)S(1)}, u32[]{:S(2)}, u32[]{:S(2)}) collective-permute-start(bf16[1,64,512]{2,1,0:T(8,128)(2,1)} %own_ref.1), channel_id=1, source_target_pairs={{0,1},{1,0},{2,3},{3,2},{4,5},{5,4},{6,7},{7,6},{8,9},{9,8},{10,11... | collective-permute-start | bytes 196616 | tf_op jit(solution)/shard_map/ppermute | solution.py:212
  2.2 0.6 %copy-start.1 = (bf16[1,64,512]{2,1,0:T(8,128)(2,1)}, bf16[1,64,512]{2,1,0:T(8,128)(2,1)S(1)}, u32[]{:S(2)}) copy-start(bf16[1,64,512]{2,1,0:T(8,128)(2,1)S(1)} %collective-permute-done.other_ref) | copy-start | bytes 196612
  2.8 4.4 %collective-permute-start.2 = (bf16[2,64,512]{2,1,0:T(8,128)(2,1)S(1)}, bf16[2,64,512]{2,1,0:T(8,128)(2,1)S(1)}, u32[]{:S(2)}, u32[]{:S(2)}) collective-permute-start(bf16[2,64,512]{2,1,0:T(8,128)(2,1)S(1)} %constant_dynamic-update-slice_fusion), channel_id=1, source_target_pairs={{4,0},{0,1},{6,2},{2,3},{8,4},{1,5},{10,6},{3,7},{12,8},{5,9},{14,... | collective-permute-start | bytes 393224 | tf_op jit(solution)/shard_map/ppermute | solution.py:225
  5.2 4.6 %collective-permute-start.1 = (bf16[2,64,512]{2,1,0:T(8,128)(2,1)S(1)}, bf16[2,64,512]{2,1,0:T(8,128)(2,1)S(1)}, u32[]{:S(2)}, u32[]{:S(2)}) collective-permute-start(bf16[2,64,512]{2,1,0:T(8,128)(2,1)S(1)} %constant_dynamic-update-slice_fusion), channel_id=1, source_target_pairs={{2,0},{0,1},{4,2},{1,3},{6,4},{3,5},{8,6},{5,7},{10,8},{7,9},{12,1... | collective-permute-start | bytes 393224 | tf_op jit(solution)/shard_map/ppermute | solution.py:225
  6.5 3.3 %copy-start.6 = (s32[4]{0:T(128)S(1)}, s32[4]{0:T(128)}, u32[]{:S(2)}) copy-start(s32[4]{0:T(128)} %param.7) | copy-start | bytes 52
  7.2 4.0 %copy-start.2 = (bf16[2,64,512]{2,1,0:T(8,128)(2,1)}, bf16[2,64,512]{2,1,0:T(8,128)(2,1)S(1)}, u32[]{:S(2)}) copy-start(bf16[2,64,512]{2,1,0:T(8,128)(2,1)S(1)} %collective-permute-done.2.far_ref) | copy-start | bytes 393220
  7.2 3.2 %collective-permute-start.4 = (bf16[2,64,512]{2,1,0:T(8,128)(2,1)S(1)}, bf16[2,64,512]{2,1,0:T(8,128)(2,1)S(1)}, u32[]{:S(2)}, u32[]{:S(2)}) collective-permute-start(bf16[2,64,512]{2,1,0:T(8,128)(2,1)S(1)} %collective-permute-done.2.far_ref), channel_id=1, source_target_pairs={{0,1},{1,0},{2,3},{3,2},{4,5},{5,4},{6,7},{7,6},{8,9},{9,8},{10,11... | collective-permute-start | bytes 393224 | tf_op jit(solution)/shard_map/ppermute | solution.py:212
  9.8 1.4 %copy-start.3 = (bf16[2,64,512]{2,1,0:T(8,128)(2,1)}, bf16[2,64,512]{2,1,0:T(8,128)(2,1)S(1)}, u32[]{:S(2)}) copy-start(bf16[2,64,512]{2,1,0:T(8,128)(2,1)S(1)} %collective-permute-done.1.near_ref) | copy-start | bytes 393220
  9.8 1.3 %collective-permute-start.3 = (bf16[2,64,512]{2,1,0:T(8,128)(2,1)S(1)}, bf16[2,64,512]{2,1,0:T(8,128)(2,1)S(1)}, u32[]{:S(2)}, u32[]{:S(2)}) collective-permute-start(bf16[2,64,512]{2,1,0:T(8,128)(2,1)S(1)} %collective-permute-done.1.near_ref), channel_id=1, source_target_pairs={{0,1},{1,0},{2,3},{3,2},{4,5},{5,4},{6,7},{7,6},{8,9},{9,8},{10,11... | collective-permute-start | bytes 393224 | tf_op jit(solution)/shard_map/ppermute | solution.py:212
  10.4 0.7 %copy-start.4 = (bf16[2,64,512]{2,1,0:T(8,128)(2,1)}, bf16[2,64,512]{2,1,0:T(8,128)(2,1)S(1)}, u32[]{:S(2)}) copy-start(bf16[2,64,512]{2,1,0:T(8,128)(2,1)S(1)} %collective-permute-done.4.swapped_far_ref) | copy-start | bytes 393220
  11.1 0.6 %copy-start.5 = (bf16[2,64,512]{2,1,0:T(8,128)(2,1)}, bf16[2,64,512]{2,1,0:T(8,128)(2,1)S(1)}, u32[]{:S(2)}) copy-start(bf16[2,64,512]{2,1,0:T(8,128)(2,1)S(1)} %collective-permute-done.3.swapped_near_ref) | copy-start | bytes 393220
  27.5 1.8 %collective-permute-start.5 = (bf16[4,64,512]{2,1,0:T(8,128)(2,1)}, bf16[4,64,512]{2,1,0:T(8,128)(2,1)S(1)}, u32[]{:S(2)}, u32[]{:S(2)}) collective-permute-start(bf16[4,64,512]{2,1,0:T(8,128)(2,1)} %get-tuple-element.9), channel_id=1, source_target_pairs={{0,1},{1,0},{2,3},{3,2},{4,5},{5,4},{6,7},{7,6},{8,9},{9,8},{10,11... | collective-permute-start | bytes 786440 | tf_op jit(solution)/shard_map/ppermute | solution.py:212
  29.3 8.1 %copy-start = (f32[2,64,512]{2,1,0:T(8,128)S(1)}, f32[2,64,512]{2,1,0:T(8,128)}, u32[]{:S(2)}) copy-start(f32[2,64,512]{2,1,0:T(8,128)} %get-tuple-element.7) | copy-start | bytes 786436
  30.4 4.3 %collective-permute-start.6 = (bf16[2,64,512]{2,1,0:T(8,128)(2,1)S(1)}, bf16[2,64,512]{2,1,0:T(8,128)(2,1)S(1)}, u32[]{:S(2)}, u32[]{:S(2)}) collective-permute-start(bf16[2,64,512]{2,1,0:T(8,128)(2,1)S(1)} %get-tuple-element.12), channel_id=1, source_target_pairs={{1,0},{3,1},{0,2},{5,3},{2,4},{7,5},{4,6},{9,7},{6,8},{11,9},{8,10... | collective-permute-start | bytes 393224 | tf_op jit(solution)/shard_map/ppermute | solution.py:225
  30.9 6.5 %collective-permute-start.7 = (bf16[2,64,512]{2,1,0:T(8,128)(2,1)S(1)}, bf16[2,64,512]{2,1,0:T(8,128)(2,1)S(1)}, u32[]{:S(2)}, u32[]{:S(2)}) collective-permute-start(bf16[2,64,512]{2,1,0:T(8,128)(2,1)S(1)} %get-tuple-element.13), channel_id=1, source_target_pairs={{1,0},{5,1},{3,2},{7,3},{0,4},{9,5},{2,6},{11,7},{4,8},{13,9},{6,1... | collective-permute-start | bytes 393224 | tf_op jit(solution)/shard_map/ppermute | solution.py:225
  37.4 1.3 %collective-permute-start.8 = (bf16[1,64,512]{2,1,0:T(8,128)(2,1)S(1)}, bf16[1,64,512]{2,1,0:T(8,128)(2,1)S(1)}, u32[]{:S(2)}, u32[]{:S(2)}) collective-permute-start(bf16[1,64,512]{2,1,0:T(8,128)(2,1)S(1)} %slice.25), channel_id=1, source_target_pairs={{0,1},{1,0},{2,3},{3,2},{4,5},{5,4},{6,7},{7,6},{8,9},{9,8},{10,11... | collective-permute-start | bytes 196616 | tf_op jit(solution)/shard_map/ppermute | solution.py:212

commit v2 on v1

v2 whole, which is shorter than its diff:
```python
from functools import partial

import jax
import jax.numpy as jnp
import numpy as np
from jax import lax
from jax.experimental import pallas as pl
from jax.experimental.pallas import tpu as pltpu
from jax.sharding import PartitionSpec as P

RADIUS = 4
KHALF = 9
SIGMAS = (1.0, 2.0, 4.0)
DEGREES = 3
NBASIS = (len(SIGMAS) * DEGREES) * DEGREES
RIDGE_TERM = 0.1
AXIS = "epoch"
CORES = 2
REACH = RADIUS // CORES
LANES = 128
SUB = 8
TAPS = 2 * KHALF + 1
SLOT = 32


def kernel_taps():
    places = np.arange(-KHALF, KHALF + 1).astype(np.float64)
    profiles = []
    for spread in SIGMAS:
        for degree in range(DEGREES):
            profile = places**degree * np.exp(-places * places / (2.0 * spread * spread))
            profiles.append(profile / np.sqrt(np.sum(profile * profile)))
    return np.stack(profiles).astype(np.float32).astype(jnp.bfloat16)


def column_bands(taps):
    kernels = taps.shape[0]
    bands = np.zeros((2 * LANES, kernels, LANES), taps.dtype)
    for x in range(LANES):
        for tap in range(TAPS):
            bands[x + 2 * KHALF - tap, :, x] = taps[:, tap]
    return bands.reshape(2 * LANES, kernels * LANES)


def row_bands(taps, rows):
    bands = np.zeros((len(SIGMAS), rows // SUB, DEGREES, SUB, rows), taps.dtype)
    for y in range(rows):
        for tap in range(TAPS):
            source = y - tap + KHALF
            if 0 <= source < rows:
                bands[:, y // SUB, :, y % SUB, source] = taps[:, tap].reshape(len(SIGMAS), DEGREES)
    return bands.reshape(len(SIGMAS), rows * DEGREES, rows)


def split3(x):
    high = x.astype(jnp.bfloat16)
    rest = x - high.astype(jnp.float32)
    middle = rest.astype(jnp.bfloat16)
    low = (rest - middle.astype(jnp.float32)).astype(jnp.bfloat16)
    return high, middle, low


def plane_order():
    order = []
    n = DEGREES
    for s in range(len(SIGMAS)):
        at = s * n * n
        for i in range(n):
            order += [at + i * n, at + i * n + 1]
        order += [at + 2, at + n + 2]
    order += [s * n * n + 2 * n + 2 for s in range(len(SIGMAS))]
    return order + [NBASIS]


def plane_maps(epochs):
    order = plane_order()
    height = len(order) * SUB
    fold = np.zeros((SLOT, height), np.float32)
    place = np.zeros((epochs, height, LANES), np.float32)
    for position, k in enumerate(order):
        rows = slice(position * SUB, (position + 1) * SUB)
        fold[k, rows] = 1
        for e in range(epochs):
            place[e, rows, e * SLOT + k] = 1
    return fold.astype(jnp.bfloat16), place.reshape(epochs * height, LANES).astype(jnp.bfloat16)


def prepare_kernel(images_hbm, good_hbm, *refs):
    count = (len(refs) - 5) // 2
    images_ref, good_ref, semaphores = refs[-3:]
    masked_ref, weight_ref = refs[count : count + 2]
    moves = [(images_hbm, images_ref), (good_hbm, good_ref)]
    moves += list(zip(refs[:count], refs[count + 2 : -3]))
    copies = [
        pltpu.make_async_copy(source, target, semaphores.at[index])
        for index, (source, target) in enumerate(moves)
    ]
    for copy in copies:
        copy.start()
    copies[0].wait()
    copies[1].wait()
    weight = good_ref[...].astype(jnp.float32)
    weight_ref[...] = weight
    masked_ref[...] = images_ref[...].astype(jnp.float32) * weight
    for copy in copies[2:]:
        copy.wait()


def fit_kernel(
    select_ref,
    pair_ref,
    near_ref,
    far_ref,
    swapped_near_ref,
    swapped_far_ref,
    masked_ref,
    weight_ref,
    column_ref,
    row_ref,
    fold_ref,
    place_ref,
    coefs_ref,
    own_sum_ref,
    near_sum_ref,
    far_sum_ref,
    swap_sum_ref,
    window_ref,
    smooth_ref,
    basis_ref,
    parts_ref,
    sums_ref,
):
    epochs, rows, cols = masked_ref.shape
    blocks = cols // LANES
    groups = rows // SUB
    spreads = len(SIGMAS)
    kernels = spreads * DEGREES
    planes = NBASIS + 1
    height = planes * SUB
    f32, bf16 = jnp.float32, jnp.bfloat16

    sources = [pair_ref, near_ref, far_ref, swapped_near_ref, swapped_far_ref]
    lane = lax.broadcasted_iota(jnp.int32, (rows, cols + LANES), 1)
    inside = jnp.logical_and(lane >= KHALF, lane < cols + KHALF)
    for e in range(epochs):
        for index, source in enumerate(sources):

            @pl.when(select_ref[e] // 2 == index)
            def _():
                template = source[select_ref[e] % 2].astype(f32)
                wide = jnp.concatenate([template, template[:, :LANES]], 1)
                wide = jnp.where(inside, pltpu.roll(wide, KHALF, 1), 0.0).astype(bf16)
                for b in range(blocks):
                    at = (e * blocks + b) * rows
                    window_ref[at : at + rows, :] = wide[:, b * LANES : (b + 2) * LANES]

    sums_ref[...] = jnp.zeros_like(sums_ref)

    for k in range(0, kernels, 2):
        width = min(2, kernels - k)
        out = jnp.dot(
            window_ref[...],
            column_ref[:, k * LANES : (k + width) * LANES],
            preferred_element_type=f32,
        ).astype(bf16)
        for e in range(epochs):
            for b in range(blocks):
                at = (e * blocks + b) * rows
                for w in range(width):
                    to = (k + w) * cols + b * LANES
                    smooth_ref[e, :, to : to + LANES] = out[at : at + rows, w * LANES : (w + 1) * LANES]

    row_a = lax.broadcasted_iota(jnp.int32, (height, height), 0)
    row_b = lax.broadcasted_iota(jnp.int32, (height, height), 1)
    same_row = row_a % SUB == row_b % SUB
    wide = 2 * LANES
    for e in range(epochs):
        for at in range(0, cols, wide):
            held = {}

            def store(pair, first, second):
                for g in range(groups):
                    for h in range(0, wide, LANES):
                        mask = weight_ref[e, g * SUB : (g + 1) * SUB, at + h : at + h + LANES]
                        tiles = [first(g, h) * mask, second(g, h) * mask]
                        to = g * cols + at + h
                        basis_ref[e, 2 * pair * SUB : 2 * (pair + 1) * SUB, to : to + LANES] = (
                            jnp.concatenate(tiles, 0).astype(bf16)
                        )

            def degree(s, i, j):
                def tile(g, h):
                    row = (g * DEGREES + j) * SUB
                    return held[s, i][row : row + SUB, h : h + LANES]

                return tile

            for s in range(spreads):
                for i in range(DEGREES):
                    here = (s * DEGREES + i) * cols + at
                    held[s, i] = jnp.dot(
                        row_ref[s], smooth_ref[e, :, here : here + wide], preferred_element_type=f32
                    )
                    store(s * 4 + i, degree(s, i, 0), degree(s, i, 1))
                    if i == 1:
                        store(s * 4 + 3, degree(s, 0, 2), degree(s, 1, 2))
            store(12, degree(0, 2, 2), degree(1, 2, 2))
            store(
                13,
                degree(2, 2, 2),
                lambda g, h: masked_ref[e, g * SUB : (g + 1) * SUB, at + h : at + h + LANES],
            )
        basis = basis_ref[e]
        gram = lax.dot_general(
            basis, basis, (((1,), (1,)), ((), ())), preferred_element_type=f32
        )
        for index, part in enumerate(split3(jnp.where(same_row, gram, 0.0))):
            parts_ref[index, e] = part
    packed = jnp.zeros((height, LANES), f32)
    for index in range(3):
        for e in range(epochs):
            packed = packed + jnp.dot(
                parts_ref[index, e],
                place_ref[e * height : (e + 1) * height],
                preferred_element_type=f32,
            )
    system = jnp.zeros((SLOT, LANES), f32)
    for part in split3(packed):
        system = system + jnp.dot(fold_ref[...], part, preferred_element_type=f32)
    plane = lax.broadcasted_iota(jnp.int32, (SLOT, LANES), 0)
    lane = lax.broadcasted_iota(jnp.int32, (SLOT, LANES), 1)
    slot = lane % SLOT
    system = system / (rows * cols) + jnp.where(plane == slot, RIDGE_TERM, 0.0)
    start = lane - slot
    for p in range(0, NBASIS, 2):
        single = p == NBASIS - 1
        row_p = jnp.broadcast_to(system[p : p + 1], (SUB, LANES))
        near = start[:SUB] + p
        col_p = jnp.take_along_axis(system, start + p, axis=1)
        a = jnp.take_along_axis(row_p, near, axis=1)
        if single:
            u_p = jnp.concatenate([row_p / a] * (SLOT // SUB), 0)
            system = jnp.where(plane == p, u_p, system - col_p * u_p)
            continue
        row_q = jnp.broadcast_to(system[p + 1 : p + 2], (SUB, LANES))
        col_q = jnp.take_along_axis(system, start + (p + 1), axis=1)
        b = jnp.take_along_axis(row_p, near + 1, axis=1)
        d = jnp.take_along_axis(row_q, near + 1, axis=1)
        scale = 1.0 / (a * d - b * b)
        u_p = jnp.concatenate([(d * row_p - b * row_q) * scale] * (SLOT // SUB), 0)
        u_q = jnp.concatenate([(a * row_q - b * row_p) * scale] * (SLOT // SUB), 0)
        system = jnp.where(
            plane == p, u_p, jnp.where(plane == p + 1, u_q, system - col_p * u_p - col_q * u_q)
        )
    fold = fold_ref[...].astype(f32)
    sub = lax.broadcasted_iota(jnp.int32, (SUB, height), 0)
    of_row = lax.broadcasted_iota(jnp.int32, (SUB, height), 1) % SUB
    for e in range(epochs):
        at = e * SLOT + NBASIS
        column = jnp.broadcast_to(system[:, at : at + 1], (SLOT, LANES))
        coefs_ref[e : e + 1, :] = jnp.sum(jnp.where(plane == lane, column, 0.0), 0, keepdims=True)[
            :, :NBASIS
        ]
        column = jnp.where(plane < NBASIS, -column, jnp.where(plane == NBASIS, 1.0, 0.0))
        column = jnp.concatenate([column, column], 1)[:, :height]
        spread = jnp.sum(fold * column, 0, keepdims=True)
        left = jnp.where(sub == of_row, jnp.broadcast_to(spread, (SUB, height)), 0.0)
        high, middle, low = split3(left)
        left = jnp.concatenate([high, middle, low, jnp.zeros_like(low)], 0)
        target = select_ref[e]
        for g in range(groups):
            value = jnp.dot(
                left, basis_ref[e, :, g * cols : (g + 1) * cols], preferred_element_type=f32
            )
            here = (target, slice(g * SUB, (g + 1) * SUB))
            sums_ref[here] = sums_ref[here] + (
                value[:SUB] + (value[SUB : 2 * SUB] + value[2 * SUB : 3 * SUB])
            )
    own_sum_ref[...] = sums_ref[0:2]
    near_sum_ref[...] = sums_ref[2:4]
    far_sum_ref[...] = sums_ref[4:6]
    swap_sum_ref[...] = sums_ref[6:10].astype(bf16)


def between_cores(block):
    n = lax.axis_size(AXIS)
    return lax.ppermute(block, AXIS, [(i, i ^ 1) for i in range(n)])


def between_chips(block, distance):
    chips = lax.axis_size(AXIS) // CORES
    route = []
    for chip in range(chips):
        for core in range(CORES):
            origin = chip + (distance if core == 0 else -distance)
            if 0 <= origin < chips:
                route.append((CORES * origin + core, CORES * chip + core))
            else:
                route.append((CORES * chip + 1 - core, CORES * chip + core))
    return lax.ppermute(block, AXIS, route)


def buffer_of(epoch_patch):
    device = lax.axis_index(AXIS)
    core = device % CORES
    chip_offset = epoch_patch // CORES - device // CORES
    same_core = epoch_patch % CORES == core
    side = jnp.where(core == 0, 1, -1)
    far = jnp.abs(chip_offset) - 1
    mine = 2 + 2 * far + jnp.where(same_core, 0, 1)
    theirs = 6 + 2 * far + jnp.where(same_core, 1, 0)
    away = jnp.where(chip_offset * side > 0, mine, theirs)
    return jnp.where(chip_offset == 0, jnp.where(same_core, 0, 1), away).astype(jnp.int32)


def shards(templates, epoch_patch, images, good_pixels):
    epochs, rows, cols = images.shape
    f32, bf16 = jnp.float32, jnp.bfloat16
    assert templates.shape[0] == 1 and epochs * SLOT <= LANES
    assert lax.axis_size(AXIS) % CORES == 0 and cols % LANES == 0 and rows % SUB == 0
    other = between_cores(templates)
    pair = jnp.concatenate([templates, other], 0)
    near, far = between_chips(pair, 1), between_chips(pair, 2)
    swapped_near, swapped_far = between_cores(near), between_cores(far)
    taps = kernel_taps()
    height = (NBASIS + 1) * SUB
    tiles = epochs * (cols // LANES) * rows
    vmem, vmem_spec = pltpu.VMEM, pl.BlockSpec(memory_space=pltpu.VMEM)
    constants = (column_bands(taps), row_bands(taps, rows)) + plane_maps(epochs)
    sources = (images, good_pixels, *(jnp.asarray(c) for c in constants))
    prepared = pl.pallas_call(
        prepare_kernel,
        out_shape=[vmem((epochs, rows, cols), f32)] * 2 + [vmem(c.shape, bf16) for c in constants],
        in_specs=[pl.BlockSpec(memory_space=pltpu.HBM)] * (2 + len(constants)),
        out_specs=[vmem_spec] * (2 + len(constants)),
        scratch_shapes=[
            vmem(images.shape, bf16),
            vmem(good_pixels.shape, jnp.int32),
            pltpu.SemaphoreType.DMA((2 + len(constants),)),
        ],
        compiler_params=pltpu.CompilerParams(vmem_limit_bytes=4 << 20),
        name="prepare",
    )(*(pltpu.with_memory_space_constraint(x, pltpu.HBM) for x in sources))
    operands = (pair, near, far, swapped_near, swapped_far, *prepared)
    coefs, own_sum, near_sum, far_sum, swap_sum = pl.pallas_call(
        fit_kernel,
        out_shape=(
            jax.ShapeDtypeStruct((epochs, NBASIS), f32),
            vmem((2, rows, cols), f32),
            vmem((2, rows, cols), f32),
            vmem((2, rows, cols), f32),
            vmem((4, rows, cols), bf16),
        ),
        in_specs=[pl.BlockSpec(memory_space=pltpu.SMEM)] + [vmem_spec] * len(operands),
        out_specs=[vmem_spec] * 5,
        scratch_shapes=[
            vmem((tiles, 2 * LANES), bf16),
            vmem((epochs, rows, taps.shape[0] * cols), bf16),
            vmem((epochs, height, rows // SUB * cols), bf16),
            vmem((3, epochs, height, height), bf16),
            vmem((10, rows, cols), f32),
        ],
        compiler_params=pltpu.CompilerParams(vmem_limit_bytes=32 << 20),
        name="fit",
    )(
        buffer_of(epoch_patch),
        *(pltpu.with_memory_space_constraint(x, pltpu.VMEM) for x in operands),
    )
    received = between_cores(swap_sum)
    near_sum = (near_sum + received[0:2].astype(f32)).astype(bf16)
    far_sum = (far_sum + received[2:4].astype(f32)).astype(bf16)
    near_back, far_back = between_chips(near_sum, -1), between_chips(far_sum, -2)
    total = own_sum + near_back.astype(f32) + far_back.astype(f32)
    deep_sum = total[0:1] + between_cores(total[1:2].astype(bf16)).astype(f32)
    return (deep_sum, coefs)


def solution(mesh):
    spec = P(("tract", AXIS), None, None)
    in_specs = (spec, P(("tract", AXIS)), spec, spec)
    out_specs = (spec, P(("tract", AXIS), None))
    return jax.shard_map(shards, mesh=mesh, in_specs=in_specs, out_specs=out_specs, check_vma=False)
```

time: 39.8 us -> 31.7 us (0.80)
  Pallas kernels: 15.7 us -> 11.6 us
  other arithmetic: 2.49 us -> 0.8 us
  local copies, waits for them, and re-layouts: 2.13 us -> 0.86 us
  starting transfers between devices: 8.5 us -> 7.26 us
    pallas_call x1, Pallas kernels: 15.7 us -> 10.1 us  [shards(): pl.pallas_call(fit_kernel, out_shape=(jax.ShapeDtypeStruct((epochs, NBASI...]
    pallas_call x0 -> x1, Pallas kernels: none -> 1.48 us  [shards(): pl.pallas_call(prepare_kernel, out_shape=[vmem((epochs, rows, cols), f32)...]
    unnamed x15 -> x3, local copies, waits for them, and re-layouts: 2.11 us -> 0.85 us
    convert_element_type x1, other arithmetic: 1.15 us -> 0.07 us  [shards(): near_sum = (near_sum + received[0:2].astype(f32)).astype(bf16)]
    ppermute x5, starting transfers between devices: 2.21 us -> 1.2 us  [between_cores(): return lax.ppermute(block, AXIS, [(i, i ^ 1) for i in range(n)])]
    ppermute x5, waiting for transfers between devices: 3.93 us -> 4.55 us  [between_cores(): return lax.ppermute(block, AXIS, [(i, i ^ 1) for i in range(n)])]
    select_n x1, other arithmetic: 0.63 us -> 0.02 us  [buffer_of(): jnp.where(chip_offset == 0, jnp.where(same_core, 0, 1), away)]
    ppermute x4, waiting for transfers between devices: 6.01 us -> 5.55 us  [between_chips(): return lax.ppermute(block, AXIS, route)]
  transfers between devices with their start and end apart: 9 -> 9, of which waited for: 8 -> 7; matrix products, arithmetic and copies ran while one was open for 4% -> 3% of each run, Pallas kernels for 0% -> 5%
where the time goes in v2:
time: 31.7 us; the launch traced here: 31.3 us
  Pallas kernels  11.6 us (37%)
  waiting for transfers between devices  10.1 us (32%)
  starting transfers between devices  7.26 us (23%)
  local copies, waits for them, and re-layouts  0.86 us (3%)
  other arithmetic  0.8 us (3%)
  between operations  0.7 us (2%)
    pallas_call x1, Pallas kernels, shards(): pl.pallas_call(fit_kernel, out_shape=(jax.ShapeDtypeStruct((epochs, NBASI...  10.1 us
    ppermute x4, starting transfers between devices, between_chips(): return lax.ppermute(block, AXIS, route)  6.06 us
    ppermute x4, waiting for transfers between devices, between_chips(): return lax.ppermute(block, AXIS, route)  5.55 us
    ppermute x5, waiting for transfers between devices, between_cores(): return lax.ppermute(block, AXIS, [(i, i ^ 1) for i in range(n)])  4.55 us
    pallas_call x1, Pallas kernels, shards(): pl.pallas_call(prepare_kernel, out_shape=[vmem((epochs, rows, cols), f32)...  1.48 us
    ppermute x5, starting transfers between devices, between_cores(): return lax.ppermute(block, AXIS, [(i, i ^ 1) for i in range(n)])  1.2 us
    unnamed x3, local copies, waits for them, and re-layouts  0.85 us
    add x1, other arithmetic, shards(): deep_sum = total[0:1] + between_cores(total[1:2].astype(bf16)).astype(f32)  0.67 us
  transfers between devices with their start and end apart: 9, of which 7 were waited for; matrix products, arithmetic and copies ran while one was open for 3% of the time, Pallas kernels for 5%

profile of v2, /device:TPU:1, one launch (start us, length us, event | category | flops | bytes accessed | tf_op | source)
XLA Modules:
  0.0 31.3 jit_solution(14181085263505663402)
XLA Ops:
  0.6 0.1 collective-permute-start
  0.7 0.8 %constant_dynamic-update-slice_fusion.1 = bf16[2,64,512]{2,1,0:T(8,128)(2,1)S(1)} fusion(bf16[1,64,512]{2,1,0:T(8,128)(2,1)} %param.8), kind=kLoop, calls=%fused_computation.6 | loop fusion | bytes 131072
  1.6 0.6 %collective-permute-done = bf16[1,64,512]{2,1,0:T(8,128)(2,1)S(1)} collective-permute-done((bf16[1,64,512]{2,1,0:T(8,128)(2,1)}, bf16[1,64,512]{2,1,0:T(8,128)(2,1)S(1)}, u32[]{:S(2)}, u32[]{:S(2)}) %collective-permute-start) | collective-permute-done | bytes 65568 | tf_op jit(solution)/shard_map/ppermute | solution.py:287
  2.2 2.4 %collective-permute-start.2 = (bf16[2,64,512]{2,1,0:T(8,128)(2,1)S(1)}, bf16[2,64,512]{2,1,0:T(8,128)(2,1)S(1)}, u32[]{:S(2)}, u32[]{:S(2)}) collective-permute-start(bf16[2,64,512]{2,1,0:T(8,128)(2,1)S(1)} %constant_dynamic-update-slice_fusion.pair_ref), channel_id=1, source_target_pairs={{4,0},{0,1},{6,2},{2,3},{8,4},{1,5},{10,6},{3,7},{12,8},{5,9},{14,... | collective-permute-start | bytes 393224 | tf_op jit(solution)/shard_map/ppermute | solution.py:300
  4.6 1.2 %collective-permute-start.1 = (bf16[2,64,512]{2,1,0:T(8,128)(2,1)S(1)}, bf16[2,64,512]{2,1,0:T(8,128)(2,1)S(1)}, u32[]{:S(2)}, u32[]{:S(2)}) collective-permute-start(bf16[2,64,512]{2,1,0:T(8,128)(2,1)S(1)} %constant_dynamic-update-slice_fusion.pair_ref), channel_id=1, source_target_pairs={{2,0},{0,1},{4,2},{1,3},{6,4},{3,5},{8,6},{5,7},{10,8},{7,9},{12,1... | collective-permute-start | bytes 393224 | tf_op jit(solution)/shard_map/ppermute | solution.py:300
  5.8 0.0 copy-start
  5.8 1.5 %prepare.1 = (f32[4,64,512]{2,1,0:T(8,128)S(1)}, f32[4,64,512]{2,1,0:T(8,128)S(1)}, bf16[256,1152]{1,0:T(8,128)(2,1)S(1)}, bf16[3,192,64]{2,1,0:T(8,128)(2,1)S(1...) custom-call(bf16[4,64,512]{2,1,0:T(8,128)(2,1)} %images_hbm.1, s32[4,64,512]{2,1,0:T(8,128)} %good_hbm.1, ...), custom_call_target="tpu_custom_call" | custom-call | tf_op jit(solution)/shard_map/prepare/pallas_call | solution.py:331
  7.3 0.0 collective-permute-done.2.far_ref
  7.3 0.8 %collective-permute-start.4 = (bf16[2,64,512]{2,1,0:T(8,128)(2,1)S(1)}, bf16[2,64,512]{2,1,0:T(8,128)(2,1)S(1)}, u32[]{:S(2)}, u32[]{:S(2)}) collective-permute-start(bf16[2,64,512]{2,1,0:T(8,128)(2,1)S(1)} %collective-permute-done.2.far_ref), channel_id=1, source_target_pairs={{0,1},{1,0},{2,3},{3,2},{4,5},{5,4},{6,7},{7,6},{8,9},{9,8},{10,11... | collective-permute-start | bytes 393224 | tf_op jit(solution)/shard_map/ppermute | solution.py:287
  8.2 1.0 %collective-permute-done.1.near_ref = bf16[2,64,512]{2,1,0:T(8,128)(2,1)S(1)} collective-permute-done((bf16[2,64,512]{2,1,0:T(8,128)(2,1)S(1)}, bf16[2,64,512]{2,1,0:T(8,128)(2,1)S(1)}, u32[]{:S(2)}, u32[]{:S(2)}) %collective-permute-start.1) | collective-permute-done | bytes 131104 | tf_op jit(solution)/shard_map/ppermute | solution.py:300
  9.2 0.0 collective-permute-start.3
  9.2 0.0 copy-done
  9.2 0.0 collective-permute-done.4.swapped_far_ref
  9.2 1.3 %collective-permute-done.3.swapped_near_ref = bf16[2,64,512]{2,1,0:T(8,128)(2,1)S(1)} collective-permute-done((bf16[2,64,512]{2,1,0:T(8,128)(2,1)S(1)}, bf16[2,64,512]{2,1,0:T(8,128)(2,1)S(1)}, u32[]{:S(2)}, u32[]{:S(2)}) %collective-permute-start.3) | collective-permute-done | bytes 131104 | tf_op jit(solution)/shard_map/ppermute | solution.py:287
  10.5 10.1 %fit.1 = (f32[4,27]{1,0:T(4,128)}, f32[2,64,512]{2,1,0:T(8,128)S(1)}, f32[2,64,512]{2,1,0:T(8,128)S(1)}, f32[2,64,512]{2,1,0:T(8,128)S(1)}, bf16[4,64,512]{2,1,0:T(8,128)(2,1)S(1)}) custom-call(s32[4]{0:T(128)S(1)} %compare_select_fusion.1.select_ref, bf16[2,64,512]{2,1,0:T(8,128)(2,1)S(1)} %constant_dynamic-update-slice_fusion.pair_ref, ...), custom_call_target="tpu_custom_call" | custom-call | tf_op jit(solution)/shard_map/fit/pallas_call | solution.py:345
  20.7 0.2 collective-permute-start.5
  20.9 1.4 %collective-permute-done.5 = bf16[4,64,512]{2,1,0:T(8,128)(2,1)S(1)} collective-permute-done((bf16[4,64,512]{2,1,0:T(8,128)(2,1)S(1)}, bf16[4,64,512]{2,1,0:T(8,128)(2,1)S(1)}, u32[]{:S(2)}, u32[]{:S(2)}) %collective-permute-start.5) | collective-permute-done | bytes 262176 | tf_op jit(solution)/shard_map/ppermute | solution.py:287
  22.3 0.1 add_convert_fusion.1
  22.3 0.2 collective-permute-start.6
  22.5 2.2 %collective-permute-start.7 = (bf16[2,64,512]{2,1,0:T(8,128)(2,1)S(1)}, bf16[2,64,512]{2,1,0:T(8,128)(2,1)S(1)}, u32[]{:S(2)}, u32[]{:S(2)}) collective-permute-start(bf16[2,64,512]{2,1,0:T(8,128)(2,1)S(1)} %get-tuple-element.25), channel_id=1, source_target_pairs={{1,0},{5,1},{3,2},{7,3},{0,4},{9,5},{2,6},{11,7},{4,8},{13,9},{6,1... | collective-permute-start | bytes 393224 | tf_op jit(solution)/shard_map/ppermute | solution.py:300
  24.7 1.9 %collective-permute-done.6 = bf16[2,64,512]{2,1,0:T(8,128)(2,1)S(1)} collective-permute-done((bf16[2,64,512]{2,1,0:T(8,128)(2,1)S(1)}, bf16[2,64,512]{2,1,0:T(8,128)(2,1)S(1)}, u32[]{:S(2)}, u32[]{:S(2)}) %collective-permute-start.6) | collective-permute-done | bytes 131104 | tf_op jit(solution)/shard_map/ppermute | solution.py:300
  26.6 2.6 %collective-permute-done.7 = bf16[2,64,512]{2,1,0:T(8,128)(2,1)S(1)} collective-permute-done((bf16[2,64,512]{2,1,0:T(8,128)(2,1)S(1)}, bf16[2,64,512]{2,1,0:T(8,128)(2,1)S(1)}, u32[]{:S(2)}, u32[]{:S(2)}) %collective-permute-start.7) | collective-permute-done | bytes 131104 | tf_op jit(solution)/shard_map/ppermute | solution.py:300
  29.3 0.1 collective-permute-start.8
  29.4 1.2 %collective-permute-done.8 = bf16[1,64,512]{2,1,0:T(8,128)(2,1)S(1)} collective-permute-done((bf16[1,64,512]{2,1,0:T(8,128)(2,1)S(1)}, bf16[1,64,512]{2,1,0:T(8,128)(2,1)S(1)}, u32[]{:S(2)}, u32[]{:S(2)}) %collective-permute-start.8) | collective-permute-done | bytes 65568 | tf_op jit(solution)/shard_map/ppermute | solution.py:287
  30.7 0.7 %slice_add_fusion = f32[1,64,512]{2,1,0:T(8,128)} fusion(f32[2,64,512]{2,1,0:T(8,128)S(1)} %convert_add_fusion, bf16[1,64,512]{2,1,0:T(8,128)(2,1)S(1)} %collective-permute-done.8), kind=kLoop, calls=%fused_computation.4 | loop fusion | flops 65536 | bytes 327680 | tf_op jit(solution)/shard_map/add | solution.py:374
  (4 shorter events, 0.1 us)
Async XLA Ops:
  0.6 1.5 %collective-permute-start = (bf16[1,64,512]{2,1,0:T(8,128)(2,1)}, bf16[1,64,512]{2,1,0:T(8,128)(2,1)S(1)}, u32[]{:S(2)}, u32[]{:S(2)}) collective-permute-start(bf16[1,64,512]{2,1,0:T(8,128)(2,1)} %param.8), channel_id=1, source_target_pairs={{0,1},{1,0},{2,3},{3,2},{4,5},{5,4},{6,7},{7,6},{8,9},{9,8},{10,11... | collective-permute-start | bytes 196616 | tf_op jit(solution)/shard_map/ppermute | solution.py:287
  2.2 5.2 %collective-permute-start.2 = (bf16[2,64,512]{2,1,0:T(8,128)(2,1)S(1)}, bf16[2,64,512]{2,1,0:T(8,128)(2,1)S(1)}, u32[]{:S(2)}, u32[]{:S(2)}) collective-permute-start(bf16[2,64,512]{2,1,0:T(8,128)(2,1)S(1)} %constant_dynamic-update-slice_fusion.pair_ref), channel_id=1, source_target_pairs={{4,0},{0,1},{6,2},{2,3},{8,4},{1,5},{10,6},{3,7},{12,8},{5,9},{14,... | collective-permute-start | bytes 393224 | tf_op jit(solution)/shard_map/ppermute | solution.py:300
  4.6 4.6 %collective-permute-start.1 = (bf16[2,64,512]{2,1,0:T(8,128)(2,1)S(1)}, bf16[2,64,512]{2,1,0:T(8,128)(2,1)S(1)}, u32[]{:S(2)}, u32[]{:S(2)}) collective-permute-start(bf16[2,64,512]{2,1,0:T(8,128)(2,1)S(1)} %constant_dynamic-update-slice_fusion.pair_ref), channel_id=1, source_target_pairs={{2,0},{0,1},{4,2},{1,3},{6,4},{3,5},{8,6},{5,7},{10,8},{7,9},{12,1... | collective-permute-start | bytes 393224 | tf_op jit(solution)/shard_map/ppermute | solution.py:300
  5.8 3.3 %copy-start = (s32[4]{0:T(128)S(1)}, s32[4]{0:T(128)}, u32[]{:S(2)}) copy-start(s32[4]{0:T(128)} %param.9) | copy-start | bytes 52
  7.3 1.8 %collective-permute-start.4 = (bf16[2,64,512]{2,1,0:T(8,128)(2,1)S(1)}, bf16[2,64,512]{2,1,0:T(8,128)(2,1)S(1)}, u32[]{:S(2)}, u32[]{:S(2)}) collective-permute-start(bf16[2,64,512]{2,1,0:T(8,128)(2,1)S(1)} %collective-permute-done.2.far_ref), channel_id=1, source_target_pairs={{0,1},{1,0},{2,3},{3,2},{4,5},{5,4},{6,7},{7,6},{8,9},{9,8},{10,11... | collective-permute-start | bytes 393224 | tf_op jit(solution)/shard_map/ppermute | solution.py:287
  9.2 1.3 %collective-permute-start.3 = (bf16[2,64,512]{2,1,0:T(8,128)(2,1)S(1)}, bf16[2,64,512]{2,1,0:T(8,128)(2,1)S(1)}, u32[]{:S(2)}, u32[]{:S(2)}) collective-permute-start(bf16[2,64,512]{2,1,0:T(8,128)(2,1)S(1)} %collective-permute-done.1.near_ref), channel_id=1, source_target_pairs={{0,1},{1,0},{2,3},{3,2},{4,5},{5,4},{6,7},{7,6},{8,9},{9,8},{10,11... | collective-permute-start | bytes 393224 | tf_op jit(solution)/shard_map/ppermute | solution.py:287
  20.7 1.6 %collective-permute-start.5 = (bf16[4,64,512]{2,1,0:T(8,128)(2,1)S(1)}, bf16[4,64,512]{2,1,0:T(8,128)(2,1)S(1)}, u32[]{:S(2)}, u32[]{:S(2)}) collective-permute-start(bf16[4,64,512]{2,1,0:T(8,128)(2,1)S(1)} %get-tuple-element.21), channel_id=1, source_target_pairs={{0,1},{1,0},{2,3},{3,2},{4,5},{5,4},{6,7},{7,6},{8,9},{9,8},{10,11... | collective-permute-start | bytes 786440 | tf_op jit(solution)/shard_map/ppermute | solution.py:287
  22.3 4.3 %collective-permute-start.6 = (bf16[2,64,512]{2,1,0:T(8,128)(2,1)S(1)}, bf16[2,64,512]{2,1,0:T(8,128)(2,1)S(1)}, u32[]{:S(2)}, u32[]{:S(2)}) collective-permute-start(bf16[2,64,512]{2,1,0:T(8,128)(2,1)S(1)} %get-tuple-element.24), channel_id=1, source_target_pairs={{1,0},{3,1},{0,2},{5,3},{2,4},{7,5},{4,6},{9,7},{6,8},{11,9},{8,10... | collective-permute-start | bytes 393224 | tf_op jit(solution)/shard_map/ppermute | solution.py:300
  22.5 6.7 %collective-permute-start.7 = (bf16[2,64,512]{2,1,0:T(8,128)(2,1)S(1)}, bf16[2,64,512]{2,1,0:T(8,128)(2,1)S(1)}, u32[]{:S(2)}, u32[]{:S(2)}) collective-permute-start(bf16[2,64,512]{2,1,0:T(8,128)(2,1)S(1)} %get-tuple-element.25), channel_id=1, source_target_pairs={{1,0},{5,1},{3,2},{7,3},{0,4},{9,5},{2,6},{11,7},{4,8},{13,9},{6,1... | collective-permute-start | bytes 393224 | tf_op jit(solution)/shard_map/ppermute | solution.py:300
  29.3 1.3 %collective-permute-start.8 = (bf16[1,64,512]{2,1,0:T(8,128)(2,1)S(1)}, bf16[1,64,512]{2,1,0:T(8,128)(2,1)S(1)}, u32[]{:S(2)}, u32[]{:S(2)}) collective-permute-start(bf16[1,64,512]{2,1,0:T(8,128)(2,1)S(1)} %slice.25), channel_id=1, source_target_pairs={{0,1},{1,0},{2,3},{3,2},{4,5},{5,4},{6,7},{7,6},{8,9},{9,8},{10,11... | collective-permute-start | bytes 196616 | tf_op jit(solution)/shard_map/ppermute | solution.py:287

commit v3 on v2

--- a/solution.py
+++ b/solution.py
@@ -124,6 +124,7 @@
     near_sum_ref,
     far_sum_ref,
     swap_sum_ref,
+    template_ref,
     window_ref,
     smooth_ref,
     basis_ref,
@@ -140,19 +141,22 @@
     f32, bf16 = jnp.float32, jnp.bfloat16
 
     sources = [pair_ref, near_ref, far_ref, swapped_near_ref, swapped_far_ref]
+    for e in range(epochs):
+        for index, source in enumerate(sources):
+
+            @pl.when(select_ref[e] // 2 == index)
+            def _():
+                template_ref[e] = source[select_ref[e] % 2]
+
     lane = lax.broadcasted_iota(jnp.int32, (rows, cols + LANES), 1)
     inside = jnp.logical_and(lane >= KHALF, lane < cols + KHALF)
     for e in range(epochs):
-        for index, source in enumerate(sources):
-
-            @pl.when(select_ref[e] // 2 == index)
-            def _():
-                template = source[select_ref[e] % 2].astype(f32)
-                wide = jnp.concatenate([template, template[:, :LANES]], 1)
-                wide = jnp.where(inside, pltpu.roll(wide, KHALF, 1), 0.0).astype(bf16)
-                for b in range(blocks):
-                    at = (e * blocks + b) * rows
-                    window_ref[at : at + rows, :] = wide[:, b * LANES : (b + 2) * LANES]
+        template = template_ref[e].astype(f32)
+        wide = jnp.concatenate([template, template[:, :LANES]], 1)
+        wide = jnp.where(inside, pltpu.roll(wide, KHALF, 1), 0.0).astype(bf16)
+        for b in range(blocks):
+            at = (e * blocks + b) * rows
+            window_ref[at : at + rows, :] = wide[:, b * LANES : (b + 2) * LANES]
 
     sums_ref[...] = jnp.zeros_like(sums_ref)
 
@@ -174,6 +178,7 @@
     row_b = lax.broadcasted_iota(jnp.int32, (height, height), 1)
     same_row = row_a % SUB == row_b % SUB
     wide = 2 * LANES
+    systems = [jnp.zeros((SLOT, LANES), f32)] * epochs
     for e in range(epochs):
         for at in range(0, cols, wide):
             held = {}
@@ -211,53 +216,55 @@
                 lambda g, h: masked_ref[e, g * SUB : (g + 1) * SUB, at + h : at + h + LANES],
             )
         basis = basis_ref[e]
-        gram = lax.dot_general(
-            basis, basis, (((1,), (1,)), ((), ())), preferred_element_type=f32
-        )
+        gram = lax.dot_general(basis, basis, (((1,), (1,)), ((), ())), preferred_element_type=f32)
         for index, part in enumerate(split3(jnp.where(same_row, gram, 0.0))):
             parts_ref[index, e] = part
-    packed = jnp.zeros((height, LANES), f32)
+    packed = [jnp.zeros((height, LANES), f32)] * 2
     for index in range(3):
         for e in range(epochs):
-            packed = packed + jnp.dot(
+            packed[e % 2] = packed[e % 2] + jnp.dot(
                 parts_ref[index, e],
                 place_ref[e * height : (e + 1) * height],
                 preferred_element_type=f32,
             )
     system = jnp.zeros((SLOT, LANES), f32)
-    for part in split3(packed):
+    for part in split3(packed[0] + packed[1]):
         system = system + jnp.dot(fold_ref[...], part, preferred_element_type=f32)
     plane = lax.broadcasted_iota(jnp.int32, (SLOT, LANES), 0)
     lane = lax.broadcasted_iota(jnp.int32, (SLOT, LANES), 1)
     slot = lane % SLOT
     system = system / (rows * cols) + jnp.where(plane == slot, RIDGE_TERM, 0.0)
     start = lane - slot
-    for p in range(0, NBASIS, 2):
-        single = p == NBASIS - 1
-        row_p = jnp.broadcast_to(system[p : p + 1], (SUB, LANES))
-        near = start[:SUB] + p
-        col_p = jnp.take_along_axis(system, start + p, axis=1)
-        a = jnp.take_along_axis(row_p, near, axis=1)
-        if single:
-            u_p = jnp.concatenate([row_p / a] * (SLOT // SUB), 0)
-            system = jnp.where(plane == p, u_p, system - col_p * u_p)
-            continue
-        row_q = jnp.broadcast_to(system[p + 1 : p + 2], (SUB, LANES))
-        col_q = jnp.take_along_axis(system, start + (p + 1), axis=1)
-        b = jnp.take_along_axis(row_p, near + 1, axis=1)
-        d = jnp.take_along_axis(row_q, near + 1, axis=1)
+    column_of = [jnp.take_along_axis(system, start + l, axis=1) for l in range(NBASIS + 1)]
+    direct, swapped = jnp.zeros((SLOT, LANES), f32), jnp.zeros((SLOT, LANES), f32)
+
+    def line(l, p):
+        return jnp.broadcast_to(column_of[l][p : p + 1], (SLOT, LANES))
+
+    for p in range(0, NBASIS - 1, 2):
+        q = p + 1
+        a, b, d = line(p, p), line(q, p), line(q, q)
         scale = 1.0 / (a * d - b * b)
-        u_p = jnp.concatenate([(d * row_p - b * row_q) * scale] * (SLOT // SUB), 0)
-        u_q = jnp.concatenate([(a * row_q - b * row_p) * scale] * (SLOT // SUB), 0)
-        system = jnp.where(
-            plane == p, u_p, jnp.where(plane == p + 1, u_q, system - col_p * u_p - col_q * u_q)
-        )
+        a, b, d = a * scale, b * scale, d * scale
+        outside = (plane != p) & (plane != q)
+        from_p = jnp.where(outside, column_of[p] * d - column_of[q] * b, 0.0)
+        from_q = jnp.where(outside, column_of[q] * a - column_of[p] * b, 0.0)
+        direct = jnp.where(plane == p, d, jnp.where(plane == q, a, direct))
+        swapped = jnp.where(outside, swapped, b)
+        for l in range(p + 2, NBASIS + 1):
+            column_of[l] = column_of[l] - from_p * line(l, p) - from_q * line(l, q)
+    p = NBASIS - 1
+    scale = 1.0 / line(p, p)
+    direct = jnp.where(plane == p, scale, direct)
+    right = column_of[NBASIS]
+    right = right - jnp.where(plane != p, column_of[p] * scale, 0.0) * line(NBASIS, p)
+    above, below = pltpu.roll(right, SLOT - 1, 0), pltpu.roll(right, 1, 0)
+    solved = direct * right - swapped * jnp.where(plane % 2 == 0, above, below)
     fold = fold_ref[...].astype(f32)
     sub = lax.broadcasted_iota(jnp.int32, (SUB, height), 0)
     of_row = lax.broadcasted_iota(jnp.int32, (SUB, height), 1) % SUB
     for e in range(epochs):
-        at = e * SLOT + NBASIS
-        column = jnp.broadcast_to(system[:, at : at + 1], (SLOT, LANES))
+        column = jnp.broadcast_to(solved[:, e * SLOT : e * SLOT + 1], (SLOT, LANES))
         coefs_ref[e : e + 1, :] = jnp.sum(jnp.where(plane == lane, column, 0.0), 0, keepdims=True)[
             :, :NBASIS
         ]
@@ -268,14 +275,23 @@
         high, middle, low = split3(left)
         left = jnp.concatenate([high, middle, low, jnp.zeros_like(low)], 0)
         target = select_ref[e]
-        for g in range(groups):
+        scale = [jnp.broadcast_to(column[k : k + 1, :LANES], (SUB, LANES)) for k in plane_order()]
+        for g in range(groups // 2):
             value = jnp.dot(
                 left, basis_ref[e, :, g * cols : (g + 1) * cols], preferred_element_type=f32
             )
+            value = value[:SUB] + (value[SUB : 2 * SUB] + value[2 * SUB : 3 * SUB])
             here = (target, slice(g * SUB, (g + 1) * SUB))
-            sums_ref[here] = sums_ref[here] + (
-                value[:SUB] + (value[SUB : 2 * SUB] + value[2 * SUB : 3 * SUB])
-            )
+            sums_ref[here] = sums_ref[here] + value
+            g = g + groups // 2
+            for b in range(blocks):
+                to = g * cols + b * LANES
+                tile = basis_ref[e, :, to : to + LANES].astype(f32)
+                value = tile[NBASIS * SUB :]
+                for k in range(NBASIS):
+                    value = value + scale[k] * tile[k * SUB : (k + 1) * SUB]
+                here = (target, slice(g * SUB, (g + 1) * SUB), slice(b * LANES, (b + 1) * LANES))
+                sums_ref[here] = sums_ref[here] + value
     own_sum_ref[...] = sums_ref[0:2]
     near_sum_ref[...] = sums_ref[2:4]
     far_sum_ref[...] = sums_ref[4:6]
@@ -345,7 +361,7 @@
     coefs, own_sum, near_sum, far_sum, swap_sum = pl.pallas_call(
         fit_kernel,
         out_shape=(
-            jax.ShapeDtypeStruct((epochs, NBASIS), f32),
+            vmem((epochs, NBASIS), f32),
             vmem((2, rows, cols), f32),
             vmem((2, rows, cols), f32),
             vmem((2, rows, cols), f32),
@@ -354,6 +370,7 @@
         in_specs=[pl.BlockSpec(memory_space=pltpu.SMEM)] + [vmem_spec] * len(operands),
         out_specs=[vmem_spec] * 5,
         scratch_shapes=[
+            vmem((epochs, rows, cols), bf16),
             vmem((tiles, 2 * LANES), bf16),
             vmem((epochs, rows, taps.shape[0] * cols), bf16),
             vmem((epochs, height, rows // SUB * cols), bf16),

time: 31.7 us -> 30.7 us (0.968)
  Pallas kernels: 11.6 us -> 10.7 us
  waiting for transfers between devices: 10.1 us -> 9.51 us
  local copies, waits for them, and re-layouts: 0.86 us -> 1.44 us
    pallas_call x1, Pallas kernels: 10.1 us -> 9.21 us  [shards(): pl.pallas_call(fit_kernel, out_shape=(vmem((epochs, NBASIS), f32), vmem((...]
    unnamed x3 -> x4, local copies, waits for them, and re-layouts: 0.85 us -> 1.43 us
    ppermute x5, waiting for transfers between devices: 4.55 us -> 3.97 us  [between_cores(): return lax.ppermute(block, AXIS, [(i, i ^ 1) for i in range(n)])]
  transfers between devices with their start and end apart: 9 -> 9, of which waited for: 7 -> 7; matrix products, arithmetic and copies ran while one was open for 3% -> 5% of each run, Pallas kernels for 5% -> 5%
where the time goes in v3:
time: 30.7 us; the launch traced here: 30.4 us
  Pallas kernels  10.7 us (35%)
  waiting for transfers between devices  9.51 us (31%)
  starting transfers between devices  7.26 us (24%)
  local copies, waits for them, and re-layouts  1.44 us (5%)
  other arithmetic  0.8 us (3%)
  between operations  0.7 us (2%)
    pallas_call x1, Pallas kernels, shards(): pl.pallas_call(fit_kernel, out_shape=(vmem((epochs, NBASIS), f32), vmem((...  9.21 us
    ppermute x4, starting transfers between devices, between_chips(): return lax.ppermute(block, AXIS, route)  6.06 us
    ppermute x4, waiting for transfers between devices, between_chips(): return lax.ppermute(block, AXIS, route)  5.54 us
    ppermute x5, waiting for transfers between devices, between_cores(): return lax.ppermute(block, AXIS, [(i, i ^ 1) for i in range(n)])  3.97 us
    pallas_call x1, Pallas kernels, shards(): pl.pallas_call(prepare_kernel, out_shape=[vmem((epochs, rows, cols), f32)...  1.48 us
    unnamed x4, local copies, waits for them, and re-layouts  1.43 us
    ppermute x5, starting transfers between devices, between_cores(): return lax.ppermute(block, AXIS, [(i, i ^ 1) for i in range(n)])  1.2 us
    add x1, other arithmetic, shards(): deep_sum = total[0:1] + between_cores(total[1:2].astype(bf16)).astype(f32)  0.67 us
  transfers between devices with their start and end apart: 9, of which 7 were waited for; matrix products, arithmetic and copies ran while one was open for 5% of the time, Pallas kernels for 5%

profile of v3, /device:TPU:1, one launch (start us, length us, event | category | flops | bytes accessed | tf_op | source)
XLA Modules:
  0.0 30.4 jit_solution(9747085947085823159)
XLA Ops:
  0.6 0.1 collective-permute-start
  0.7 0.8 %constant_dynamic-update-slice_fusion.1 = bf16[2,64,512]{2,1,0:T(8,128)(2,1)S(1)} fusion(bf16[1,64,512]{2,1,0:T(8,128)(2,1)} %param.8), kind=kLoop, calls=%fused_computation.6 | loop fusion | bytes 131072
  1.6 0.6 %collective-permute-done = bf16[1,64,512]{2,1,0:T(8,128)(2,1)S(1)} collective-permute-done((bf16[1,64,512]{2,1,0:T(8,128)(2,1)}, bf16[1,64,512]{2,1,0:T(8,128)(2,1)S(1)}, u32[]{:S(2)}, u32[]{:S(2)}) %collective-permute-start) | collective-permute-done | bytes 65568 | tf_op jit(solution)/shard_map/ppermute | solution.py:303
  2.2 2.4 %collective-permute-start.2 = (bf16[2,64,512]{2,1,0:T(8,128)(2,1)S(1)}, bf16[2,64,512]{2,1,0:T(8,128)(2,1)S(1)}, u32[]{:S(2)}, u32[]{:S(2)}) collective-permute-start(bf16[2,64,512]{2,1,0:T(8,128)(2,1)S(1)} %constant_dynamic-update-slice_fusion.pair_ref), channel_id=1, source_target_pairs={{4,0},{0,1},{6,2},{2,3},{8,4},{1,5},{10,6},{3,7},{12,8},{5,9},{14,... | collective-permute-start | bytes 393224 | tf_op jit(solution)/shard_map/ppermute | solution.py:316
  4.6 1.2 %collective-permute-start.1 = (bf16[2,64,512]{2,1,0:T(8,128)(2,1)S(1)}, bf16[2,64,512]{2,1,0:T(8,128)(2,1)S(1)}, u32[]{:S(2)}, u32[]{:S(2)}) collective-permute-start(bf16[2,64,512]{2,1,0:T(8,128)(2,1)S(1)} %constant_dynamic-update-slice_fusion.pair_ref), channel_id=1, source_target_pairs={{2,0},{0,1},{4,2},{1,3},{6,4},{3,5},{8,6},{5,7},{10,8},{7,9},{12,1... | collective-permute-start | bytes 393224 | tf_op jit(solution)/shard_map/ppermute | solution.py:316
  5.8 0.0 copy-start
  5.8 1.5 %prepare.1 = (f32[4,64,512]{2,1,0:T(8,128)S(1)}, f32[4,64,512]{2,1,0:T(8,128)S(1)}, bf16[256,1152]{1,0:T(8,128)(2,1)S(1)}, bf16[3,192,64]{2,1,0:T(8,128)(2,1)S(1...) custom-call(bf16[4,64,512]{2,1,0:T(8,128)(2,1)} %images_hbm.1, s32[4,64,512]{2,1,0:T(8,128)} %good_hbm.1, ...), custom_call_target="tpu_custom_call" | custom-call | tf_op jit(solution)/shard_map/prepare/pallas_call | solution.py:347
  7.3 0.0 collective-permute-done.2.far_ref
  7.3 0.8 %collective-permute-start.4 = (bf16[2,64,512]{2,1,0:T(8,128)(2,1)S(1)}, bf16[2,64,512]{2,1,0:T(8,128)(2,1)S(1)}, u32[]{:S(2)}, u32[]{:S(2)}) collective-permute-start(bf16[2,64,512]{2,1,0:T(8,128)(2,1)S(1)} %collective-permute-done.2.far_ref), channel_id=1, source_target_pairs={{0,1},{1,0},{2,3},{3,2},{4,5},{5,4},{6,7},{7,6},{8,9},{9,8},{10,11... | collective-permute-start | bytes 393224 | tf_op jit(solution)/shard_map/ppermute | solution.py:303
  8.2 1.0 %collective-permute-done.1.near_ref = bf16[2,64,512]{2,1,0:T(8,128)(2,1)S(1)} collective-permute-done((bf16[2,64,512]{2,1,0:T(8,128)(2,1)S(1)}, bf16[2,64,512]{2,1,0:T(8,128)(2,1)S(1)}, u32[]{:S(2)}, u32[]{:S(2)}) %collective-permute-start.1) | collective-permute-done | bytes 131104 | tf_op jit(solution)/shard_map/ppermute | solution.py:316
  9.2 0.0 collective-permute-start.3
  9.2 0.0 copy-done
  9.2 0.0 collective-permute-done.4.swapped_far_ref
  9.2 1.3 %collective-permute-done.3.swapped_near_ref = bf16[2,64,512]{2,1,0:T(8,128)(2,1)S(1)} collective-permute-done((bf16[2,64,512]{2,1,0:T(8,128)(2,1)S(1)}, bf16[2,64,512]{2,1,0:T(8,128)(2,1)S(1)}, u32[]{:S(2)}, u32[]{:S(2)}) %collective-permute-start.3) | collective-permute-done | bytes 131104 | tf_op jit(solution)/shard_map/ppermute | solution.py:303
  10.5 9.2 %fit.1 = (f32[4,27]{1,0:T(4,128)S(1)}, f32[2,64,512]{2,1,0:T(8,128)S(1)}, f32[2,64,512]{2,1,0:T(8,128)S(1)}, f32[2,64,512]{2,1,0:T(8,128)S(1)}, bf16[4,64,512]{2,1,0:T(8,128)(2,1)S(1)}) custom-call(s32[4]{0:T(128)S(1)} %compare_select_fusion.1.select_ref, bf16[2,64,512]{2,1,0:T(8,128)(2,1)S(1)} %constant_dynamic-update-slice_fusion.pair_ref, ...), custom_call_target="tpu_custom_call" | custom-call | tf_op jit(solution)/shard_map/fit/pallas_call | solution.py:361
  19.7 0.2 collective-permute-start.5
  19.9 1.4 %collective-permute-done.5 = bf16[4,64,512]{2,1,0:T(8,128)(2,1)S(1)} collective-permute-done((bf16[4,64,512]{2,1,0:T(8,128)(2,1)S(1)}, bf16[4,64,512]{2,1,0:T(8,128)(2,1)S(1)}, u32[]{:S(2)}, u32[]{:S(2)}) %collective-permute-start.5) | collective-permute-done | bytes 262176 | tf_op jit(solution)/shard_map/ppermute | solution.py:303
  21.3 0.1 add_convert_fusion.1
  21.4 0.2 collective-permute-start.6
  21.6 2.2 %collective-permute-start.7 = (bf16[2,64,512]{2,1,0:T(8,128)(2,1)S(1)}, bf16[2,64,512]{2,1,0:T(8,128)(2,1)S(1)}, u32[]{:S(2)}, u32[]{:S(2)}) collective-permute-start(bf16[2,64,512]{2,1,0:T(8,128)(2,1)S(1)} %get-tuple-element.25), channel_id=1, source_target_pairs={{1,0},{5,1},{3,2},{7,3},{0,4},{9,5},{2,6},{11,7},{4,8},{13,9},{6,1... | collective-permute-start | bytes 393224 | tf_op jit(solution)/shard_map/ppermute | solution.py:316
  23.8 1.9 %collective-permute-done.6 = bf16[2,64,512]{2,1,0:T(8,128)(2,1)S(1)} collective-permute-done((bf16[2,64,512]{2,1,0:T(8,128)(2,1)S(1)}, bf16[2,64,512]{2,1,0:T(8,128)(2,1)S(1)}, u32[]{:S(2)}, u32[]{:S(2)}) %collective-permute-start.6) | collective-permute-done | bytes 131104 | tf_op jit(solution)/shard_map/ppermute | solution.py:316
  25.7 2.6 %collective-permute-done.7 = bf16[2,64,512]{2,1,0:T(8,128)(2,1)S(1)} collective-permute-done((bf16[2,64,512]{2,1,0:T(8,128)(2,1)S(1)}, bf16[2,64,512]{2,1,0:T(8,128)(2,1)S(1)}, u32[]{:S(2)}, u32[]{:S(2)}) %collective-permute-start.7) | collective-permute-done | bytes 131104 | tf_op jit(solution)/shard_map/ppermute | solution.py:316
  28.4 0.1 collective-permute-start.8
  28.5 0.6 %copy.11 = f32[4,27]{1,0:T(4,128)} copy(f32[4,27]{1,0:T(4,128)S(1)} %get-tuple-element.27) | data formatting | bytes 864
  29.1 0.7 %collective-permute-done.8 = bf16[1,64,512]{2,1,0:T(8,128)(2,1)S(1)} collective-permute-done((bf16[1,64,512]{2,1,0:T(8,128)(2,1)S(1)}, bf16[1,64,512]{2,1,0:T(8,128)(2,1)S(1)}, u32[]{:S(2)}, u32[]{:S(2)}) %collective-permute-start.8) | collective-permute-done | bytes 65568 | tf_op jit(solution)/shard_map/ppermute | solution.py:303
  29.7 0.7 %slice_add_fusion = f32[1,64,512]{2,1,0:T(8,128)} fusion(f32[2,64,512]{2,1,0:T(8,128)S(1)} %convert_add_fusion, bf16[1,64,512]{2,1,0:T(8,128)(2,1)S(1)} %collective-permute-done.8), kind=kLoop, calls=%fused_computation.4 | loop fusion | flops 65536 | bytes 327680 | tf_op jit(solution)/shard_map/add | solution.py:391
  (4 shorter events, 0.1 us)
Async XLA Ops:
  0.6 1.5 %collective-permute-start = (bf16[1,64,512]{2,1,0:T(8,128)(2,1)}, bf16[1,64,512]{2,1,0:T(8,128)(2,1)S(1)}, u32[]{:S(2)}, u32[]{:S(2)}) collective-permute-start(bf16[1,64,512]{2,1,0:T(8,128)(2,1)} %param.8), channel_id=1, source_target_pairs={{0,1},{1,0},{2,3},{3,2},{4,5},{5,4},{6,7},{7,6},{8,9},{9,8},{10,11... | collective-permute-start | bytes 196616 | tf_op jit(solution)/shard_map/ppermute | solution.py:303
  2.2 5.2 %collective-permute-start.2 = (bf16[2,64,512]{2,1,0:T(8,128)(2,1)S(1)}, bf16[2,64,512]{2,1,0:T(8,128)(2,1)S(1)}, u32[]{:S(2)}, u32[]{:S(2)}) collective-permute-start(bf16[2,64,512]{2,1,0:T(8,128)(2,1)S(1)} %constant_dynamic-update-slice_fusion.pair_ref), channel_id=1, source_target_pairs={{4,0},{0,1},{6,2},{2,3},{8,4},{1,5},{10,6},{3,7},{12,8},{5,9},{14,... | collective-permute-start | bytes 393224 | tf_op jit(solution)/shard_map/ppermute | solution.py:316
  4.6 4.6 %collective-permute-start.1 = (bf16[2,64,512]{2,1,0:T(8,128)(2,1)S(1)}, bf16[2,64,512]{2,1,0:T(8,128)(2,1)S(1)}, u32[]{:S(2)}, u32[]{:S(2)}) collective-permute-start(bf16[2,64,512]{2,1,0:T(8,128)(2,1)S(1)} %constant_dynamic-update-slice_fusion.pair_ref), channel_id=1, source_target_pairs={{2,0},{0,1},{4,2},{1,3},{6,4},{3,5},{8,6},{5,7},{10,8},{7,9},{12,1... | collective-permute-start | bytes 393224 | tf_op jit(solution)/shard_map/ppermute | solution.py:316
  5.8 3.3 %copy-start = (s32[4]{0:T(128)S(1)}, s32[4]{0:T(128)}, u32[]{:S(2)}) copy-start(s32[4]{0:T(128)} %param.9) | copy-start | bytes 52
  7.3 1.8 %collective-permute-start.4 = (bf16[2,64,512]{2,1,0:T(8,128)(2,1)S(1)}, bf16[2,64,512]{2,1,0:T(8,128)(2,1)S(1)}, u32[]{:S(2)}, u32[]{:S(2)}) collective-permute-start(bf16[2,64,512]{2,1,0:T(8,128)(2,1)S(1)} %collective-permute-done.2.far_ref), channel_id=1, source_target_pairs={{0,1},{1,0},{2,3},{3,2},{4,5},{5,4},{6,7},{7,6},{8,9},{9,8},{10,11... | collective-permute-start | bytes 393224 | tf_op jit(solution)/shard_map/ppermute | solution.py:303
  9.2 1.3 %collective-permute-start.3 = (bf16[2,64,512]{2,1,0:T(8,128)(2,1)S(1)}, bf16[2,64,512]{2,1,0:T(8,128)(2,1)S(1)}, u32[]{:S(2)}, u32[]{:S(2)}) collective-permute-start(bf16[2,64,512]{2,1,0:T(8,128)(2,1)S(1)} %collective-permute-done.1.near_ref), channel_id=1, source_target_pairs={{0,1},{1,0},{2,3},{3,2},{4,5},{5,4},{6,7},{7,6},{8,9},{9,8},{10,11... | collective-permute-start | bytes 393224 | tf_op jit(solution)/shard_map/ppermute | solution.py:303
  19.7 1.6 %collective-permute-start.5 = (bf16[4,64,512]{2,1,0:T(8,128)(2,1)S(1)}, bf16[4,64,512]{2,1,0:T(8,128)(2,1)S(1)}, u32[]{:S(2)}, u32[]{:S(2)}) collective-permute-start(bf16[4,64,512]{2,1,0:T(8,128)(2,1)S(1)} %get-tuple-element.21), channel_id=1, source_target_pairs={{0,1},{1,0},{2,3},{3,2},{4,5},{5,4},{6,7},{7,6},{8,9},{9,8},{10,11... | collective-permute-start | bytes 786440 | tf_op jit(solution)/shard_map/ppermute | solution.py:303
  21.4 4.3 %collective-permute-start.6 = (bf16[2,64,512]{2,1,0:T(8,128)(2,1)S(1)}, bf16[2,64,512]{2,1,0:T(8,128)(2,1)S(1)}, u32[]{:S(2)}, u32[]{:S(2)}) collective-permute-start(bf16[2,64,512]{2,1,0:T(8,128)(2,1)S(1)} %get-tuple-element.24), channel_id=1, source_target_pairs={{1,0},{3,1},{0,2},{5,3},{2,4},{7,5},{4,6},{9,7},{6,8},{11,9},{8,10... | collective-permute-start | bytes 393224 | tf_op jit(solution)/shard_map/ppermute | solution.py:316
  21.6 6.7 %collective-permute-start.7 = (bf16[2,64,512]{2,1,0:T(8,128)(2,1)S(1)}, bf16[2,64,512]{2,1,0:T(8,128)(2,1)S(1)}, u32[]{:S(2)}, u32[]{:S(2)}) collective-permute-start(bf16[2,64,512]{2,1,0:T(8,128)(2,1)S(1)} %get-tuple-element.25), channel_id=1, source_target_pairs={{1,0},{5,1},{3,2},{7,3},{0,4},{9,5},{2,6},{11,7},{4,8},{13,9},{6,1... | collective-permute-start | bytes 393224 | tf_op jit(solution)/shard_map/ppermute | solution.py:316
  28.4 1.3 %collective-permute-start.8 = (bf16[1,64,512]{2,1,0:T(8,128)(2,1)S(1)}, bf16[1,64,512]{2,1,0:T(8,128)(2,1)S(1)}, u32[]{:S(2)}, u32[]{:S(2)}) collective-permute-start(bf16[1,64,512]{2,1,0:T(8,128)(2,1)S(1)} %slice.25), channel_id=1, source_target_pairs={{0,1},{1,0},{2,3},{3,2},{4,5},{5,4},{6,7},{7,6},{8,9},{9,8},{10,11... | collective-permute-start | bytes 196616 | tf_op jit(solution)/shard_map/ppermute | solution.py:303

commit v4 on v3

--- a/solution.py
+++ b/solution.py
@@ -16,7 +16,6 @@
 RIDGE_TERM = 0.1
 AXIS = "epoch"
 CORES = 2
-REACH = RADIUS // CORES
 LANES = 128
 SUB = 8
 TAPS = 2 * KHALF + 1
@@ -76,13 +75,15 @@
     order = plane_order()
     height = len(order) * SUB
     fold = np.zeros((SLOT, height), np.float32)
+    permute = np.zeros((SLOT, SLOT), np.float32)
     place = np.zeros((epochs, height, LANES), np.float32)
     for position, k in enumerate(order):
         rows = slice(position * SUB, (position + 1) * SUB)
         fold[k, rows] = 1
+        permute[k, position] = 1
         for e in range(epochs):
             place[e, rows, e * SLOT + k] = 1
-    return fold.astype(jnp.bfloat16), place.reshape(epochs * height, LANES).astype(jnp.bfloat16)
+    return fold.astype(jnp.bfloat16), permute.astype(jnp.bfloat16), place.reshape(epochs * height, LANES).astype(jnp.bfloat16)
 
 
 def prepare_kernel(images_hbm, good_hbm, *refs):
@@ -118,13 +119,13 @@
     column_ref,
     row_ref,
     fold_ref,
+    permute_ref,
     place_ref,
     coefs_ref,
     own_sum_ref,
     near_sum_ref,
     far_sum_ref,
     swap_sum_ref,
-    template_ref,
     window_ref,
     smooth_ref,
     basis_ref,
@@ -141,17 +142,14 @@
     f32, bf16 = jnp.float32, jnp.bfloat16
 
     sources = [pair_ref, near_ref, far_ref, swapped_near_ref, swapped_far_ref]
-    for e in range(epochs):
-        for index, source in enumerate(sources):
-
-            @pl.when(select_ref[e] // 2 == index)
-            def _():
-                template_ref[e] = source[select_ref[e] % 2]
-
     lane = lax.broadcasted_iota(jnp.int32, (rows, cols + LANES), 1)
     inside = jnp.logical_and(lane >= KHALF, lane < cols + KHALF)
     for e in range(epochs):
-        template = template_ref[e].astype(f32)
+        kind, slot = select_ref[e] // 2, select_ref[e] % 2
+        template = sources[0][slot]
+        for index, source in enumerate(sources[1:], 1):
+            template = jnp.where(kind == index, source[slot], template)
+        template = template.astype(f32)
         wide = jnp.concatenate([template, template[:, :LANES]], 1)
         wide = jnp.where(inside, pltpu.roll(wide, KHALF, 1), 0.0).astype(bf16)
         for b in range(blocks):
@@ -215,21 +213,23 @@
                 degree(2, 2, 2),
                 lambda g, h: masked_ref[e, g * SUB : (g + 1) * SUB, at + h : at + h + LANES],
             )
-        basis = basis_ref[e]
-        gram = lax.dot_general(basis, basis, (((1,), (1,)), ((), ())), preferred_element_type=f32)
-        for index, part in enumerate(split3(jnp.where(same_row, gram, 0.0))):
-            parts_ref[index, e] = part
-    packed = [jnp.zeros((height, LANES), f32)] * 2
+        pieces = 2 if e == epochs - 1 else 1
+        length = basis_ref.shape[2] // pieces
+        gram = jnp.zeros((height, height), f32)
+        for piece in range(pieces):
+            basis = basis_ref[e, :, piece * length : (piece + 1) * length]
+            product = lax.dot_general(
+                basis, basis, (((1,), (1,)), ((), ())), preferred_element_type=f32
+            )
+            gram = gram + jnp.where(same_row, product, 0.0)
+        gram = gram.reshape(planes, SUB, height).sum(1)
+        gram = jnp.concatenate([gram, jnp.zeros((SLOT - planes, height), f32)], 0)
+        for index, part in enumerate(split3(gram)):
+            parts_ref[index, :, e * height : (e + 1) * height] = part
+    system = jnp.zeros((SLOT, LANES), f32)
     for index in range(3):
-        for e in range(epochs):
-            packed[e % 2] = packed[e % 2] + jnp.dot(
-                parts_ref[index, e],
-                place_ref[e * height : (e + 1) * height],
-                preferred_element_type=f32,
-            )
-    system = jnp.zeros((SLOT, LANES), f32)
-    for part in split3(packed[0] + packed[1]):
-        system = system + jnp.dot(fold_ref[...], part, preferred_element_type=f32)
+        system = system + jnp.dot(parts_ref[index], place_ref[...], preferred_element_type=f32)
+    system = sum(jnp.dot(permute_ref[...], part, preferred_element_type=f32) for part in split3(system))
     plane = lax.broadcasted_iota(jnp.int32, (SLOT, LANES), 0)
     lane = lax.broadcasted_iota(jnp.int32, (SLOT, LANES), 1)
     slot = lane % SLOT
@@ -276,14 +276,14 @@
         left = jnp.concatenate([high, middle, low, jnp.zeros_like(low)], 0)
         target = select_ref[e]
         scale = [jnp.broadcast_to(column[k : k + 1, :LANES], (SUB, LANES)) for k in plane_order()]
-        for g in range(groups // 2):
+        for g in range(6):
             value = jnp.dot(
                 left, basis_ref[e, :, g * cols : (g + 1) * cols], preferred_element_type=f32
             )
             value = value[:SUB] + (value[SUB : 2 * SUB] + value[2 * SUB : 3 * SUB])
             here = (target, slice(g * SUB, (g + 1) * SUB))
             sums_ref[here] = sums_ref[here] + value
-            g = g + groups // 2
+        for g in range(6, groups):
             for b in range(blocks):
                 to = g * cols + b * LANES
                 tile = basis_ref[e, :, to : to + LANES].astype(f32)
@@ -370,11 +370,10 @@
         in_specs=[pl.BlockSpec(memory_space=pltpu.SMEM)] + [vmem_spec] * len(operands),
         out_specs=[vmem_spec] * 5,
         scratch_shapes=[
-            vmem((epochs, rows, cols), bf16),
             vmem((tiles, 2 * LANES), bf16),
             vmem((epochs, rows, taps.shape[0] * cols), bf16),
             vmem((epochs, height, rows // SUB * cols), bf16),
-            vmem((3, epochs, height, height), bf16),
+            vmem((3, SLOT, epochs * height), bf16),
             vmem((10, rows, cols), f32),
         ],
         compiler_params=pltpu.CompilerParams(vmem_limit_bytes=32 << 20),

time: 30.7 us -> 29.5 us (0.961)
  Pallas kernels: 10.7 us -> 9.5 us
    pallas_call x1, Pallas kernels: 9.21 us -> 7.99 us  [shards(): pl.pallas_call(fit_kernel, out_shape=(vmem((epochs, NBASIS), f32), vmem((...]
where the time goes in v4:
time: 29.5 us; the launch traced here: 29.2 us
  waiting for transfers between devices  9.5 us (32%)
  Pallas kernels  9.5 us (32%)
  starting transfers between devices  7.25 us (25%)
  local copies, waits for them, and re-layouts  1.44 us (5%)
  other arithmetic  0.81 us (3%)
  between operations  0.7 us (2%)
    pallas_call x1, Pallas kernels, shards(): pl.pallas_call(fit_kernel, out_shape=(vmem((epochs, NBASIS), f32), vmem((...  7.99 us
    ppermute x4, starting transfers between devices, between_chips(): return lax.ppermute(block, AXIS, route)  6.07 us
    ppermute x4, waiting for transfers between devices, between_chips(): return lax.ppermute(block, AXIS, route)  5.53 us
    ppermute x5, waiting for transfers between devices, between_cores(): return lax.ppermute(block, AXIS, [(i, i ^ 1) for i in range(n)])  3.97 us
    pallas_call x1, Pallas kernels, shards(): pl.pallas_call(prepare_kernel, out_shape=[vmem((epochs, rows, cols), f32)...  1.5 us
    unnamed x4, local copies, waits for them, and re-layouts  1.43 us
    ppermute x5, starting transfers between devices, between_cores(): return lax.ppermute(block, AXIS, [(i, i ^ 1) for i in range(n)])  1.18 us
    add x1, other arithmetic, shards(): deep_sum = total[0:1] + between_cores(total[1:2].astype(bf16)).astype(f32)  0.67 us
  transfers between devices with their start and end apart: 9, of which 7 were waited for; matrix products, arithmetic and copies ran while one was open for 5% of the time, Pallas kernels for 5%

profile of v4, /device:TPU:1, one launch (start us, length us, event | category | flops | bytes accessed | tf_op | source)
XLA Modules:
  0.0 29.2 jit_solution(13375216957599407775)
XLA Ops:
  0.6 0.1 collective-permute-start
  0.7 0.8 %constant_dynamic-update-slice_fusion.1 = bf16[2,64,512]{2,1,0:T(8,128)(2,1)S(1)} fusion(bf16[1,64,512]{2,1,0:T(8,128)(2,1)} %param.9), kind=kLoop, calls=%fused_computation.6 | loop fusion | bytes 131072
  1.6 0.6 %collective-permute-done = bf16[1,64,512]{2,1,0:T(8,128)(2,1)S(1)} collective-permute-done((bf16[1,64,512]{2,1,0:T(8,128)(2,1)}, bf16[1,64,512]{2,1,0:T(8,128)(2,1)S(1)}, u32[]{:S(2)}, u32[]{:S(2)}) %collective-permute-start) | collective-permute-done | bytes 65568 | tf_op jit(solution)/shard_map/ppermute | solution.py:303
  2.2 2.4 %collective-permute-start.2 = (bf16[2,64,512]{2,1,0:T(8,128)(2,1)S(1)}, bf16[2,64,512]{2,1,0:T(8,128)(2,1)S(1)}, u32[]{:S(2)}, u32[]{:S(2)}) collective-permute-start(bf16[2,64,512]{2,1,0:T(8,128)(2,1)S(1)} %constant_dynamic-update-slice_fusion.pair_ref), channel_id=1, source_target_pairs={{4,0},{0,1},{6,2},{2,3},{8,4},{1,5},{10,6},{3,7},{12,8},{5,9},{14,... | collective-permute-start | bytes 393224 | tf_op jit(solution)/shard_map/ppermute | solution.py:316
  4.6 1.2 %collective-permute-start.1 = (bf16[2,64,512]{2,1,0:T(8,128)(2,1)S(1)}, bf16[2,64,512]{2,1,0:T(8,128)(2,1)S(1)}, u32[]{:S(2)}, u32[]{:S(2)}) collective-permute-start(bf16[2,64,512]{2,1,0:T(8,128)(2,1)S(1)} %constant_dynamic-update-slice_fusion.pair_ref), channel_id=1, source_target_pairs={{2,0},{0,1},{4,2},{1,3},{6,4},{3,5},{8,6},{5,7},{10,8},{7,9},{12,1... | collective-permute-start | bytes 393224 | tf_op jit(solution)/shard_map/ppermute | solution.py:316
  5.8 0.0 copy-start
  5.8 1.5 %prepare.1 = (f32[4,64,512]{2,1,0:T(8,128)S(1)}, f32[4,64,512]{2,1,0:T(8,128)S(1)}, bf16[256,1152]{1,0:T(8,128)(2,1)S(1)}, bf16[3,192,64]{2,1,0:T(8,128)(2,1)S(1...) custom-call(bf16[4,64,512]{2,1,0:T(8,128)(2,1)} %images_hbm.1, ...), custom_call_target="tpu_custom_call" | custom-call | tf_op jit(solution)/shard_map/prepare/pallas_call | solution.py:347
  7.4 0.0 collective-permute-done.2.far_ref
  7.4 0.8 %collective-permute-start.4 = (bf16[2,64,512]{2,1,0:T(8,128)(2,1)S(1)}, bf16[2,64,512]{2,1,0:T(8,128)(2,1)S(1)}, u32[]{:S(2)}, u32[]{:S(2)}) collective-permute-start(bf16[2,64,512]{2,1,0:T(8,128)(2,1)S(1)} %collective-permute-done.2.far_ref), channel_id=1, source_target_pairs={{0,1},{1,0},{2,3},{3,2},{4,5},{5,4},{6,7},{7,6},{8,9},{9,8},{10,11... | collective-permute-start | bytes 393224 | tf_op jit(solution)/shard_map/ppermute | solution.py:303
  8.2 1.0 %collective-permute-done.1.near_ref = bf16[2,64,512]{2,1,0:T(8,128)(2,1)S(1)} collective-permute-done((bf16[2,64,512]{2,1,0:T(8,128)(2,1)S(1)}, bf16[2,64,512]{2,1,0:T(8,128)(2,1)S(1)}, u32[]{:S(2)}, u32[]{:S(2)}) %collective-permute-start.1) | collective-permute-done | bytes 131104 | tf_op jit(solution)/shard_map/ppermute | solution.py:316
  9.2 0.0 collective-permute-start.3
  9.2 0.0 copy-done
  9.2 0.0 collective-permute-done.4.swapped_far_ref
  9.2 1.3 %collective-permute-done.3.swapped_near_ref = bf16[2,64,512]{2,1,0:T(8,128)(2,1)S(1)} collective-permute-done((bf16[2,64,512]{2,1,0:T(8,128)(2,1)S(1)}, bf16[2,64,512]{2,1,0:T(8,128)(2,1)S(1)}, u32[]{:S(2)}, u32[]{:S(2)}) %collective-permute-start.3) | collective-permute-done | bytes 131104 | tf_op jit(solution)/shard_map/ppermute | solution.py:303
  10.5 8.0 %fit.1 = (f32[4,27]{1,0:T(4,128)S(1)}, f32[2,64,512]{2,1,0:T(8,128)S(1)}, f32[2,64,512]{2,1,0:T(8,128)S(1)}, f32[2,64,512]{2,1,0:T(8,128)S(1)}, bf16[4,64,512]{2,1,0:T(8,128)(2,1)S(1)}) custom-call(s32[4]{0:T(128)S(1)} %compare_select_fusion.1.select_ref, bf16[2,64,512]{2,1,0:T(8,128)(2,1)S(1)} %constant_dynamic-update-slice_fusion.pair_ref, ...), custom_call_target="tpu_custom_call" | custom-call | tf_op jit(solution)/shard_map/fit/pallas_call | solution.py:361
  18.5 0.2 collective-permute-start.5
  18.7 1.4 %collective-permute-done.5 = bf16[4,64,512]{2,1,0:T(8,128)(2,1)S(1)} collective-permute-done((bf16[4,64,512]{2,1,0:T(8,128)(2,1)S(1)}, bf16[4,64,512]{2,1,0:T(8,128)(2,1)S(1)}, u32[]{:S(2)}, u32[]{:S(2)}) %collective-permute-start.5) | collective-permute-done | bytes 262176 | tf_op jit(solution)/shard_map/ppermute | solution.py:303
  20.1 0.1 add_convert_fusion.1
  20.2 0.2 collective-permute-start.6
  20.4 2.2 %collective-permute-start.7 = (bf16[2,64,512]{2,1,0:T(8,128)(2,1)S(1)}, bf16[2,64,512]{2,1,0:T(8,128)(2,1)S(1)}, u32[]{:S(2)}, u32[]{:S(2)}) collective-permute-start(bf16[2,64,512]{2,1,0:T(8,128)(2,1)S(1)} %get-tuple-element.27), channel_id=1, source_target_pairs={{1,0},{5,1},{3,2},{7,3},{0,4},{9,5},{2,6},{11,7},{4,8},{13,9},{6,1... | collective-permute-start | bytes 393224 | tf_op jit(solution)/shard_map/ppermute | solution.py:316
  22.6 1.9 %collective-permute-done.6 = bf16[2,64,512]{2,1,0:T(8,128)(2,1)S(1)} collective-permute-done((bf16[2,64,512]{2,1,0:T(8,128)(2,1)S(1)}, bf16[2,64,512]{2,1,0:T(8,128)(2,1)S(1)}, u32[]{:S(2)}, u32[]{:S(2)}) %collective-permute-start.6) | collective-permute-done | bytes 131104 | tf_op jit(solution)/shard_map/ppermute | solution.py:316
  24.5 2.6 %collective-permute-done.7 = bf16[2,64,512]{2,1,0:T(8,128)(2,1)S(1)} collective-permute-done((bf16[2,64,512]{2,1,0:T(8,128)(2,1)S(1)}, bf16[2,64,512]{2,1,0:T(8,128)(2,1)S(1)}, u32[]{:S(2)}, u32[]{:S(2)}) %collective-permute-start.7) | collective-permute-done | bytes 131104 | tf_op jit(solution)/shard_map/ppermute | solution.py:316
  27.2 0.1 collective-permute-start.8
  27.3 0.6 %copy.12 = f32[4,27]{1,0:T(4,128)} copy(f32[4,27]{1,0:T(4,128)S(1)} %get-tuple-element.29) | data formatting | bytes 864
  27.9 0.7 %collective-permute-done.8 = bf16[1,64,512]{2,1,0:T(8,128)(2,1)S(1)} collective-permute-done((bf16[1,64,512]{2,1,0:T(8,128)(2,1)S(1)}, bf16[1,64,512]{2,1,0:T(8,128)(2,1)S(1)}, u32[]{:S(2)}, u32[]{:S(2)}) %collective-permute-start.8) | collective-permute-done | bytes 65568 | tf_op jit(solution)/shard_map/ppermute | solution.py:303
  28.5 0.7 %slice_add_fusion = f32[1,64,512]{2,1,0:T(8,128)} fusion(f32[2,64,512]{2,1,0:T(8,128)S(1)} %convert_add_fusion, bf16[1,64,512]{2,1,0:T(8,128)(2,1)S(1)} %collective-permute-done.8), kind=kLoop, calls=%fused_computation.4 | loop fusion | flops 65536 | bytes 327680 | tf_op jit(solution)/shard_map/add | solution.py:390
  (4 shorter events, 0.1 us)
Async XLA Ops:
  0.6 1.5 %collective-permute-start = (bf16[1,64,512]{2,1,0:T(8,128)(2,1)}, bf16[1,64,512]{2,1,0:T(8,128)(2,1)S(1)}, u32[]{:S(2)}, u32[]{:S(2)}) collective-permute-start(bf16[1,64,512]{2,1,0:T(8,128)(2,1)} %param.9), channel_id=1, source_target_pairs={{0,1},{1,0},{2,3},{3,2},{4,5},{5,4},{6,7},{7,6},{8,9},{9,8},{10,11... | collective-permute-start | bytes 196616 | tf_op jit(solution)/shard_map/ppermute | solution.py:303
  2.2 5.2 %collective-permute-start.2 = (bf16[2,64,512]{2,1,0:T(8,128)(2,1)S(1)}, bf16[2,64,512]{2,1,0:T(8,128)(2,1)S(1)}, u32[]{:S(2)}, u32[]{:S(2)}) collective-permute-start(bf16[2,64,512]{2,1,0:T(8,128)(2,1)S(1)} %constant_dynamic-update-slice_fusion.pair_ref), channel_id=1, source_target_pairs={{4,0},{0,1},{6,2},{2,3},{8,4},{1,5},{10,6},{3,7},{12,8},{5,9},{14,... | collective-permute-start | bytes 393224 | tf_op jit(solution)/shard_map/ppermute | solution.py:316
  4.6 4.6 %collective-permute-start.1 = (bf16[2,64,512]{2,1,0:T(8,128)(2,1)S(1)}, bf16[2,64,512]{2,1,0:T(8,128)(2,1)S(1)}, u32[]{:S(2)}, u32[]{:S(2)}) collective-permute-start(bf16[2,64,512]{2,1,0:T(8,128)(2,1)S(1)} %constant_dynamic-update-slice_fusion.pair_ref), channel_id=1, source_target_pairs={{2,0},{0,1},{4,2},{1,3},{6,4},{3,5},{8,6},{5,7},{10,8},{7,9},{12,1... | collective-permute-start | bytes 393224 | tf_op jit(solution)/shard_map/ppermute | solution.py:316
  5.8 3.3 %copy-start = (s32[4]{0:T(128)S(1)}, s32[4]{0:T(128)}, u32[]{:S(2)}) copy-start(s32[4]{0:T(128)} %param.10) | copy-start | bytes 52
  7.4 1.8 %collective-permute-start.4 = (bf16[2,64,512]{2,1,0:T(8,128)(2,1)S(1)}, bf16[2,64,512]{2,1,0:T(8,128)(2,1)S(1)}, u32[]{:S(2)}, u32[]{:S(2)}) collective-permute-start(bf16[2,64,512]{2,1,0:T(8,128)(2,1)S(1)} %collective-permute-done.2.far_ref), channel_id=1, source_target_pairs={{0,1},{1,0},{2,3},{3,2},{4,5},{5,4},{6,7},{7,6},{8,9},{9,8},{10,11... | collective-permute-start | bytes 393224 | tf_op jit(solution)/shard_map/ppermute | solution.py:303
  9.2 1.3 %collective-permute-start.3 = (bf16[2,64,512]{2,1,0:T(8,128)(2,1)S(1)}, bf16[2,64,512]{2,1,0:T(8,128)(2,1)S(1)}, u32[]{:S(2)}, u32[]{:S(2)}) collective-permute-start(bf16[2,64,512]{2,1,0:T(8,128)(2,1)S(1)} %collective-permute-done.1.near_ref), channel_id=1, source_target_pairs={{0,1},{1,0},{2,3},{3,2},{4,5},{5,4},{6,7},{7,6},{8,9},{9,8},{10,11... | collective-permute-start | bytes 393224 | tf_op jit(solution)/shard_map/ppermute | solution.py:303
  18.5 1.6 %collective-permute-start.5 = (bf16[4,64,512]{2,1,0:T(8,128)(2,1)S(1)}, bf16[4,64,512]{2,1,0:T(8,128)(2,1)S(1)}, u32[]{:S(2)}, u32[]{:S(2)}) collective-permute-start(bf16[4,64,512]{2,1,0:T(8,128)(2,1)S(1)} %get-tuple-element.23), channel_id=1, source_target_pairs={{0,1},{1,0},{2,3},{3,2},{4,5},{5,4},{6,7},{7,6},{8,9},{9,8},{10,11... | collective-permute-start | bytes 786440 | tf_op jit(solution)/shard_map/ppermute | solution.py:303
  20.2 4.3 %collective-permute-start.6 = (bf16[2,64,512]{2,1,0:T(8,128)(2,1)S(1)}, bf16[2,64,512]{2,1,0:T(8,128)(2,1)S(1)}, u32[]{:S(2)}, u32[]{:S(2)}) collective-permute-start(bf16[2,64,512]{2,1,0:T(8,128)(2,1)S(1)} %get-tuple-element.26), channel_id=1, source_target_pairs={{1,0},{3,1},{0,2},{5,3},{2,4},{7,5},{4,6},{9,7},{6,8},{11,9},{8,10... | collective-permute-start | bytes 393224 | tf_op jit(solution)/shard_map/ppermute | solution.py:316
  20.4 6.7 %collective-permute-start.7 = (bf16[2,64,512]{2,1,0:T(8,128)(2,1)S(1)}, bf16[2,64,512]{2,1,0:T(8,128)(2,1)S(1)}, u32[]{:S(2)}, u32[]{:S(2)}) collective-permute-start(bf16[2,64,512]{2,1,0:T(8,128)(2,1)S(1)} %get-tuple-element.27), channel_id=1, source_target_pairs={{1,0},{5,1},{3,2},{7,3},{0,4},{9,5},{2,6},{11,7},{4,8},{13,9},{6,1... | collective-permute-start | bytes 393224 | tf_op jit(solution)/shard_map/ppermute | solution.py:316
  27.2 1.3 %collective-permute-start.8 = (bf16[1,64,512]{2,1,0:T(8,128)(2,1)S(1)}, bf16[1,64,512]{2,1,0:T(8,128)(2,1)S(1)}, u32[]{:S(2)}, u32[]{:S(2)}) collective-permute-start(bf16[1,64,512]{2,1,0:T(8,128)(2,1)S(1)} %slice.25), channel_id=1, source_target_pairs={{0,1},{1,0},{2,3},{3,2},{4,5},{5,4},{6,7},{7,6},{8,9},{9,8},{10,11... | collective-permute-start | bytes 196616 | tf_op jit(solution)/shard_map/ppermute | solution.py:303

commit v5 on v4

--- a/solution.py
+++ b/solution.py
@@ -74,16 +74,13 @@
 def plane_maps(epochs):
     order = plane_order()
     height = len(order) * SUB
-    fold = np.zeros((SLOT, height), np.float32)
-    permute = np.zeros((SLOT, SLOT), np.float32)
+    natural = np.zeros((SLOT, SLOT), np.float32)
     place = np.zeros((epochs, height, LANES), np.float32)
     for position, k in enumerate(order):
-        rows = slice(position * SUB, (position + 1) * SUB)
-        fold[k, rows] = 1
-        permute[k, position] = 1
+        natural[position, k] = 1
         for e in range(epochs):
-            place[e, rows, e * SLOT + k] = 1
-    return fold.astype(jnp.bfloat16), permute.astype(jnp.bfloat16), place.reshape(epochs * height, LANES).astype(jnp.bfloat16)
+            place[e, position * SUB : (position + 1) * SUB, e * SLOT + position] = 1
+    return natural.astype(jnp.bfloat16), place.reshape(epochs * height, LANES).astype(jnp.bfloat16)
 
 
 def prepare_kernel(images_hbm, good_hbm, *refs):
@@ -118,19 +115,15 @@
     weight_ref,
     column_ref,
     row_ref,
-    fold_ref,
-    permute_ref,
+    natural_ref,
     place_ref,
     coefs_ref,
-    own_sum_ref,
-    near_sum_ref,
-    far_sum_ref,
+    sums_ref,
     swap_sum_ref,
     window_ref,
     smooth_ref,
     basis_ref,
     parts_ref,
-    sums_ref,
 ):
     epochs, rows, cols = masked_ref.shape
     blocks = cols // LANES
@@ -229,7 +222,6 @@
     system = jnp.zeros((SLOT, LANES), f32)
     for index in range(3):
         system = system + jnp.dot(parts_ref[index], place_ref[...], preferred_element_type=f32)
-    system = sum(jnp.dot(permute_ref[...], part, preferred_element_type=f32) for part in split3(system))
     plane = lax.broadcasted_iota(jnp.int32, (SLOT, LANES), 0)
     lane = lax.broadcasted_iota(jnp.int32, (SLOT, LANES), 1)
     slot = lane % SLOT
@@ -260,14 +252,16 @@
     right = right - jnp.where(plane != p, column_of[p] * scale, 0.0) * line(NBASIS, p)
     above, below = pltpu.roll(right, SLOT - 1, 0), pltpu.roll(right, 1, 0)
     solved = direct * right - swapped * jnp.where(plane % 2 == 0, above, below)
-    fold = fold_ref[...].astype(f32)
+    natural = natural_ref[...].astype(f32)
+    fold = (
+        lax.broadcasted_iota(jnp.int32, (SLOT, height), 0)
+        == lax.broadcasted_iota(jnp.int32, (SLOT, height), 1) // SUB
+    ).astype(f32)
     sub = lax.broadcasted_iota(jnp.int32, (SUB, height), 0)
     of_row = lax.broadcasted_iota(jnp.int32, (SUB, height), 1) % SUB
     for e in range(epochs):
         column = jnp.broadcast_to(solved[:, e * SLOT : e * SLOT + 1], (SLOT, LANES))
-        coefs_ref[e : e + 1, :] = jnp.sum(jnp.where(plane == lane, column, 0.0), 0, keepdims=True)[
-            :, :NBASIS
-        ]
+        coefs_ref[e : e + 1, :] = jnp.sum(natural * column[:, :SLOT], 0, keepdims=True)[:, :NBASIS]
         column = jnp.where(plane < NBASIS, -column, jnp.where(plane == NBASIS, 1.0, 0.0))
         column = jnp.concatenate([column, column], 1)[:, :height]
         spread = jnp.sum(fold * column, 0, keepdims=True)
@@ -275,7 +269,7 @@
         high, middle, low = split3(left)
         left = jnp.concatenate([high, middle, low, jnp.zeros_like(low)], 0)
         target = select_ref[e]
-        scale = [jnp.broadcast_to(column[k : k + 1, :LANES], (SUB, LANES)) for k in plane_order()]
+        scale = [jnp.broadcast_to(column[k : k + 1, :LANES], (SUB, LANES)) for k in range(NBASIS)]
         for g in range(6):
             value = jnp.dot(
                 left, basis_ref[e, :, g * cols : (g + 1) * cols], preferred_element_type=f32
@@ -292,9 +286,6 @@
                     value = value + scale[k] * tile[k * SUB : (k + 1) * SUB]
                 here = (target, slice(g * SUB, (g + 1) * SUB), slice(b * LANES, (b + 1) * LANES))
                 sums_ref[here] = sums_ref[here] + value
-    own_sum_ref[...] = sums_ref[0:2]
-    near_sum_ref[...] = sums_ref[2:4]
-    far_sum_ref[...] = sums_ref[4:6]
     swap_sum_ref[...] = sums_ref[6:10].astype(bf16)
 
 
@@ -358,23 +349,20 @@
         name="prepare",
     )(*(pltpu.with_memory_space_constraint(x, pltpu.HBM) for x in sources))
     operands = (pair, near, far, swapped_near, swapped_far, *prepared)
-    coefs, own_sum, near_sum, far_sum, swap_sum = pl.pallas_call(
+    coefs, sums, swap_sum = pl.pallas_call(
         fit_kernel,
         out_shape=(
             vmem((epochs, NBASIS), f32),
-            vmem((2, rows, cols), f32),
-            vmem((2, rows, cols), f32),
-            vmem((2, rows, cols), f32),
+            vmem((10, rows, cols), f32),
             vmem((4, rows, cols), bf16),
         ),
         in_specs=[pl.BlockSpec(memory_space=pltpu.SMEM)] + [vmem_spec] * len(operands),
-        out_specs=[vmem_spec] * 5,
+        out_specs=[vmem_spec] * 3,
         scratch_shapes=[
             vmem((tiles, 2 * LANES), bf16),
             vmem((epochs, rows, taps.shape[0] * cols), bf16),
             vmem((epochs, height, rows // SUB * cols), bf16),
             vmem((3, SLOT, epochs * height), bf16),
-            vmem((10, rows, cols), f32),
         ],
         compiler_params=pltpu.CompilerParams(vmem_limit_bytes=32 << 20),
         name="fit",
@@ -383,10 +371,10 @@
         *(pltpu.with_memory_space_constraint(x, pltpu.VMEM) for x in operands),
     )
     received = between_cores(swap_sum)
-    near_sum = (near_sum + received[0:2].astype(f32)).astype(bf16)
-    far_sum = (far_sum + received[2:4].astype(f32)).astype(bf16)
+    near_sum = (sums[2:4] + received[0:2].astype(f32)).astype(bf16)
+    far_sum = (sums[4:6] + received[2:4].astype(f32)).astype(bf16)
     near_back, far_back = between_chips(near_sum, -1), between_chips(far_sum, -2)
-    total = own_sum + near_back.astype(f32) + far_back.astype(f32)
+    total = sums[0:2] + near_back.astype(f32) + far_back.astype(f32)
     deep_sum = total[0:1] + between_cores(total[1:2].astype(bf16)).astype(f32)
     return (deep_sum, coefs)
 

time: 29.5 us -> 29.4 us (level)
  no operation moved by 1% of the time
where the time goes in v5:
time: 29.4 us; the launch traced here: 29 us
  waiting for transfers between devices  9.5 us (32%)
  Pallas kernels  9.28 us (32%)
  starting transfers between devices  7.29 us (25%)
  local copies, waits for them, and re-layouts  1.45 us (5%)
  other arithmetic  0.83 us (3%)
  between operations  0.7 us (2%)
    pallas_call x1, Pallas kernels, shards(): pl.pallas_call(fit_kernel, out_shape=(vmem((epochs, NBASIS), f32), vmem((...  7.81 us
    ppermute x4, starting transfers between devices, between_chips(): return lax.ppermute(block, AXIS, route)  6.07 us
    ppermute x4, waiting for transfers between devices, between_chips(): return lax.ppermute(block, AXIS, route)  5.53 us
    ppermute x5, waiting for transfers between devices, between_cores(): return lax.ppermute(block, AXIS, [(i, i ^ 1) for i in range(n)])  3.97 us
    pallas_call x1, Pallas kernels, shards(): pl.pallas_call(prepare_kernel, out_shape=[vmem((epochs, rows, cols), f32)...  1.46 us
    unnamed x4, local copies, waits for them, and re-layouts  1.43 us
    ppermute x5, starting transfers between devices, between_cores(): return lax.ppermute(block, AXIS, [(i, i ^ 1) for i in range(n)])  1.22 us
    add x1, other arithmetic, shards(): deep_sum = total[0:1] + between_cores(total[1:2].astype(bf16)).astype(f32)  0.67 us
  transfers between devices with their start and end apart: 9, of which 7 were waited for; matrix products, arithmetic and copies ran while one was open for 5% of the time, Pallas kernels for 5%

profile of v5, /device:TPU:1, one launch (start us, length us, event | category | flops | bytes accessed | tf_op | source)
XLA Modules:
  0.0 29.0 jit_solution(13611211729462791627)
XLA Ops:
  0.6 0.0 copy-start
  0.6 0.1 collective-permute-start
  0.7 0.8 %constant_dynamic-update-slice_fusion.1 = bf16[2,64,512]{2,1,0:T(8,128)(2,1)S(1)} fusion(bf16[1,64,512]{2,1,0:T(8,128)(2,1)} %param.8), kind=kLoop, calls=%fused_computation.6 | loop fusion | bytes 131072
  1.6 0.6 %collective-permute-done = bf16[1,64,512]{2,1,0:T(8,128)(2,1)S(1)} collective-permute-done((bf16[1,64,512]{2,1,0:T(8,128)(2,1)}, bf16[1,64,512]{2,1,0:T(8,128)(2,1)S(1)}, u32[]{:S(2)}, u32[]{:S(2)}) %collective-permute-start) | collective-permute-done | bytes 65568 | tf_op jit(solution)/shard_map/ppermute | solution.py:294
  2.2 2.4 %collective-permute-start.2 = (bf16[2,64,512]{2,1,0:T(8,128)(2,1)S(1)}, bf16[2,64,512]{2,1,0:T(8,128)(2,1)S(1)}, u32[]{:S(2)}, u32[]{:S(2)}) collective-permute-start(bf16[2,64,512]{2,1,0:T(8,128)(2,1)S(1)} %constant_dynamic-update-slice_fusion.pair_ref), channel_id=1, source_target_pairs={{4,0},{0,1},{6,2},{2,3},{8,4},{1,5},{10,6},{3,7},{12,8},{5,9},{14,... | collective-permute-start | bytes 393224 | tf_op jit(solution)/shard_map/ppermute | solution.py:307
  4.6 1.2 %collective-permute-start.1 = (bf16[2,64,512]{2,1,0:T(8,128)(2,1)S(1)}, bf16[2,64,512]{2,1,0:T(8,128)(2,1)S(1)}, u32[]{:S(2)}, u32[]{:S(2)}) collective-permute-start(bf16[2,64,512]{2,1,0:T(8,128)(2,1)S(1)} %constant_dynamic-update-slice_fusion.pair_ref), channel_id=1, source_target_pairs={{2,0},{0,1},{4,2},{1,3},{6,4},{3,5},{8,6},{5,7},{10,8},{7,9},{12,1... | collective-permute-start | bytes 393224 | tf_op jit(solution)/shard_map/ppermute | solution.py:307
  5.9 1.5 %prepare.1 = (f32[4,64,512]{2,1,0:T(8,128)S(1)}, f32[4,64,512]{2,1,0:T(8,128)S(1)}, bf16[256,1152]{1,0:T(8,128)(2,1)S(1)}, bf16[3,192,64]{2,1,0:T(8,128)(2,1)S(1...) custom-call(bf16[4,64,512]{2,1,0:T(8,128)(2,1)} %images_hbm.1, s32[4,64,512]{2,1,0:T(8,128)} %good_hbm.1, ...), custom_call_target="tpu_custom_call" | custom-call | tf_op jit(solution)/shard_map/prepare/pallas_call | solution.py:338
  7.3 0.0 collective-permute-done.2.far_ref
  7.3 0.9 %collective-permute-start.4 = (bf16[2,64,512]{2,1,0:T(8,128)(2,1)S(1)}, bf16[2,64,512]{2,1,0:T(8,128)(2,1)S(1)}, u32[]{:S(2)}, u32[]{:S(2)}) collective-permute-start(bf16[2,64,512]{2,1,0:T(8,128)(2,1)S(1)} %collective-permute-done.2.far_ref), channel_id=1, source_target_pairs={{0,1},{1,0},{2,3},{3,2},{4,5},{5,4},{6,7},{7,6},{8,9},{9,8},{10,11... | collective-permute-start | bytes 393224 | tf_op jit(solution)/shard_map/ppermute | solution.py:294
  8.2 1.0 %collective-permute-done.1.near_ref = bf16[2,64,512]{2,1,0:T(8,128)(2,1)S(1)} collective-permute-done((bf16[2,64,512]{2,1,0:T(8,128)(2,1)S(1)}, bf16[2,64,512]{2,1,0:T(8,128)(2,1)S(1)}, u32[]{:S(2)}, u32[]{:S(2)}) %collective-permute-start.1) | collective-permute-done | bytes 131104 | tf_op jit(solution)/shard_map/ppermute | solution.py:307
  9.2 0.0 collective-permute-start.3
  9.2 0.0 copy-done
  9.2 0.0 collective-permute-done.4.swapped_far_ref
  9.2 1.3 %collective-permute-done.3.swapped_near_ref = bf16[2,64,512]{2,1,0:T(8,128)(2,1)S(1)} collective-permute-done((bf16[2,64,512]{2,1,0:T(8,128)(2,1)S(1)}, bf16[2,64,512]{2,1,0:T(8,128)(2,1)S(1)}, u32[]{:S(2)}, u32[]{:S(2)}) %collective-permute-start.3) | collective-permute-done | bytes 131104 | tf_op jit(solution)/shard_map/ppermute | solution.py:294
  10.5 7.8 %fit.1 = (f32[4,27]{1,0:T(4,128)S(1)}, f32[10,64,512]{2,1,0:T(8,128)S(1)}, bf16[4,64,512]{2,1,0:T(8,128)(2,1)S(1)}) custom-call(s32[4]{0:T(128)S(1)} %compare_select_fusion.1.select_ref, bf16[2,64,512]{2,1,0:T(8,128)(2,1)S(1)} %constant_dynamic-update-slice_fusion.pair_ref, bf16[2,64,512]{2,1,0:T(8,128)(2,1)S(1)} %collective-permute-done.1.near_ref, ...), custom_call_target="tpu_custom_call" | custom-call | tf_op jit(solution)/shard_map/fit/pallas_call | solution.py:352
  18.3 0.2 collective-permute-start.5
  18.6 1.4 %collective-permute-done.5 = bf16[4,64,512]{2,1,0:T(8,128)(2,1)S(1)} collective-permute-done((bf16[4,64,512]{2,1,0:T(8,128)(2,1)S(1)}, bf16[4,64,512]{2,1,0:T(8,128)(2,1)S(1)}, u32[]{:S(2)}, u32[]{:S(2)}) %collective-permute-start.5) | collective-permute-done | bytes 262176 | tf_op jit(solution)/shard_map/ppermute | solution.py:294
  19.9 0.1 add_convert_fusion.1
  20.0 0.2 collective-permute-start.6
  20.2 2.2 %collective-permute-start.7 = (bf16[2,64,512]{2,1,0:T(8,128)(2,1)S(1)}, bf16[2,64,512]{2,1,0:T(8,128)(2,1)S(1)}, u32[]{:S(2)}, u32[]{:S(2)}) collective-permute-start(bf16[2,64,512]{2,1,0:T(8,128)(2,1)S(1)} %get-tuple-element.21), channel_id=1, source_target_pairs={{1,0},{5,1},{3,2},{7,3},{0,4},{9,5},{2,6},{11,7},{4,8},{13,9},{6,1... | collective-permute-start | bytes 393224 | tf_op jit(solution)/shard_map/ppermute | solution.py:307
  22.4 1.9 %collective-permute-done.6 = bf16[2,64,512]{2,1,0:T(8,128)(2,1)S(1)} collective-permute-done((bf16[2,64,512]{2,1,0:T(8,128)(2,1)S(1)}, bf16[2,64,512]{2,1,0:T(8,128)(2,1)S(1)}, u32[]{:S(2)}, u32[]{:S(2)}) %collective-permute-start.6) | collective-permute-done | bytes 131104 | tf_op jit(solution)/shard_map/ppermute | solution.py:307
  24.3 2.6 %collective-permute-done.7 = bf16[2,64,512]{2,1,0:T(8,128)(2,1)S(1)} collective-permute-done((bf16[2,64,512]{2,1,0:T(8,128)(2,1)S(1)}, bf16[2,64,512]{2,1,0:T(8,128)(2,1)S(1)}, u32[]{:S(2)}, u32[]{:S(2)}) %collective-permute-start.7) | collective-permute-done | bytes 131104 | tf_op jit(solution)/shard_map/ppermute | solution.py:307
  27.0 0.1 convert_add_fusion
  27.1 0.1 collective-permute-start.8
  27.1 0.6 %copy.11 = f32[4,27]{1,0:T(4,128)} copy(f32[4,27]{1,0:T(4,128)S(1)} %get-tuple-element.23) | data formatting | bytes 864
  27.7 0.7 %collective-permute-done.8 = bf16[1,64,512]{2,1,0:T(8,128)(2,1)S(1)} collective-permute-done((bf16[1,64,512]{2,1,0:T(8,128)(2,1)S(1)}, bf16[1,64,512]{2,1,0:T(8,128)(2,1)S(1)}, u32[]{:S(2)}, u32[]{:S(2)}) %collective-permute-start.8) | collective-permute-done | bytes 65568 | tf_op jit(solution)/shard_map/ppermute | solution.py:294
  28.4 0.7 %slice_add_fusion = f32[1,64,512]{2,1,0:T(8,128)} fusion(f32[2,64,512]{2,1,0:T(8,128)S(1)} %convert_add_fusion, bf16[1,64,512]{2,1,0:T(8,128)(2,1)S(1)} %collective-permute-done.8), kind=kLoop, calls=%fused_computation.4 | loop fusion | flops 65536 | bytes 327680 | tf_op jit(solution)/shard_map/add | solution.py:378
  (3 shorter events, 0.0 us)
Async XLA Ops:
  0.6 8.5 %copy-start = (s32[4]{0:T(128)S(1)}, s32[4]{0:T(128)}, u32[]{:S(2)}) copy-start(s32[4]{0:T(128)} %param.9) | copy-start | bytes 52
  0.6 1.5 %collective-permute-start = (bf16[1,64,512]{2,1,0:T(8,128)(2,1)}, bf16[1,64,512]{2,1,0:T(8,128)(2,1)S(1)}, u32[]{:S(2)}, u32[]{:S(2)}) collective-permute-start(bf16[1,64,512]{2,1,0:T(8,128)(2,1)} %param.8), channel_id=1, source_target_pairs={{0,1},{1,0},{2,3},{3,2},{4,5},{5,4},{6,7},{7,6},{8,9},{9,8},{10,11... | collective-permute-start | bytes 196616 | tf_op jit(solution)/shard_map/ppermute | solution.py:294
  2.2 5.2 %collective-permute-start.2 = (bf16[2,64,512]{2,1,0:T(8,128)(2,1)S(1)}, bf16[2,64,512]{2,1,0:T(8,128)(2,1)S(1)}, u32[]{:S(2)}, u32[]{:S(2)}) collective-permute-start(bf16[2,64,512]{2,1,0:T(8,128)(2,1)S(1)} %constant_dynamic-update-slice_fusion.pair_ref), channel_id=1, source_target_pairs={{4,0},{0,1},{6,2},{2,3},{8,4},{1,5},{10,6},{3,7},{12,8},{5,9},{14,... | collective-permute-start | bytes 393224 | tf_op jit(solution)/shard_map/ppermute | solution.py:307
  4.6 4.6 %collective-permute-start.1 = (bf16[2,64,512]{2,1,0:T(8,128)(2,1)S(1)}, bf16[2,64,512]{2,1,0:T(8,128)(2,1)S(1)}, u32[]{:S(2)}, u32[]{:S(2)}) collective-permute-start(bf16[2,64,512]{2,1,0:T(8,128)(2,1)S(1)} %constant_dynamic-update-slice_fusion.pair_ref), channel_id=1, source_target_pairs={{2,0},{0,1},{4,2},{1,3},{6,4},{3,5},{8,6},{5,7},{10,8},{7,9},{12,1... | collective-permute-start | bytes 393224 | tf_op jit(solution)/shard_map/ppermute | solution.py:307
  7.3 1.9 %collective-permute-start.4 = (bf16[2,64,512]{2,1,0:T(8,128)(2,1)S(1)}, bf16[2,64,512]{2,1,0:T(8,128)(2,1)S(1)}, u32[]{:S(2)}, u32[]{:S(2)}) collective-permute-start(bf16[2,64,512]{2,1,0:T(8,128)(2,1)S(1)} %collective-permute-done.2.far_ref), channel_id=1, source_target_pairs={{0,1},{1,0},{2,3},{3,2},{4,5},{5,4},{6,7},{7,6},{8,9},{9,8},{10,11... | collective-permute-start | bytes 393224 | tf_op jit(solution)/shard_map/ppermute | solution.py:294
  9.2 1.3 %collective-permute-start.3 = (bf16[2,64,512]{2,1,0:T(8,128)(2,1)S(1)}, bf16[2,64,512]{2,1,0:T(8,128)(2,1)S(1)}, u32[]{:S(2)}, u32[]{:S(2)}) collective-permute-start(bf16[2,64,512]{2,1,0:T(8,128)(2,1)S(1)} %collective-permute-done.1.near_ref), channel_id=1, source_target_pairs={{0,1},{1,0},{2,3},{3,2},{4,5},{5,4},{6,7},{7,6},{8,9},{9,8},{10,11... | collective-permute-start | bytes 393224 | tf_op jit(solution)/shard_map/ppermute | solution.py:294
  18.3 1.6 %collective-permute-start.5 = (bf16[4,64,512]{2,1,0:T(8,128)(2,1)S(1)}, bf16[4,64,512]{2,1,0:T(8,128)(2,1)S(1)}, u32[]{:S(2)}, u32[]{:S(2)}) collective-permute-start(bf16[4,64,512]{2,1,0:T(8,128)(2,1)S(1)} %get-tuple-element.18), channel_id=1, source_target_pairs={{0,1},{1,0},{2,3},{3,2},{4,5},{5,4},{6,7},{7,6},{8,9},{9,8},{10,11... | collective-permute-start | bytes 786440 | tf_op jit(solution)/shard_map/ppermute | solution.py:294
  20.0 4.3 %collective-permute-start.6 = (bf16[2,64,512]{2,1,0:T(8,128)(2,1)S(1)}, bf16[2,64,512]{2,1,0:T(8,128)(2,1)S(1)}, u32[]{:S(2)}, u32[]{:S(2)}) collective-permute-start(bf16[2,64,512]{2,1,0:T(8,128)(2,1)S(1)} %get-tuple-element.20), channel_id=1, source_target_pairs={{1,0},{3,1},{0,2},{5,3},{2,4},{7,5},{4,6},{9,7},{6,8},{11,9},{8,10... | collective-permute-start | bytes 393224 | tf_op jit(solution)/shard_map/ppermute | solution.py:307
  20.2 6.7 %collective-permute-start.7 = (bf16[2,64,512]{2,1,0:T(8,128)(2,1)S(1)}, bf16[2,64,512]{2,1,0:T(8,128)(2,1)S(1)}, u32[]{:S(2)}, u32[]{:S(2)}) collective-permute-start(bf16[2,64,512]{2,1,0:T(8,128)(2,1)S(1)} %get-tuple-element.21), channel_id=1, source_target_pairs={{1,0},{5,1},{3,2},{7,3},{0,4},{9,5},{2,6},{11,7},{4,8},{13,9},{6,1... | collective-permute-start | bytes 393224 | tf_op jit(solution)/shard_map/ppermute | solution.py:307
  27.1 1.3 %collective-permute-start.8 = (bf16[1,64,512]{2,1,0:T(8,128)(2,1)S(1)}, bf16[1,64,512]{2,1,0:T(8,128)(2,1)S(1)}, u32[]{:S(2)}, u32[]{:S(2)}) collective-permute-start(bf16[1,64,512]{2,1,0:T(8,128)(2,1)S(1)} %slice.40), channel_id=1, source_target_pairs={{0,1},{1,0},{2,3},{3,2},{4,5},{5,4},{6,7},{7,6},{8,9},{9,8},{10,11... | collective-permute-start | bytes 196616 | tf_op jit(solution)/shard_map/ppermute | solution.py:294

commit v6 on v5

--- a/solution.py
+++ b/solution.py
@@ -316,7 +316,8 @@
     far = jnp.abs(chip_offset) - 1
     mine = 2 + 2 * far + jnp.where(same_core, 0, 1)
     theirs = 6 + 2 * far + jnp.where(same_core, 1, 0)
-    away = jnp.where(chip_offset * side > 0, mine, theirs)
+    lean = jnp.where(far == 0, -side, side)
+    away = jnp.where(chip_offset * lean > 0, mine, theirs)
     return jnp.where(chip_offset == 0, jnp.where(same_core, 0, 1), away).astype(jnp.int32)
 
 
@@ -327,7 +328,7 @@
     assert lax.axis_size(AXIS) % CORES == 0 and cols % LANES == 0 and rows % SUB == 0
     other = between_cores(templates)
     pair = jnp.concatenate([templates, other], 0)
-    near, far = between_chips(pair, 1), between_chips(pair, 2)
+    near, far = between_chips(pair, -1), between_chips(pair, 2)
     swapped_near, swapped_far = between_cores(near), between_cores(far)
     taps = kernel_taps()
     height = (NBASIS + 1) * SUB
@@ -373,7 +374,7 @@
     received = between_cores(swap_sum)
     near_sum = (sums[2:4] + received[0:2].astype(f32)).astype(bf16)
     far_sum = (sums[4:6] + received[2:4].astype(f32)).astype(bf16)
-    near_back, far_back = between_chips(near_sum, -1), between_chips(far_sum, -2)
+    near_back, far_back = between_chips(near_sum, 1), between_chips(far_sum, -2)
     total = sums[0:2] + near_back.astype(f32) + far_back.astype(f32)
     deep_sum = total[0:1] + between_cores(total[1:2].astype(bf16)).astype(f32)
     return (deep_sum, coefs)

time: 29.4 us -> 29.3 us (level)
    ppermute x4, starting transfers between devices: 6.07 us -> 5.14 us  [between_chips(): return lax.ppermute(block, AXIS, route)]
    ppermute x5, starting transfers between devices: 1.22 us -> 2 us  [between_cores(): return lax.ppermute(block, AXIS, [(i, i ^ 1) for i in range(n)])]
  transfers between devices with their start and end apart: 9 -> 9, of which waited for: 7 -> 9; matrix products, arithmetic and copies ran while one was open for 5% -> 5% of each run, Pallas kernels for 5% -> 5%
where the time goes in v6:
time: 29.3 us; the launch traced here: 29 us
  waiting for transfers between devices  9.61 us (33%)
  Pallas kernels  9.28 us (32%)
  starting transfers between devices  7.14 us (24%)
  local copies, waits for them, and re-layouts  1.45 us (5%)
  other arithmetic  0.83 us (3%)
  between operations  0.69 us (2%)
    pallas_call x1, Pallas kernels, shards(): pl.pallas_call(fit_kernel, out_shape=(vmem((epochs, NBASIS), f32), vmem((...  7.81 us
    ppermute x4, waiting for transfers between devices, between_chips(): return lax.ppermute(block, AXIS, route)  5.64 us
    ppermute x4, starting transfers between devices, between_chips(): return lax.ppermute(block, AXIS, route)  5.14 us
    ppermute x5, waiting for transfers between devices, between_cores(): return lax.ppermute(block, AXIS, [(i, i ^ 1) for i in range(n)])  3.97 us
    ppermute x5, starting transfers between devices, between_cores(): return lax.ppermute(block, AXIS, [(i, i ^ 1) for i in range(n)])  2 us
    pallas_call x1, Pallas kernels, shards(): pl.pallas_call(prepare_kernel, out_shape=[vmem((epochs, rows, cols), f32)...  1.46 us
    unnamed x4, local copies, waits for them, and re-layouts  1.43 us
    add x1, other arithmetic, shards(): deep_sum = total[0:1] + between_cores(total[1:2].astype(bf16)).astype(f32)  0.67 us
  transfers between devices with their start and end apart: 9, of which 9 were waited for; matrix products, arithmetic and copies ran while one was open for 5% of the time, Pallas kernels for 5%

profile of v6, /device:TPU:1, one launch (start us, length us, event | category | flops | bytes accessed | tf_op | source)
XLA Modules:
  0.0 29.0 jit_solution(13958604260560841818)
XLA Ops:
  0.6 0.0 copy-start
  0.6 0.1 collective-permute-start
  0.7 0.8 %constant_dynamic-update-slice_fusion.1 = bf16[2,64,512]{2,1,0:T(8,128)(2,1)S(1)} fusion(bf16[1,64,512]{2,1,0:T(8,128)(2,1)} %param.8), kind=kLoop, calls=%fused_computation.6 | loop fusion | bytes 131072
  1.6 0.6 %collective-permute-done = bf16[1,64,512]{2,1,0:T(8,128)(2,1)S(1)} collective-permute-done((bf16[1,64,512]{2,1,0:T(8,128)(2,1)}, bf16[1,64,512]{2,1,0:T(8,128)(2,1)S(1)}, u32[]{:S(2)}, u32[]{:S(2)}) %collective-permute-start) | collective-permute-done | bytes 65568 | tf_op jit(solution)/shard_map/ppermute | solution.py:294
  2.2 2.4 %collective-permute-start.2 = (bf16[2,64,512]{2,1,0:T(8,128)(2,1)S(1)}, bf16[2,64,512]{2,1,0:T(8,128)(2,1)S(1)}, u32[]{:S(2)}, u32[]{:S(2)}) collective-permute-start(bf16[2,64,512]{2,1,0:T(8,128)(2,1)S(1)} %constant_dynamic-update-slice_fusion.pair_ref), channel_id=1, source_target_pairs={{4,0},{0,1},{6,2},{2,3},{8,4},{1,5},{10,6},{3,7},{12,8},{5,9},{14,... | collective-permute-start | bytes 393224 | tf_op jit(solution)/shard_map/ppermute | solution.py:307
  4.6 0.0 collective-permute-start.1
  4.6 1.5 %prepare.1 = (f32[4,64,512]{2,1,0:T(8,128)S(1)}, f32[4,64,512]{2,1,0:T(8,128)S(1)}, bf16[256,1152]{1,0:T(8,128)(2,1)S(1)}, bf16[3,192,64]{2,1,0:T(8,128)(2,1)S(1...) custom-call(bf16[4,64,512]{2,1,0:T(8,128)(2,1)} %images_hbm.1, s32[4,64,512]{2,1,0:T(8,128)} %good_hbm.1, ...), custom_call_target="tpu_custom_call" | custom-call | tf_op jit(solution)/shard_map/prepare/pallas_call | solution.py:339
  6.1 0.5 %collective-permute-done.2.far_ref = bf16[2,64,512]{2,1,0:T(8,128)(2,1)S(1)} collective-permute-done((bf16[2,64,512]{2,1,0:T(8,128)(2,1)S(1)}, bf16[2,64,512]{2,1,0:T(8,128)(2,1)S(1)}, u32[]{:S(2)}, u32[]{:S(2)}) %collective-permute-start.2) | collective-permute-done | bytes 131104 | tf_op jit(solution)/shard_map/ppermute | solution.py:307
  6.6 1.6 %collective-permute-start.4 = (bf16[2,64,512]{2,1,0:T(8,128)(2,1)S(1)}, bf16[2,64,512]{2,1,0:T(8,128)(2,1)S(1)}, u32[]{:S(2)}, u32[]{:S(2)}) collective-permute-start(bf16[2,64,512]{2,1,0:T(8,128)(2,1)S(1)} %collective-permute-done.2.far_ref), channel_id=1, source_target_pairs={{0,1},{1,0},{2,3},{3,2},{4,5},{5,4},{6,7},{7,6},{8,9},{9,8},{10,11... | collective-permute-start | bytes 393224 | tf_op jit(solution)/shard_map/ppermute | solution.py:294
  8.2 0.2 collective-permute-done.1.near_ref
  8.4 0.0 collective-permute-start.3
  8.4 0.0 copy-done
  8.5 0.7 %collective-permute-done.4.swapped_far_ref = bf16[2,64,512]{2,1,0:T(8,128)(2,1)S(1)} collective-permute-done((bf16[2,64,512]{2,1,0:T(8,128)(2,1)S(1)}, bf16[2,64,512]{2,1,0:T(8,128)(2,1)S(1)}, u32[]{:S(2)}, u32[]{:S(2)}) %collective-permute-start.4) | collective-permute-done | bytes 131104 | tf_op jit(solution)/shard_map/ppermute | solution.py:294
  9.2 0.6 %collective-permute-done.3.swapped_near_ref = bf16[2,64,512]{2,1,0:T(8,128)(2,1)S(1)} collective-permute-done((bf16[2,64,512]{2,1,0:T(8,128)(2,1)S(1)}, bf16[2,64,512]{2,1,0:T(8,128)(2,1)S(1)}, u32[]{:S(2)}, u32[]{:S(2)}) %collective-permute-start.3) | collective-permute-done | bytes 131104 | tf_op jit(solution)/shard_map/ppermute | solution.py:294
  9.8 7.8 %fit.1 = (f32[4,27]{1,0:T(4,128)S(1)}, f32[10,64,512]{2,1,0:T(8,128)S(1)}, bf16[4,64,512]{2,1,0:T(8,128)(2,1)S(1)}) custom-call(s32[4]{0:T(128)S(1)} %compare_select_fusion.2.select_ref, bf16[2,64,512]{2,1,0:T(8,128)(2,1)S(1)} %constant_dynamic-update-slice_fusion.pair_ref, bf16[2,64,512]{2,1,0:T(8,128)(2,1)S(1)} %collective-permute-done.1.near_ref, ...), custom_call_target="tpu_custom_call" | custom-call | tf_op jit(solution)/shard_map/fit/pallas_call | solution.py:353
  17.6 0.2 collective-permute-start.5
  17.8 1.4 %collective-permute-done.5 = bf16[4,64,512]{2,1,0:T(8,128)(2,1)S(1)} collective-permute-done((bf16[4,64,512]{2,1,0:T(8,128)(2,1)S(1)}, bf16[4,64,512]{2,1,0:T(8,128)(2,1)S(1)}, u32[]{:S(2)}, u32[]{:S(2)}) %collective-permute-start.5) | collective-permute-done | bytes 262176 | tf_op jit(solution)/shard_map/ppermute | solution.py:294
  19.2 0.1 add_convert_fusion.1
  19.3 2.7 %collective-permute-start.6 = (bf16[2,64,512]{2,1,0:T(8,128)(2,1)S(1)}, bf16[2,64,512]{2,1,0:T(8,128)(2,1)S(1)}, u32[]{:S(2)}, u32[]{:S(2)}) collective-permute-start(bf16[2,64,512]{2,1,0:T(8,128)(2,1)S(1)} %get-tuple-element.20), channel_id=1, source_target_pairs={{2,0},{0,1},{4,2},{1,3},{6,4},{3,5},{8,6},{5,7},{10,8},{7,9},{12,1... | collective-permute-start | bytes 393224 | tf_op jit(solution)/shard_map/ppermute | solution.py:307
  22.0 0.0 collective-permute-start.7
  22.0 1.9 %collective-permute-done.6 = bf16[2,64,512]{2,1,0:T(8,128)(2,1)S(1)} collective-permute-done((bf16[2,64,512]{2,1,0:T(8,128)(2,1)S(1)}, bf16[2,64,512]{2,1,0:T(8,128)(2,1)S(1)}, u32[]{:S(2)}, u32[]{:S(2)}) %collective-permute-start.6) | collective-permute-done | bytes 131104 | tf_op jit(solution)/shard_map/ppermute | solution.py:307
  23.9 3.0 %collective-permute-done.7 = bf16[2,64,512]{2,1,0:T(8,128)(2,1)S(1)} collective-permute-done((bf16[2,64,512]{2,1,0:T(8,128)(2,1)S(1)}, bf16[2,64,512]{2,1,0:T(8,128)(2,1)S(1)}, u32[]{:S(2)}, u32[]{:S(2)}) %collective-permute-start.7) | collective-permute-done | bytes 131104 | tf_op jit(solution)/shard_map/ppermute | solution.py:307
  26.9 0.1 convert_add_fusion
  27.0 0.1 collective-permute-start.8
  27.1 0.6 %copy.11 = f32[4,27]{1,0:T(4,128)} copy(f32[4,27]{1,0:T(4,128)S(1)} %get-tuple-element.23) | data formatting | bytes 864
  27.7 0.7 %collective-permute-done.8 = bf16[1,64,512]{2,1,0:T(8,128)(2,1)S(1)} collective-permute-done((bf16[1,64,512]{2,1,0:T(8,128)(2,1)S(1)}, bf16[1,64,512]{2,1,0:T(8,128)(2,1)S(1)}, u32[]{:S(2)}, u32[]{:S(2)}) %collective-permute-start.8) | collective-permute-done | bytes 65568 | tf_op jit(solution)/shard_map/ppermute | solution.py:294
  28.3 0.7 %slice_add_fusion = f32[1,64,512]{2,1,0:T(8,128)} fusion(f32[2,64,512]{2,1,0:T(8,128)S(1)} %convert_add_fusion, bf16[1,64,512]{2,1,0:T(8,128)(2,1)S(1)} %collective-permute-done.8), kind=kLoop, calls=%fused_computation.4 | loop fusion | flops 65536 | bytes 327680 | tf_op jit(solution)/shard_map/add | solution.py:379
  (3 shorter events, 0.0 us)
Async XLA Ops:
  0.6 7.8 %copy-start = (s32[4]{0:T(128)S(1)}, s32[4]{0:T(128)}, u32[]{:S(2)}) copy-start(s32[4]{0:T(128)} %param.9) | copy-start | bytes 52
  0.6 1.5 %collective-permute-start = (bf16[1,64,512]{2,1,0:T(8,128)(2,1)}, bf16[1,64,512]{2,1,0:T(8,128)(2,1)S(1)}, u32[]{:S(2)}, u32[]{:S(2)}) collective-permute-start(bf16[1,64,512]{2,1,0:T(8,128)(2,1)} %param.8), channel_id=1, source_target_pairs={{0,1},{1,0},{2,3},{3,2},{4,5},{5,4},{6,7},{7,6},{8,9},{9,8},{10,11... | collective-permute-start | bytes 196616 | tf_op jit(solution)/shard_map/ppermute | solution.py:294
  2.2 4.4 %collective-permute-start.2 = (bf16[2,64,512]{2,1,0:T(8,128)(2,1)S(1)}, bf16[2,64,512]{2,1,0:T(8,128)(2,1)S(1)}, u32[]{:S(2)}, u32[]{:S(2)}) collective-permute-start(bf16[2,64,512]{2,1,0:T(8,128)(2,1)S(1)} %constant_dynamic-update-slice_fusion.pair_ref), channel_id=1, source_target_pairs={{4,0},{0,1},{6,2},{2,3},{8,4},{1,5},{10,6},{3,7},{12,8},{5,9},{14,... | collective-permute-start | bytes 393224 | tf_op jit(solution)/shard_map/ppermute | solution.py:307
  4.6 3.8 %collective-permute-start.1 = (bf16[2,64,512]{2,1,0:T(8,128)(2,1)S(1)}, bf16[2,64,512]{2,1,0:T(8,128)(2,1)S(1)}, u32[]{:S(2)}, u32[]{:S(2)}) collective-permute-start(bf16[2,64,512]{2,1,0:T(8,128)(2,1)S(1)} %constant_dynamic-update-slice_fusion.pair_ref), channel_id=1, source_target_pairs={{1,0},{3,1},{0,2},{5,3},{2,4},{7,5},{4,6},{9,7},{6,8},{11,9},{8,10... | collective-permute-start | bytes 393224 | tf_op jit(solution)/shard_map/ppermute | solution.py:307
  6.6 2.6 %collective-permute-start.4 = (bf16[2,64,512]{2,1,0:T(8,128)(2,1)S(1)}, bf16[2,64,512]{2,1,0:T(8,128)(2,1)S(1)}, u32[]{:S(2)}, u32[]{:S(2)}) collective-permute-start(bf16[2,64,512]{2,1,0:T(8,128)(2,1)S(1)} %collective-permute-done.2.far_ref), channel_id=1, source_target_pairs={{0,1},{1,0},{2,3},{3,2},{4,5},{5,4},{6,7},{7,6},{8,9},{9,8},{10,11... | collective-permute-start | bytes 393224 | tf_op jit(solution)/shard_map/ppermute | solution.py:294
  8.4 1.3 %collective-permute-start.3 = (bf16[2,64,512]{2,1,0:T(8,128)(2,1)S(1)}, bf16[2,64,512]{2,1,0:T(8,128)(2,1)S(1)}, u32[]{:S(2)}, u32[]{:S(2)}) collective-permute-start(bf16[2,64,512]{2,1,0:T(8,128)(2,1)S(1)} %collective-permute-done.1.near_ref), channel_id=1, source_target_pairs={{0,1},{1,0},{2,3},{3,2},{4,5},{5,4},{6,7},{7,6},{8,9},{9,8},{10,11... | collective-permute-start | bytes 393224 | tf_op jit(solution)/shard_map/ppermute | solution.py:294
  17.6 1.6 %collective-permute-start.5 = (bf16[4,64,512]{2,1,0:T(8,128)(2,1)S(1)}, bf16[4,64,512]{2,1,0:T(8,128)(2,1)S(1)}, u32[]{:S(2)}, u32[]{:S(2)}) collective-permute-start(bf16[4,64,512]{2,1,0:T(8,128)(2,1)S(1)} %get-tuple-element.18), channel_id=1, source_target_pairs={{0,1},{1,0},{2,3},{3,2},{4,5},{5,4},{6,7},{7,6},{8,9},{9,8},{10,11... | collective-permute-start | bytes 786440 | tf_op jit(solution)/shard_map/ppermute | solution.py:294
  19.3 4.6 %collective-permute-start.6 = (bf16[2,64,512]{2,1,0:T(8,128)(2,1)S(1)}, bf16[2,64,512]{2,1,0:T(8,128)(2,1)S(1)}, u32[]{:S(2)}, u32[]{:S(2)}) collective-permute-start(bf16[2,64,512]{2,1,0:T(8,128)(2,1)S(1)} %get-tuple-element.20), channel_id=1, source_target_pairs={{2,0},{0,1},{4,2},{1,3},{6,4},{3,5},{8,6},{5,7},{10,8},{7,9},{12,1... | collective-permute-start | bytes 393224 | tf_op jit(solution)/shard_map/ppermute | solution.py:307
  22.0 4.9 %collective-permute-start.7 = (bf16[2,64,512]{2,1,0:T(8,128)(2,1)S(1)}, bf16[2,64,512]{2,1,0:T(8,128)(2,1)S(1)}, u32[]{:S(2)}, u32[]{:S(2)}) collective-permute-start(bf16[2,64,512]{2,1,0:T(8,128)(2,1)S(1)} %get-tuple-element.21), channel_id=1, source_target_pairs={{1,0},{5,1},{3,2},{7,3},{0,4},{9,5},{2,6},{11,7},{4,8},{13,9},{6,1... | collective-permute-start | bytes 393224 | tf_op jit(solution)/shard_map/ppermute | solution.py:307
  27.0 1.3 %collective-permute-start.8 = (bf16[1,64,512]{2,1,0:T(8,128)(2,1)S(1)}, bf16[1,64,512]{2,1,0:T(8,128)(2,1)S(1)}, u32[]{:S(2)}, u32[]{:S(2)}) collective-permute-start(bf16[1,64,512]{2,1,0:T(8,128)(2,1)S(1)} %slice.40), channel_id=1, source_target_pairs={{0,1},{1,0},{2,3},{3,2},{4,5},{5,4},{6,7},{7,6},{8,9},{9,8},{10,11... | collective-permute-start | bytes 196616 | tf_op jit(solution)/shard_map/ppermute | solution.py:294
